TPU v7x, 256 devices: a whole 4x4x8 slice. The times are simulated.
256 devices in a mesh: pool: 4 (over x_hi, core), frame: 16 (over x_lo, z), tensor: 4 (over y).
Axes of the slice: x: 4 (x_hi: 2, x_lo: 2; x = x_hi * 2 + x_lo), y: 4, z: 8, core: 2. Of those that a mesh axis runs over, the one named last changes fastest.
Arguments:
- latents: bfloat16 [32768, 2240], P(('pool', 'frame', 'tensor')), parts along dimension 0, may hold values from -6 to 6
- queries: bfloat16 [32768, 2240], P(('pool', 'frame'), 'tensor'), parts along dimension 0, may hold values from -6 to 6
- keys: bfloat16 [32768, 2240], P(('pool', 'frame'), 'tensor'), parts along dimension 0, may hold values from -6 to 6
- values: bfloat16 [32768, 2240], P(('pool', 'frame'), 'tensor'), parts along dimension 0, may hold values from -6 to 6
- log_decay: float32 [20, 32768], P('tensor', ('pool', 'frame')), parts along dimension 1, may hold values from -0.6 to 0, as said below
- block_ids: int32 [32768], P(('pool', 'frame')), parts along dimension 0, may hold values from 0 to 3, as said below
- t_index: int32 [4], P('pool'), parts along dimension 0, may hold values from 0 to 49
- w_mod: bfloat16 [256, 8960], replicated, may hold values from -0.375 to 0.375
- w_out: bfloat16 [2240, 2240], P('tensor', 'frame'), may hold values from -0.125 to 0.125
- w_up: bfloat16 [2240, 4480], P('frame', 'tensor'), may hold values from -0.125 to 0.125
- w_down: bfloat16 [4480, 2240], P('tensor', 'frame'), may hold values from -0.09375 to 0.09375
Outputs:
- velocity: bfloat16 [32768, 2240], P(('pool', 'frame', 'tensor')), parts along dimension 0
- advanced: bfloat16 [32768, 2240], P(('pool', 'frame', 'tensor')), parts along dimension 0
There are 4 independent parts, one for each index of `pool`. A program takes and returns all parts, laid end to end along the dimension named above; an argument that names none is the same for every part. Nothing has to cross between parts.
Inputs may be any that keep to these rules, and one draw needn't show every extreme that they name: `block_ids`: within each span of 512 tokens the value never falls, starts at 0 and ends at 3. `log_decay`: every entry is negative.
All inputs are finite; a program needn't handle non-finite values.
Results may differ from a plain program's by a relative error of at most 0.0085.
Values may be sent and summed in bfloat16 or wider, within the bound.
No kernel may reach another device: no remote copies, remote signals or barrier semaphores. Data moves between devices by JAX's collectives and lax.ppermute only.
A program may use at most 128 MiB of HBM per device.

v0:
```python
import functools
import math

import jax
import jax.numpy as jnp
import numpy as np
from jax import lax
from jax.experimental import pallas as pl
from jax.experimental.pallas import tpu as pltpu
from jax.sharding import Mesh, PartitionSpec as P


STEPS = 50
BF = jnp.bfloat16
F32 = jnp.float32
AXES = {"xh": 2, "c": 2, "xl": 2, "z": 8, "y": 4}
HEADS = 5
DH = 112
TOKENS = 512
SHARE = 128
WIDTH = 2240
PIECE = 70
PADDED = 72
PIECES = 32
ROWS = PIECES * PADDED
VMEM = pl.BlockSpec(memory_space=pltpu.VMEM)
SMEM = pl.BlockSpec(memory_space=pltpu.SMEM)


def permute(block, axes, route):
    sizes = [AXES[a] for a in axes]
    pairs = []
    for i in range(int(np.prod(sizes))):
        target = route(*[int(v) for v in np.unravel_index(i, sizes)])
        if target is not None:
            pairs.append((i, int(np.ravel_multi_index(target, sizes))))
    return lax.ppermute(block, tuple(axes) if len(axes) > 1 else axes[0], pairs)


def along_y(block, d):
    return permute(block, ("y",), lambda y: ((y + d) % 4,))


def along_x(block, d):
    def route(xh, xl):
        x = (2 * xh + xl + d) % 4
        return (x // 2, x % 2)

    return permute(block, ("xh", "xl"), route)


def other_core(block):
    return permute(block, ("c",), lambda c: (1 - c,))


def in_vmem(block):
    return pltpu.with_memory_space_constraint(block, pltpu.VMEM)


def cost(flops, size):
    return pl.CostEstimate(flops=flops, bytes_accessed=size, transcendentals=0)


def modulation_of(t_index, w_mod):
    fraction = 1.0 - t_index[0].astype(F32) / STEPS
    following = fraction - 1.0 / STEPS
    sigma_now = 3.0 * fraction / (1.0 + 2.0 * fraction)
    sigma_next = 3.0 * following / (1.0 + 2.0 * following)
    half_width = w_mod.shape[0] // 2
    frequency = jnp.exp(-math.log(10000.0) * jnp.arange(half_width).astype(F32) / half_width)
    angles = 1000.0 * sigma_now * frequency
    embedding = jnp.concatenate([jnp.cos(angles), jnp.sin(angles)])
    time_features = jax.nn.silu(embedding).astype(BF)
    shifts = jnp.dot(time_features[None, :], w_mod, preferred_element_type=F32)[0]
    return (lax.optimization_barrier(shifts), sigma_next - sigma_now)


def padded_pieces(rows):
    pieces = rows.reshape(-1, PIECE, rows.shape[1])
    return jnp.pad(pieces, ((0, 0), (0, PADDED - PIECE), (0, 0)))


STATE_ROWS = 640


def total_lanes(total):
    hi = total.astype(BF).astype(F32)
    mid = (total - hi).astype(BF).astype(F32)
    low = total - hi - mid
    lane = lax.broadcasted_iota(jnp.int32, (DH, 16), 1)
    zero = jnp.zeros((DH, 16), F32)
    return jnp.where(lane == 0, hi, jnp.where(lane == 1, mid, jnp.where(lane == 2, low, zero))).astype(BF)


def state_kernel(k_ref, v_ref, decay_ref, cumulative_ref, packed_ref):
    decay = decay_ref[...]
    hi = decay.astype(BF)
    rest = decay - hi.astype(F32)
    mid = rest.astype(BF)
    low = (rest - mid.astype(F32)).astype(BF)
    row = lax.broadcasted_iota(jnp.int32, (TOKENS, TOKENS), 0)
    column = lax.broadcasted_iota(jnp.int32, (TOKENS, TOKENS), 1)
    triangle = jnp.where(row <= column, 1.0, 0.0).astype(BF)
    cumulative = sum(
        jnp.dot(part, triangle, preferred_element_type=F32) for part in (low, mid, hi)
    )
    cumulative_ref[...] = cumulative
    for h in range(HEADS):
        mine = cumulative[h : h + 1, :]
        total = mine[:, TOKENS - 1 :]
        heads = pl.ds(DH * h, DH)
        scaled = (k_ref[heads, :].astype(F32) * jnp.exp(total - mine)).astype(BF)
        state = lax.dot_general(
            v_ref[heads, :], scaled, (((1,), (1,)), ((), ())), preferred_element_type=F32
        )
        packed_ref[heads, 0:DH] = state.astype(BF)
        packed_ref[heads, DH:SHARE] = total_lanes(total)
    packed_ref[HEADS * DH :, :] = jnp.zeros((STATE_ROWS - HEADS * DH, SHARE), BF)


def own_state(keys, values, log_decay):
    return pl.pallas_call(
        state_kernel,
        out_shape=(
            jax.ShapeDtypeStruct((HEADS, TOKENS), F32),
            jax.ShapeDtypeStruct((STATE_ROWS, SHARE), BF),
        ),
        in_specs=[VMEM] * 3,
        out_specs=(VMEM, VMEM),
        cost_estimate=cost(10**9, 3 * 10**6),
    )(keys, values, log_decay)


def scan_kernel(blocks_ref, before_ref):
    state = jnp.zeros(before_ref.shape[1:], F32)
    for f in range(blocks_ref.shape[0]):
        before_ref[f] = state.astype(BF)
        packed = blocks_ref[f].astype(F32)
        total = jnp.sum(packed[:, DH : DH + 3], axis=1, keepdims=True)
        state = packed + jnp.exp(total) * state


def scan_blocks(blocks):
    return pl.pallas_call(
        scan_kernel,
        out_shape=jax.ShapeDtypeStruct(blocks.shape, BF),
        in_specs=[VMEM],
        out_specs=VMEM,
        cost_estimate=cost(10**6, 10**6),
    )(in_vmem(blocks))


def inner_kernel(q_ref, k_ref, v_ref, cumulative_ref, labels_ref, out_ref):
    cumulative = cumulative_ref[...]
    labels = labels_ref[...].astype(F32)
    stacked = jnp.concatenate([cumulative, labels, jnp.zeros((2, TOKENS), F32)], axis=0)
    columns = stacked.T
    visible = columns[:, HEADS : HEADS + 1] <= labels
    for h in range(HEADS):
        heads = pl.ds(DH * h, DH)
        scores = lax.dot_general(
            k_ref[heads, :], q_ref[heads, :], (((0,), (0,)), ((), ())), preferred_element_type=F32
        )
        decay = jnp.exp(jnp.minimum(cumulative[h : h + 1, :] - columns[:, h : h + 1], 0.0))
        weights = jnp.where(visible, decay * (DH**-0.5), 0.0)
        probs = (scores * weights).astype(BF)
        out_ref[heads, :] = jnp.dot(v_ref[heads, :], probs, preferred_element_type=F32)


def inner_part(queries, keys, values, cumulative, labels):
    return pl.pallas_call(
        inner_kernel,
        out_shape=jax.ShapeDtypeStruct((HEADS * DH, TOKENS), F32),
        in_specs=[VMEM] * 5,
        out_specs=VMEM,
        cost_estimate=cost(5 * 10**9, 4 * 10**6),
    )(queries, keys, values, cumulative, labels)


def mix_kernel(q_ref, inner_ref, cumulative_ref, before_ref, out_ref):
    for h in range(HEADS):
        heads = pl.ds(DH * h, DH)
        carried = jnp.dot(
            before_ref[heads, :][:, 0:DH], q_ref[heads, :], preferred_element_type=F32
        )
        numerator = inner_ref[heads, :] + carried * (
            jnp.exp(cumulative_ref[h : h + 1, :]) * (DH**-0.5)
        )
        mean = jnp.sum(numerator * numerator, axis=0, keepdims=True) * (1.0 / DH)
        out_ref[heads, :] = (numerator * lax.rsqrt(mean + 1e-06)).astype(BF)


def mix(queries, inner, cumulative, before):
    return pl.pallas_call(
        mix_kernel,
        out_shape=jax.ShapeDtypeStruct((HEADS * DH, TOKENS), BF),
        in_specs=[VMEM] * 4,
        out_specs=VMEM,
        cost_estimate=cost(10**8, 4 * 10**6),
    )(queries, inner, cumulative, in_vmem(before))


def piece_table(place_ref):
    c, xl = place_ref[0], place_ref[1]
    for hr in range(2):
        for z in range(8):
            for xr in range(2):
                h = c if hr == 0 else 1 - c
                x = xl if xr == 0 else 1 - xl
                yield hr * 16 + z * 2 + xr, 2 * (8 * x + z) + h, 4 * z + 2 * xr + h


def norm_kernel(place_ref, t0, t1, t2, t3, latent_ref, vector_ref, hidden_ref, normed_ref, work):
    sums = jnp.zeros((PADDED, SHARE), F32)
    for own, natural, term in piece_table(place_ref):
        attention = sum(t[term].astype(F32) for t in (t0, t1, t2, t3))
        hidden = latent_ref[natural].astype(F32) + vector_ref[natural][:, 3:4] * attention
        hidden_ref[own] = hidden
        sums = sums + hidden
    mean = jnp.sum(sums, axis=0, keepdims=True) * (1.0 / WIDTH)
    real = lax.broadcasted_iota(jnp.int32, (PADDED, SHARE), 0) < PIECE
    squares = jnp.zeros((PADDED, SHARE), F32)
    for own in range(PIECES):
        centered = hidden_ref[own] - mean
        squares = squares + centered * centered
    squares = jnp.where(real, squares, 0.0)
    scaling = lax.rsqrt(jnp.sum(squares, axis=0, keepdims=True) * (1.0 / WIDTH) + 1e-06)
    for own, natural, _ in piece_table(place_ref):
        vectors = vector_ref[natural]
        normed = (hidden_ref[own] - mean) * scaling * (1.0 + vectors[:, 1:2]) + vectors[:, 0:1]
        work[own * PADDED : (own + 1) * PADDED, :] = jnp.where(real, normed, 0.0)
    for i in range(ROWS // 256):
        normed_ref[:, 256 * i : 256 * (i + 1)] = work[256 * i : 256 * (i + 1), :].T.astype(BF)


def norm(place, terms, latents, vectors):
    return pl.pallas_call(
        norm_kernel,
        out_shape=(
            jax.ShapeDtypeStruct((PIECES, PADDED, SHARE), F32),
            jax.ShapeDtypeStruct((SHARE, ROWS), BF),
        ),
        in_specs=[SMEM] + [VMEM] * 6,
        out_specs=(VMEM, VMEM),
        scratch_shapes=[pltpu.VMEM((ROWS, SHARE), F32)],
        cost_estimate=cost(10**7, 8 * 10**6),
    )(place, *[in_vmem(t.reshape(PIECES, PADDED, SHARE)) for t in terms], latents, vectors)


def last_kernel(place_ref, step_ref, f0, f1, f2, f3, hidden_ref, latent_ref, vector_ref, v_ref, a_ref, v_work, a_work):
    step = step_ref[0]
    c, xl = place_ref[0], place_ref[1]
    for natural in range(PIECES):
        f, h = natural // 2, natural % 2
        hr = c if h == 0 else 1 - c
        xr = xl if f < 8 else 1 - xl
        own = hr * 16 + (f % 8) * 2 + xr
        feed = sum(f[own].astype(F32) for f in (f0, f1, f2, f3))
        velocity = (hidden_ref[own] + vector_ref[natural][:, 2:3] * feed).astype(BF).astype(F32)
        rows = slice(PIECE * natural, PIECE * (natural + 1))
        v_work[rows, :] = velocity[:PIECE]
        a_work[rows, :] = (latent_ref[natural].astype(F32) + step * velocity)[:PIECE]
    v_ref[...] = v_work[...].astype(BF)
    a_ref[...] = a_work[...].astype(BF)


def last(place, step_size, feeds, hidden, latents, vectors):
    shape = jax.ShapeDtypeStruct((WIDTH, SHARE), BF)
    return pl.pallas_call(
        last_kernel,
        out_shape=(shape, shape),
        in_specs=[SMEM] * 2 + [VMEM] * 7,
        out_specs=(VMEM, VMEM),
        scratch_shapes=[pltpu.VMEM((WIDTH, SHARE), F32)] * 2,
        cost_estimate=cost(10**7, 8 * 10**6),
    )(place, step_size, *[in_vmem(f.reshape(PIECES, PADDED, SHARE)) for f in feeds], hidden, latents, vectors)


HALF = ROWS // 2


def units_kernel(chunks, *refs):
    token_refs = refs[:chunks]
    own_ref, other_ref = refs[chunks : chunks + 2]
    out_refs = refs[chunks + 2 : 2 * chunks + 2]
    tokens, sums, units = refs[2 * chunks + 2 :]
    step = pl.program_id(0)

    def up(ref, first):
        weight = ref[...].reshape(HALF, -1)
        return jnp.dot(tokens[:, first : first + HALF], weight, preferred_element_type=F32)

    def down(ref):
        weight = ref[...].reshape(HALF, -1)
        feed = lax.dot_general(
            weight, units[...], (((1,), (1,)), ((), ())), preferred_element_type=F32
        ).astype(BF)
        for n in range(chunks):
            out_refs[n][...] = feed[:, SHARE * n : SHARE * (n + 1)]

    @pl.when(step == 0)
    def _():
        for n in range(chunks):
            tokens[SHARE * n : SHARE * (n + 1), :] = token_refs[n][...]
        sums[...] = up(own_ref, 0)

    @pl.when(step == 1)
    def _():
        units[...] = jax.nn.gelu(sums[...] + up(other_ref, HALF), approximate=True).astype(BF)

    @pl.when(step == 2)
    def _():
        down(own_ref)

    @pl.when(step == 3)
    def _():
        down(other_ref)


def unit_terms(tokens, own, other):
    chunks = len(tokens)
    hidden_units = own.shape[4]
    block = (8, 2, 1, PADDED, hidden_units)
    return pl.pallas_call(
        functools.partial(units_kernel, chunks),
        grid=(4,),
        out_shape=[jax.ShapeDtypeStruct((ROWS, SHARE), BF)] * chunks,
        in_specs=[pl.BlockSpec((SHARE, ROWS), lambda i: (0, 0))] * chunks
        + [
            pl.BlockSpec(block, lambda i: (0, 0, jnp.where(i >= 2, 1, 0), 0, 0)),
            pl.BlockSpec(block, lambda i: (0, 0, jnp.where(i >= 3, 1, 0), 0, 0)),
        ],
        out_specs=[pl.BlockSpec((HALF, SHARE), lambda i: (jnp.where(i >= 3, 1, 0), 0))] * chunks,
        scratch_shapes=[
            pltpu.VMEM((SHARE * chunks, ROWS), BF),
            pltpu.VMEM((SHARE * chunks, hidden_units), F32),
            pltpu.VMEM((SHARE * chunks, hidden_units), BF),
        ],
        cost_estimate=cost(4 * SHARE * chunks * ROWS * hidden_units, 4 * ROWS * hidden_units),
    )(*tokens, own, other)


def block(
    latents, queries, keys, values, log_decay, block_ids, t_index, w_mod, w_out, w_up, w_down
):
    y, c, xl = lax.axis_index("y"), lax.axis_index("c"), lax.axis_index("xl")
    place = jnp.stack([c, xl]).astype(jnp.int32)

    out_mine = padded_pieces(w_out.T).reshape(2 * PADDED, -1)
    out_pair = jnp.stack([out_mine, along_x(out_mine, 1)])
    out_weight = lax.all_gather(out_pair, "z", axis=0).reshape(ROWS, -1)
    both = jnp.stack([padded_pieces(w_up), padded_pieces(w_down.T)])
    mine = jnp.where(c == 0, both[:, 0], both[:, 1])

    queries, keys, values = queries.T, keys.T, values.T
    cumulative, packed = own_state(keys, values, log_decay)
    slices = lax.all_to_all(packed.reshape(16, -1, SHARE), ("xl", "z"), 0, 0)
    mine, _ = lax.optimization_barrier((mine, slices))
    mine_x = along_x(mine, 1)
    ahead = scan_blocks(slices)
    before = lax.all_to_all(ahead, ("xl", "z"), 0, 0).reshape(STATE_ROWS, SHARE)
    mine, mine_x, _ = lax.optimization_barrier((mine, mine_x, before))
    pair = jnp.stack([mine, mine_x])
    half = lax.all_gather(pair, "z", axis=0)
    inner = inner_part(queries, keys, values, cumulative, block_ids[None, :])
    mixed = mix(queries, inner, cumulative, before)

    def head_terms(d):
        tokens = lax.dynamic_slice_in_dim(mixed, ((y + d) % 4) * SHARE, SHARE, axis=1)
        return jnp.dot(out_weight, tokens, preferred_element_type=F32).astype(BF)

    terms = [along_y(head_terms(d), d) for d in (2, 1, 3)] + [head_terms(0)]

    shifts, step_size = modulation_of(t_index, w_mod)
    vectors = padded_pieces(shifts.reshape(4, WIDTH).T)
    latent_pieces = padded_pieces(latents.T)
    hidden, normed = norm(place, terms, latent_pieces, vectors)

    theirs = {d: along_y(normed, -d) for d in (1, 3, 2)}
    half, _ = lax.optimization_barrier((half, theirs))
    other = other_core(half)
    near = unit_terms([theirs[1], theirs[3]], half, other)
    feeds = []
    for d, part in zip((1, 3), near):
        feeds.append(along_y(part, d))
    normed, _ = lax.optimization_barrier((normed, near[0]))
    rest = unit_terms([normed, theirs[2]], half, other)
    feeds += [rest[0], along_y(rest[1], 2)]
    step = step_size[None] if step_size.ndim == 0 else step_size
    velocity, advanced = last(place, step, feeds, hidden, latent_pieces, vectors)
    return (velocity.T, advanced.T)


def solution(mesh):
    fine = Mesh(mesh.devices.reshape(tuple(AXES.values())), tuple(AXES))
    pool, frame = ("xh", "c"), ("xl", "z")
    rows = P(pool + frame + ("y",), None)
    return jax.shard_map(
        block,
        mesh=fine,
        in_specs=(
            rows,
            P(pool + frame, "y"),
            P(pool + frame, "y"),
            P(pool + frame, "y"),
            P("y", pool + frame),
            P(pool + frame),
            P(pool),
            P(),
            P("y", frame),
            P(frame, "y"),
            P("y", frame),
        ),
        out_specs=(rows, rows),
        check_vma=False,
    )
```

profile of v0, /device:TPU:1, one launch (start us, length us, event | category | flops | bytes accessed | tf_op | source)
XLA Modules:
  0.0 202.2 jit_solution(13566500474618192262)
XLA Ops:
  8.3 2.1 %collective-permute-start = (bf16[144,560]{1,0:T(8,128)(2,1)S(1)}, bf16[144,560]{1,0:T(8,128)(2,1)S(1)}, u32[]{:S(2)}, u32[]{:S(2)}) collective-permute-start(bf16[144,560]{1,0:T(8,128)(2,1)S(1)} %bitcast.63), channel_id=1, source_target_pairs={{0,32},{32,128},{128,160},{160,0},{1,33},{33,129},{129,161},{161,1... | collective-permute-start | bytes 483848 | tf_op jit(solution)/shard_map/ppermute | solution.py:37
  10.4 4.2 %collective-permute-done = bf16[144,560]{1,0:T(8,128)(2,1)S(1)} collective-permute-done((bf16[144,560]{1,0:T(8,128)(2,1)S(1)}, bf16[144,560]{1,0:T(8,128)(2,1)S(1)}, u32[]{:S(2)}, u32[]{:S(2)}) %collective-permute-start) | collective-permute-done | bytes 161312 | tf_op jit(solution)/shard_map/ppermute | solution.py:37
  15.4 2.7 %shard_map.122 = (f32[5,512]{1,0:T(8,128)}, bf16[640,128]{1,0:T(8,128)(2,1)}) custom-call(bf16[560,512]{1,0:T(8,128)(2,1)} %bitcast.74, bf16[560,512]{1,0:T(8,128)(2,1)} %bitcast.76, f32[5,512]{1,0:T(8,128)} %decay_ref.1), custom_call_target="tpu_custom_call" | custom-call | flops 1000000000 | bytes 3000000 | tf_op jit(solution)/shard_map/pallas_call | solution.py:122
  18.1 9.6 %all-to-all-start = ((bf16[16,40,128]{2,1,0:T(8,128)(2,1)}), bf16[16,40,128]{2,1,0:T(8,128)(2,1)S(1)}, u32[]{:S(2)}, u32[]{:S(2)}) async-start(bf16[16,40,128]{2,1,0:T(8,128)(2,1)} %bitcast.72), calls=%async_computation | async-start | bytes 327680 | tf_op jit(solution)/shard_map/all_to_all | solution.py:357
  28.1 7.0 %all-to-all-done.blocks_ref = bf16[16,40,128]{2,1,0:T(8,128)(2,1)S(1)} async-done(((bf16[16,40,128]{2,1,0:T(8,128)(2,1)}), bf16[16,40,128]{2,1,0:T(8,128)(2,1)S(1)}, u32[]{:S(2)}, u32[]{:S(2)}) %all-to-all-start) | async-done | bytes 163872 | tf_op jit(solution)/shard_map/all_to_all | solution.py:357
  35.9 1.6 shard_map.124
  37.5 12.6 %all_to_all.10 = bf16[16,40,128]{2,1,0:T(8,128)(2,1)S(1)} all-to-all(bf16[16,40,128]{2,1,0:T(8,128)(2,1)} %shard_map.124), channel_id=1, replica_groups=mesh['xh'=2,'c'=2,'xl'=2,'z'=8,'y'=4] {'xl','z'}, dimensions={0} | all-to-all | bytes 327680 | tf_op jit(solution)/shard_map/all_to_all | solution.py:361
  51.8 4.9 %shard_map.123.inner_ref = f32[560,512]{1,0:T(8,128)} custom-call(bf16[560,512]{1,0:T(8,128)(2,1)} %bitcast.65, bf16[560,512]{1,0:T(8,128)(2,1)} %bitcast.75, bf16[560,512]{1,0:T(8,128)(2,1)} %bitcast.77, f32[5,512]{1,0:T(8,128)} %get-tuple-element.17.cumulative_ref, s32[1,512]{1,0:T(1,128)} %bitcast.80), custom_call_target="tpu_custom_call" | custom-call | flops 5000000000 | bytes 4000000 | tf_op jit(solution)/shard_map/pallas_call | solution.py:171
  56.7 2.7 %shard_map.125 = bf16[560,512]{1,0:T(8,128)(2,1)} custom-call(bf16[560,512]{1,0:T(8,128)(2,1)} %bitcast.66, f32[560,512]{1,0:T(8,128)} %shard_map.123.inner_ref, f32[5,512]{1,0:T(8,128)} %get-tuple-element.17.cumulative_ref, bf16[640,128]{1,0:T(8,128)(2,1)S(1)} %bitcast.45), custom_call_target="tpu_custom_call" | custom-call | flops 100000000 | bytes 4000000 | tf_op jit(solution)/shard_map/pallas_call | solution.py:194
  59.4 7.4 %all-gather.5.cloned.1.call-done = bf16[16,144,560]{2,1,0:T(8,128)(2,1)} async-done(((bf16[2,144,560]{2,1,0:T(8,128)(2,1)}), bf16[16,144,560]{2,1,0:T(8,128)(2,1)}) %all-gather.5.cloned.1.call-update) | async-done | bytes 2580496 | tf_op jit(solution)/shard_map/all_gather | solution.py:351
  66.8 3.8 %convolution_convert_fusion.3 = bf16[2304,128]{1,0:T(8,128)(2,1)} fusion(bf16[2304,560]{1,0:T(8,128)(2,1)} %bitcast.53, bf16[560,512]{1,0:T(8,128)(2,1)} %shard_map.125, s32[]{:T(128)S(6)} %select_n.43), kind=kOutput, calls=%fused_computation.3 | convolution fusion | flops 330596352 | bytes 3682308 | tf_op jit(solution)/shard_map/dot_general | solution.py:370
  70.7 3.0 %collective-permute-start.1 = (bf16[2304,128]{1,0:T(8,128)(2,1)}, bf16[2304,128]{1,0:T(8,128)(2,1)S(1)}, u32[]{:S(2)}, u32[]{:S(2)}) collective-permute-start(bf16[2304,128]{1,0:T(8,128)(2,1)} %convolution_convert_fusion.3), channel_id=1, source_target_pairs={{0,2},{1,3},{2,0},{3,1},{4,6},{5,7},{6,4},{7,5},{8,10},{9,11},{10,... | collective-permute-start | bytes 1769480 | tf_op jit(solution)/shard_map/ppermute | solution.py:37
  73.6 1.8 convolution_convert_fusion.2
  75.8 1.8 convolution_convert_fusion.1
  77.7 2.3 %collective-permute-start.3 = (bf16[2304,128]{1,0:T(8,128)(2,1)}, bf16[2304,128]{1,0:T(8,128)(2,1)S(1)}, u32[]{:S(2)}, u32[]{:S(2)}) collective-permute-start(bf16[2304,128]{1,0:T(8,128)(2,1)} %convolution_convert_fusion.1), channel_id=1, source_target_pairs={{0,3},{1,0},{2,1},{3,2},{4,7},{5,4},{6,5},{7,6},{8,11},{9,8},{10,9... | collective-permute-start | bytes 1769480 | tf_op jit(solution)/shard_map/ppermute | solution.py:37
  82.6 1.3 copy.14
  83.9 1.1 pad.21.vector_ref
  85.6 2.8 %convolution_convert_fusion = bf16[2304,128]{1,0:T(8,128)(2,1)S(1)} fusion(bf16[2304,560]{1,0:T(8,128)(2,1)} %bitcast.54, bf16[560,512]{1,0:T(8,128)(2,1)S(1)} %copy-done.2, s32[]{:T(128)S(6)} %select_n.49), kind=kOutput, calls=%fused_computation | convolution fusion | flops 330596352 | bytes 3313668 | tf_op jit(solution)/shard_map/dot_general | solution.py:370
  88.3 12.0 %collective-permute-done.2 = bf16[2304,128]{1,0:T(8,128)(2,1)S(1)} collective-permute-done((bf16[2304,128]{1,0:T(8,128)(2,1)}, bf16[2304,128]{1,0:T(8,128)(2,1)S(1)}, u32[]{:S(2)}, u32[]{:S(2)}) %collective-permute-start.2) | collective-permute-done | bytes 589856 | tf_op jit(solution)/shard_map/ppermute | solution.py:37
  100.4 3.8 %shard_map.126 = (f32[32,72,128]{2,1,0:T(8,128)}, bf16[128,2304]{1,0:T(8,128)(2,1)}) custom-call(s32[2]{0:T(128)} %pad_add_fusion.place_ref, bf16[32,72,128]{2,1,0:T(8,128)(2,1)S(1)} %bitcast.46, bf16[32,72,128]{2,1,0:T(8,128)(2,1)S(1)} %bitcast.47, bf16[32,72,128]{2,1,0:T(8,128)(2,1)S(1)} %bitcast.48, bf16[32,72,128]{2,1,0:T(8,128)(2,1)S(1)} %bitcast.44, ...), custom_call_target="tpu_custom_call" | custom-call | flops 10000000 | bytes 8000000 | tf_op jit(solution)/shard_map/pallas_call | solution.py:237
  104.2 3.0 %collective-permute-start.7 = (bf16[128,2304]{1,0:T(8,128)(2,1)}, bf16[128,2304]{1,0:T(8,128)(2,1)S(1)}, u32[]{:S(2)}, u32[]{:S(2)}) collective-permute-start(bf16[128,2304]{1,0:T(8,128)(2,1)} %get-tuple-element.26.refs_0_), channel_id=1, source_target_pairs={{0,2},{1,3},{2,0},{3,1},{4,6},{5,7},{6,4},{7,5},{8,10},{9,11},{10,... | collective-permute-start | bytes 1769480 | tf_op jit(solution)/shard_map/ppermute | solution.py:37
  107.6 2.3 %collective-permute-start.4 = (bf16[128,2304]{1,0:T(8,128)(2,1)}, bf16[128,2304]{1,0:T(8,128)(2,1)S(1)}, u32[]{:S(2)}, u32[]{:S(2)}) collective-permute-start(bf16[128,2304]{1,0:T(8,128)(2,1)} %get-tuple-element.26.refs_0_), channel_id=1, source_target_pairs={{0,3},{1,0},{2,1},{3,2},{4,7},{5,4},{6,5},{7,6},{8,11},{9,8},{10,9... | collective-permute-start | bytes 1769480 | tf_op jit(solution)/shard_map/ppermute | solution.py:37
  109.9 10.2 %collective-permute-done.7.refs_1_ = bf16[128,2304]{1,0:T(8,128)(2,1)S(1)} collective-permute-done((bf16[128,2304]{1,0:T(8,128)(2,1)}, bf16[128,2304]{1,0:T(8,128)(2,1)S(1)}, u32[]{:S(2)}, u32[]{:S(2)}) %collective-permute-start.7) | collective-permute-done | bytes 589856 | tf_op jit(solution)/shard_map/ppermute | solution.py:37
  120.1 13.7 %collective-permute-done.5.refs_1_ = bf16[128,2304]{1,0:T(8,128)(2,1)S(1)} collective-permute-done((bf16[128,2304]{1,0:T(8,128)(2,1)}, bf16[128,2304]{1,0:T(8,128)(2,1)S(1)}, u32[]{:S(2)}, u32[]{:S(2)}) %collective-permute-start.5) | collective-permute-done | bytes 589856 | tf_op jit(solution)/shard_map/ppermute | solution.py:37
  134.8 8.7 %collective-permute-done.8.refs_3_ = bf16[8,2,2,72,1120]{4,3,2,1,0:T(8,128)(2,1)} collective-permute-done((bf16[8,2,2,72,1120]{4,3,2,1,0:T(8,128)(2,1)}, bf16[8,2,2,72,1120]{4,3,2,1,0:T(8,128)(2,1)}, u32[]{:S(2)}, u32[]{:S(2)}) %collective-permute-start.8) | collective-permute-done | bytes 5160992 | tf_op jit(solution)/shard_map/ppermute | solution.py:37
  143.5 8.7 %shard_map.127 = (bf16[2304,128]{1,0:T(8,128)(2,1)}, bf16[2304,128]{1,0:T(8,128)(2,1)}) custom-call(bf16[128,2304]{1,0:T(8,128)(2,1)} %copy-done.5, bf16[128,2304]{1,0:T(8,128)(2,1)} %copy-done.4, bf16[8,2,2,72,1120]{4,3,2,1,0:T(8,128)(2,1)} %bitcast.58, bf16[8,2,2,72,1120]{4,3,2,1,0:T(8,128)(2,1)} %collective-permute-done.8.refs_3_), custom_call_target="tpu_custom_call" | custom-call | flops 2642411520 | bytes 10321920 | tf_op jit(solution)/shard_map/pallas_call | solution.py:324
  152.3 8.8 %shard_map.128 = (bf16[2304,128]{1,0:T(8,128)(2,1)}, bf16[2304,128]{1,0:T(8,128)(2,1)}) custom-call(bf16[128,2304]{1,0:T(8,128)(2,1)} %get-tuple-element.26.refs_0_, bf16[128,2304]{1,0:T(8,128)(2,1)} %copy-done.3, bf16[8,2,2,72,1120]{4,3,2,1,0:T(8,128)(2,1)} %bitcast.59, bf16[8,2,2,72,1120]{4,3,2,1,0:T(8,128)(2,1)} %collective-permute-done.8.refs_3_), custom_call_target="tpu_custom_call" | custom-call | flops 2642411520 | bytes 10321920 | tf_op jit(solution)/shard_map/pallas_call | solution.py:324
  161.1 2.1 %collective-permute-start.11 = (bf16[2304,128]{1,0:T(8,128)(2,1)}, bf16[2304,128]{1,0:T(8,128)(2,1)S(1)}, u32[]{:S(2)}, u32[]{:S(2)}) collective-permute-start(bf16[2304,128]{1,0:T(8,128)(2,1)} %get-tuple-element.28), channel_id=1, source_target_pairs={{0,2},{1,3},{2,0},{3,1},{4,6},{5,7},{6,4},{7,5},{8,10},{9,11},{10,... | collective-permute-start | bytes 1769480 | tf_op jit(solution)/shard_map/ppermute | solution.py:37
  163.2 1.7 collective-permute-start.10
  165.0 12.4 %collective-permute-done.11 = bf16[2304,128]{1,0:T(8,128)(2,1)S(1)} collective-permute-done((bf16[2304,128]{1,0:T(8,128)(2,1)}, bf16[2304,128]{1,0:T(8,128)(2,1)S(1)}, u32[]{:S(2)}, u32[]{:S(2)}) %collective-permute-start.11) | collective-permute-done | bytes 589856 | tf_op jit(solution)/shard_map/ppermute | solution.py:37
  177.4 12.6 %collective-permute-done.10 = bf16[2304,128]{1,0:T(8,128)(2,1)S(1)} collective-permute-done((bf16[2304,128]{1,0:T(8,128)(2,1)S(1)}, bf16[2304,128]{1,0:T(8,128)(2,1)S(1)}, u32[]{:S(2)}, u32[]{:S(2)}) %collective-permute-start.10) | collective-permute-done | bytes 589856 | tf_op jit(solution)/shard_map/ppermute | solution.py:37
  191.8 3.6 %shard_map.129 = (bf16[2240,128]{1,0:T(8,128)(2,1)}, bf16[2240,128]{1,0:T(8,128)(2,1)}) custom-call(s32[2]{0:T(128)} %pad_add_fusion.place_ref, f32[1]{0:T(128)S(6)} %sub.13.step_ref, bf16[32,72,128]{2,1,0:T(8,128)(2,1)S(1)} %bitcast.52, bf16[32,72,128]{2,1,0:T(8,128)(2,1)S(1)} %bitcast.51, bf16[32,72,128]{2,1,0:T(8,128)(2,1)S(1)} %bitcast.49, ...), custom_call_target="tpu_custom_call" | custom-call | flops 10000000 | bytes 8000000 | tf_op jit(solution)/shard_map/pallas_call | solution.py:269
  (59 shorter events, 10.6 us)
Async XLA Ops:
  7.2 20.6 %copy-start.7 = (bf16[140,1120]{1,0:T(8,128)(2,1)S(1)}, bf16[140,1120]{1,0:T(8,128)(2,1)}, u32[]{:S(2)}) copy-start(bf16[140,1120]{1,0:T(8,128)(2,1)} %param.20) | copy-start | bytes 940804
  7.2 59.7 %all-gather.5.cloned.1.call-start = ((), (), s32[]{:S(2)}) async-start(), calls=%async_computation.2 | async-start | bytes 3317760 | tf_op jit(solution)/shard_map/all_gather | solution.py:351
  8.3 19.6 %copy-start.8 = (bf16[1120,140]{0,1:T(8,128)(2,1)S(1)}, bf16[1120,140]{0,1:T(8,128)(2,1)}, u32[]{:S(2)}) copy-start(bf16[1120,140]{0,1:T(8,128)(2,1)} %param.21) | copy-start | bytes 940804
  8.3 6.3 %collective-permute-start = (bf16[144,560]{1,0:T(8,128)(2,1)S(1)}, bf16[144,560]{1,0:T(8,128)(2,1)S(1)}, u32[]{:S(2)}, u32[]{:S(2)}) collective-permute-start(bf16[144,560]{1,0:T(8,128)(2,1)S(1)} %bitcast.63), channel_id=1, source_target_pairs={{0,32},{32,128},{128,160},{160,0},{1,33},{33,129},{129,161},{161,1... | collective-permute-start | bytes 483848 | tf_op jit(solution)/shard_map/ppermute | solution.py:37
  18.1 17.1 %all-to-all-start = ((bf16[16,40,128]{2,1,0:T(8,128)(2,1)}), bf16[16,40,128]{2,1,0:T(8,128)(2,1)S(1)}, u32[]{:S(2)}, u32[]{:S(2)}) async-start(bf16[16,40,128]{2,1,0:T(8,128)(2,1)} %bitcast.72), calls=%async_computation | async-start | bytes 327680 | tf_op jit(solution)/shard_map/all_to_all | solution.py:357
  27.7 106.2 %all-gather.7.cloned.1.call-start = ((), (), s32[]{:S(2)}) async-start(), calls=%async_computation.3 | async-start | bytes 5971968 | tf_op jit(solution)/shard_map/all_gather | solution.py:364
  35.1 14.9 %collective-permute-start.6 = (bf16[2,72,1120]{2,1,0:T(8,128)(2,1)S(1)}, bf16[2,72,1120]{2,1,0:T(8,128)(2,1)S(1)}, u32[]{:S(2)}, u32[]{:S(2)}) collective-permute-start(bf16[2,72,1120]{2,1,0:T(8,128)(2,1)S(1)} %fusion.2), channel_id=1, source_target_pairs={{0,32},{32,128},{128,160},{160,0},{1,33},{33,129},{129,161},{161,1... | collective-permute-start | bytes 967688 | tf_op jit(solution)/shard_map/ppermute | solution.py:37
  59.4 14.2 %copy-start.2 = (bf16[560,512]{1,0:T(8,128)(2,1)S(1)}, bf16[560,512]{1,0:T(8,128)(2,1)}, u32[]{:S(2)}) copy-start(bf16[560,512]{1,0:T(8,128)(2,1)} %shard_map.125) | copy-start | bytes 1720324
  66.8 6.8 %copy-start.1 = (bf16[16,144,560]{2,1,0:T(8,128)(2,1)S(1)}, bf16[16,144,560]{2,1,0:T(8,128)(2,1)}, u32[]{:S(2)}) copy-start(bf16[16,144,560]{2,1,0:T(8,128)(2,1)} %all-gather.5.cloned.1.call-done) | copy-start | bytes 7741444
  66.8 13.1 %slice-start = ((s8[4587520]{0:T(1024)(128)(4,1)}), s8[4194304]{0:T(1024)(128)(4,1)S(1)}, s32[]{:S(2)}) async-start(s8[4587520]{0:T(1024)(128)(4,1)} %bitcast.60), calls=%async_computation.4 | async-start | bytes 8388608
  70.6 9.3 %slice-start.1 = ((s8[4587520]{0:T(1024)(128)(4,1)}), s8[393216]{0:T(1024)(128)(4,1)S(1)}, s32[]{:S(2)}) async-start(s8[4587520]{0:T(1024)(128)(4,1)} %bitcast.60), calls=%async_computation.5 | async-start | bytes 786432
  70.7 17.7 %collective-permute-start.1 = (bf16[2304,128]{1,0:T(8,128)(2,1)}, bf16[2304,128]{1,0:T(8,128)(2,1)S(1)}, u32[]{:S(2)}, u32[]{:S(2)}) collective-permute-start(bf16[2304,128]{1,0:T(8,128)(2,1)} %convolution_convert_fusion.3), channel_id=1, source_target_pairs={{0,2},{1,3},{2,0},{3,1},{4,6},{5,7},{6,4},{7,5},{8,10},{9,11},{10,... | collective-permute-start | bytes 1769480 | tf_op jit(solution)/shard_map/ppermute | solution.py:37
  75.4 24.9 %collective-permute-start.2 = (bf16[2304,128]{1,0:T(8,128)(2,1)}, bf16[2304,128]{1,0:T(8,128)(2,1)S(1)}, u32[]{:S(2)}, u32[]{:S(2)}) collective-permute-start(bf16[2304,128]{1,0:T(8,128)(2,1)} %convolution_convert_fusion.2), channel_id=1, source_target_pairs={{0,1},{1,2},{2,3},{3,0},{4,5},{5,6},{6,7},{7,4},{8,9},{9,10},{10,1... | collective-permute-start | bytes 1769480 | tf_op jit(solution)/shard_map/ppermute | solution.py:37
  77.7 3.9 %copy-start.6 = (bf16[128,2240]{0,1:T(8,128)(2,1)S(1)}, bf16[128,2240]{0,1:T(8,128)(2,1)}, u32[]{:S(2)}) copy-start(bf16[128,2240]{0,1:T(8,128)(2,1)} %param.11) | copy-start | bytes 1720324
  77.7 22.7 %collective-permute-start.3 = (bf16[2304,128]{1,0:T(8,128)(2,1)}, bf16[2304,128]{1,0:T(8,128)(2,1)S(1)}, u32[]{:S(2)}, u32[]{:S(2)}) collective-permute-start(bf16[2304,128]{1,0:T(8,128)(2,1)} %convolution_convert_fusion.1), channel_id=1, source_target_pairs={{0,3},{1,0},{2,1},{3,2},{4,7},{5,4},{6,5},{7,6},{8,11},{9,8},{10,9... | collective-permute-start | bytes 1769480 | tf_op jit(solution)/shard_map/ppermute | solution.py:37
  104.2 15.9 %collective-permute-start.7 = (bf16[128,2304]{1,0:T(8,128)(2,1)}, bf16[128,2304]{1,0:T(8,128)(2,1)S(1)}, u32[]{:S(2)}, u32[]{:S(2)}) collective-permute-start(bf16[128,2304]{1,0:T(8,128)(2,1)} %get-tuple-element.26.refs_0_), channel_id=1, source_target_pairs={{0,2},{1,3},{2,0},{3,1},{4,6},{5,7},{6,4},{7,5},{8,10},{9,11},{10,... | collective-permute-start | bytes 1769480 | tf_op jit(solution)/shard_map/ppermute | solution.py:37
  107.2 26.6 %collective-permute-start.5 = (bf16[128,2304]{1,0:T(8,128)(2,1)}, bf16[128,2304]{1,0:T(8,128)(2,1)S(1)}, u32[]{:S(2)}, u32[]{:S(2)}) collective-permute-start(bf16[128,2304]{1,0:T(8,128)(2,1)} %get-tuple-element.26.refs_0_), channel_id=1, source_target_pairs={{0,1},{1,2},{2,3},{3,0},{4,5},{5,6},{6,7},{7,4},{8,9},{9,10},{10,1... | collective-permute-start | bytes 1769480 | tf_op jit(solution)/shard_map/ppermute | solution.py:37
  107.6 26.3 %collective-permute-start.4 = (bf16[128,2304]{1,0:T(8,128)(2,1)}, bf16[128,2304]{1,0:T(8,128)(2,1)S(1)}, u32[]{:S(2)}, u32[]{:S(2)}) collective-permute-start(bf16[128,2304]{1,0:T(8,128)(2,1)} %get-tuple-element.26.refs_0_), channel_id=1, source_target_pairs={{0,3},{1,0},{2,1},{3,2},{4,7},{5,4},{6,5},{7,6},{8,11},{9,8},{10,9... | collective-permute-start | bytes 1769480 | tf_op jit(solution)/shard_map/ppermute | solution.py:37
  120.1 32.1 %copy-start.3 = (bf16[128,2304]{1,0:T(8,128)(2,1)}, bf16[128,2304]{1,0:T(8,128)(2,1)S(1)}, u32[]{:S(2)}) copy-start(bf16[128,2304]{1,0:T(8,128)(2,1)S(1)} %collective-permute-done.7.refs_1_) | copy-start | bytes 1769476
  133.8 9.7 %copy-start.4 = (bf16[128,2304]{1,0:T(8,128)(2,1)}, bf16[128,2304]{1,0:T(8,128)(2,1)S(1)}, u32[]{:S(2)}) copy-start(bf16[128,2304]{1,0:T(8,128)(2,1)S(1)} %collective-permute-done.5.refs_1_) | copy-start | bytes 1769476
  133.8 9.7 %copy-start.5 = (bf16[128,2304]{1,0:T(8,128)(2,1)}, bf16[128,2304]{1,0:T(8,128)(2,1)S(1)}, u32[]{:S(2)}) copy-start(bf16[128,2304]{1,0:T(8,128)(2,1)S(1)} %collective-permute-done.4.refs_0_) | copy-start | bytes 1769476
  133.9 9.6 %collective-permute-start.8 = (bf16[8,2,2,72,1120]{4,3,2,1,0:T(8,128)(2,1)}, bf16[8,2,2,72,1120]{4,3,2,1,0:T(8,128)(2,1)}, u32[]{:S(2)}, u32[]{:S(2)}) collective-permute-start(bf16[8,2,2,72,1120]{4,3,2,1,0:T(8,128)(2,1)} %bitcast.57), channel_id=1, source_target_pairs={{0,64},{64,0},{1,65},{65,1},{2,66},{66,2},{3,67},{67,3},{4,68},{68... | collective-permute-start | bytes 15482888 | tf_op jit(solution)/shard_map/ppermute | solution.py:37
  152.2 10.9 %copy-start.10 = (bf16[2304,128]{1,0:T(8,128)(2,1)S(1)}, bf16[2304,128]{1,0:T(8,128)(2,1)}, u32[]{:S(2)}) copy-start(bf16[2304,128]{1,0:T(8,128)(2,1)} %get-tuple-element.25) | copy-start | bytes 1769476
  152.2 12.6 %copy-start.9 = (bf16[2304,128]{1,0:T(8,128)(2,1)S(1)}, bf16[2304,128]{1,0:T(8,128)(2,1)}, u32[]{:S(2)}) copy-start(bf16[2304,128]{1,0:T(8,128)(2,1)} %get-tuple-element.24) | copy-start | bytes 1769476
  161.1 16.3 %collective-permute-start.11 = (bf16[2304,128]{1,0:T(8,128)(2,1)}, bf16[2304,128]{1,0:T(8,128)(2,1)S(1)}, u32[]{:S(2)}, u32[]{:S(2)}) collective-permute-start(bf16[2304,128]{1,0:T(8,128)(2,1)} %get-tuple-element.28), channel_id=1, source_target_pairs={{0,2},{1,3},{2,0},{3,1},{4,6},{5,7},{6,4},{7,5},{8,10},{9,11},{10,... | collective-permute-start | bytes 1769480 | tf_op jit(solution)/shard_map/ppermute | solution.py:37
  163.2 26.8 %collective-permute-start.10 = (bf16[2304,128]{1,0:T(8,128)(2,1)S(1)}, bf16[2304,128]{1,0:T(8,128)(2,1)S(1)}, u32[]{:S(2)}, u32[]{:S(2)}) collective-permute-start(bf16[2304,128]{1,0:T(8,128)(2,1)S(1)} %copy-done.10), channel_id=1, source_target_pairs={{0,3},{1,0},{2,1},{3,2},{4,7},{5,4},{6,5},{7,6},{8,11},{9,8},{10,9... | collective-permute-start | bytes 1769480 | tf_op jit(solution)/shard_map/ppermute | solution.py:37
  164.9 25.8 %collective-permute-start.9 = (bf16[2304,128]{1,0:T(8,128)(2,1)S(1)}, bf16[2304,128]{1,0:T(8,128)(2,1)S(1)}, u32[]{:S(2)}, u32[]{:S(2)}) collective-permute-start(bf16[2304,128]{1,0:T(8,128)(2,1)S(1)} %copy-done.9), channel_id=1, source_target_pairs={{0,1},{1,2},{2,3},{3,0},{4,5},{5,6},{6,7},{7,4},{8,9},{9,10},{10,1... | collective-permute-start | bytes 1769480 | tf_op jit(solution)/shard_map/ppermute | solution.py:37
  190.7 1.1 copy-start
Sparse Core Ops, SparseCore 0:
  15.5 51.2 all-gather.4
  68.6 64.1 all-gather.6
where the time goes:
time: 203 us; the launch traced here: 202 us
  waiting for transfers between devices  89.2 us (44%)
  Pallas kernels  36.8 us (18%)
  starting transfers between devices  28.5 us (14%)
  between operations  15 us (7%)
  blocking collectives  12.6 us (6%)
  matrix products  10.9 us (5%)
  local copies, waits for them, and re-layouts  6.67 us (3%)
  other arithmetic  2.41 us (1%)
    ppermute x12, waiting for transfers between devices, permute(): return lax.ppermute(block, tuple(axes) if len(axes) > 1 else axes[0], pairs)  74.7 us
    ppermute x12, starting transfers between devices, permute(): return lax.ppermute(block, tuple(axes) if len(axes) > 1 else axes[0], pairs)  18.8 us
    pallas_call x2, Pallas kernels, unit_terms(): pl.pallas_call(functools.partial(units_kernel, chunks), grid=(4,), out_sh...  17.6 us
    all_to_all x1, blocking collectives, block(): before = lax.all_to_all(ahead, ('xl', 'z'), 0, 0).reshape(STATE_ROWS, SHARE)  12.6 us
    dot_general x4, matrix products, head_terms(): return jnp.dot(out_weight, tokens, preferred_element_type=F32).astype(BF)  10.2 us
    all_to_all x1, starting transfers between devices, block(): slices = lax.all_to_all(packed.reshape(16, -1, SHARE), ('xl', 'z'), 0, 0)  9.62 us
    all_gather x1, waiting for transfers between devices, block(): out_weight = lax.all_gather(out_pair, 'z', axis=0).reshape(ROWS, -1)  7.45 us
    all_to_all x1, waiting for transfers between devices, block(): slices = lax.all_to_all(packed.reshape(16, -1, SHARE), ('xl', 'z'), 0, 0)  7.04 us
  transfers between devices with their start and end apart: 15, of which 10 were waited for; matrix products, arithmetic and copies ran while one was open for 8% of the time, Pallas kernels for 8%

commit v1 on v0

--- a/solution.py
+++ b/solution.py
@@ -200,6 +200,33 @@
     )(queries, inner, cumulative, in_vmem(before))
 
 
+FARTHEST_FIRST = (2, 1, 3, 0)
+
+
+def head_kernel(place_ref, mixed_ref, own_ref, first_ref, second_ref, *out_refs):
+    for d, out_ref in zip(FARTHEST_FIRST, out_refs):
+        start = pl.multiple_of(((place_ref[2] + d) % 4) * SHARE, SHARE)
+        tokens = mixed_ref[:, pl.ds(start, SHARE)]
+        row = 0
+        for weight_ref in (own_ref, first_ref, second_ref):
+            weight = weight_ref[...].reshape(-1, weight_ref.shape[2])
+            rows = weight.shape[0]
+            out_ref[row : row + rows, :] = jnp.dot(
+                weight, tokens, preferred_element_type=F32
+            ).astype(BF)
+            row += rows
+
+
+def head_terms(place, mixed, weights):
+    return pl.pallas_call(
+        head_kernel,
+        out_shape=[jax.ShapeDtypeStruct((ROWS, SHARE), BF)] * 4,
+        in_specs=[SMEM] + [VMEM] * 4,
+        out_specs=[VMEM] * 4,
+        cost_estimate=cost(2 * 10**9, 5 * 10**6),
+    )(place, mixed, weights[0], *[in_vmem(w) for w in weights[1:]])
+
+
 def piece_table(place_ref):
     c, xl = place_ref[0], place_ref[1]
     for hr in range(2):
@@ -207,7 +234,7 @@
             for xr in range(2):
                 h = c if hr == 0 else 1 - c
                 x = xl if xr == 0 else 1 - xl
-                yield hr * 16 + z * 2 + xr, 2 * (8 * x + z) + h, 4 * z + 2 * xr + h
+                yield hr * 16 + z * 2 + xr, 2 * (8 * x + z) + h, 16 * xr + 2 * z + h
 
 
 def norm_kernel(place_ref, t0, t1, t2, t3, latent_ref, vector_ref, hidden_ref, normed_ref, work):
@@ -233,6 +260,11 @@
         normed_ref[:, 256 * i : 256 * (i + 1)] = work[256 * i : 256 * (i + 1), :].T.astype(BF)
 
 
+def arrived(parts):
+    pieces = [p.reshape(PIECES, PADDED, SHARE) for p in parts]
+    return [in_vmem(p) for p in pieces[:-1]] + pieces[-1:]
+
+
 def norm(place, terms, latents, vectors):
     return pl.pallas_call(
         norm_kernel,
@@ -244,7 +276,7 @@
         out_specs=(VMEM, VMEM),
         scratch_shapes=[pltpu.VMEM((ROWS, SHARE), F32)],
         cost_estimate=cost(10**7, 8 * 10**6),
-    )(place, *[in_vmem(t.reshape(PIECES, PADDED, SHARE)) for t in terms], latents, vectors)
+    )(place, *arrived(terms), latents, vectors)
 
 
 def last_kernel(place_ref, step_ref, f0, f1, f2, f3, hidden_ref, latent_ref, vector_ref, v_ref, a_ref, v_work, a_work):
@@ -273,7 +305,7 @@
         out_specs=(VMEM, VMEM),
         scratch_shapes=[pltpu.VMEM((WIDTH, SHARE), F32)] * 2,
         cost_estimate=cost(10**7, 8 * 10**6),
-    )(place, step_size, *[in_vmem(f.reshape(PIECES, PADDED, SHARE)) for f in feeds], hidden, latents, vectors)
+    )(place, step_size, *arrived(feeds), hidden, latents, vectors)
 
 
 HALF = ROWS // 2
@@ -344,11 +376,11 @@
     latents, queries, keys, values, log_decay, block_ids, t_index, w_mod, w_out, w_up, w_down
 ):
     y, c, xl = lax.axis_index("y"), lax.axis_index("c"), lax.axis_index("xl")
-    place = jnp.stack([c, xl]).astype(jnp.int32)
+    place = jnp.stack([c, xl, y]).astype(jnp.int32)
 
     out_mine = padded_pieces(w_out.T).reshape(2 * PADDED, -1)
-    out_pair = jnp.stack([out_mine, along_x(out_mine, 1)])
-    out_weight = lax.all_gather(out_pair, "z", axis=0).reshape(ROWS, -1)
+    out_own = lax.all_gather(out_mine, "z", axis=0)
+    out_first, out_second = along_x(out_own[:4], 1), along_x(out_own[4:], -1)
     both = jnp.stack([padded_pieces(w_up), padded_pieces(w_down.T)])
     mine = jnp.where(c == 0, both[:, 0], both[:, 1])
 
@@ -365,19 +397,17 @@
     inner = inner_part(queries, keys, values, cumulative, block_ids[None, :])
     mixed = mix(queries, inner, cumulative, before)
 
-    def head_terms(d):
-        tokens = lax.dynamic_slice_in_dim(mixed, ((y + d) % 4) * SHARE, SHARE, axis=1)
-        return jnp.dot(out_weight, tokens, preferred_element_type=F32).astype(BF)
-
-    terms = [along_y(head_terms(d), d) for d in (2, 1, 3)] + [head_terms(0)]
+    parts = head_terms(place, mixed, [out_own, out_first, out_second])
+    terms = [along_y(parts[i], d) for i, d in enumerate(FARTHEST_FIRST[:3])] + [parts[3]]
 
     shifts, step_size = modulation_of(t_index, w_mod)
     vectors = padded_pieces(shifts.reshape(4, WIDTH).T)
     latent_pieces = padded_pieces(latents.T)
     hidden, normed = norm(place, terms, latent_pieces, vectors)
 
-    theirs = {d: along_y(normed, -d) for d in (1, 3, 2)}
-    half, _ = lax.optimization_barrier((half, theirs))
+    theirs = {d: along_y(normed, -d) for d in (1, 3)}
+    theirs[2] = along_y(normed, -2)
+    half, _ = lax.optimization_barrier((half, (theirs[1], theirs[3])))
     other = other_core(half)
     near = unit_terms([theirs[1], theirs[3]], half, other)
     feeds = []
@@ -385,7 +415,7 @@
         feeds.append(along_y(part, d))
     normed, _ = lax.optimization_barrier((normed, near[0]))
     rest = unit_terms([normed, theirs[2]], half, other)
-    feeds += [rest[0], along_y(rest[1], 2)]
+    feeds += [along_y(rest[1], 2), rest[0]]
     step = step_size[None] if step_size.ndim == 0 else step_size
     velocity, advanced = last(place, step, feeds, hidden, latent_pieces, vectors)
     return (velocity.T, advanced.T)

time: 203 us -> 193 us (0.951)
  waiting for transfers between devices: 89.2 us -> 79.1 us
  matrix products: 10.9 us -> 3.07 us
  Pallas kernels: 36.8 us -> 42.9 us
    dot_general x4 -> x0, matrix products: 10.2 us -> none  [head_terms(): return jnp.dot(out_weight, tokens, preferred_element_type=F32).astype(BF)]
    ppermute x12 -> x13, waiting for transfers between devices: 74.7 us -> 67.4 us  [permute(): return lax.ppermute(block, tuple(axes) if len(axes) > 1 else axes[0], pairs)]
    pallas_call x0 -> x1, Pallas kernels: none -> 5.88 us  [head_terms(): pl.pallas_call(head_kernel, out_shape=[jax.ShapeDtypeStruct((ROWS, SHARE)...]
    all_gather x1, waiting for transfers between devices: 7.45 us -> 4.64 us  [block(): out_own = lax.all_gather(out_mine, 'z', axis=0)]
    dot_general x1, matrix products: 0.73 us -> 3.07 us  [modulation_of(): jnp.dot(time_features[None, :], w_mod, preferred_element_type=F32)[0]]
    ppermute x12 -> x13, starting transfers between devices: 18.8 us -> 19.6 us  [permute(): return lax.ppermute(block, tuple(axes) if len(axes) > 1 else axes[0], pairs)]
  transfers between devices with their start and end apart: 15 -> 16, of which waited for: 10 -> 10; matrix products, arithmetic and copies ran while one was open for 8% -> 5% of each run, Pallas kernels for 8% -> 16%
where the time goes in v1:
time: 193 us; the launch traced here: 192 us
  waiting for transfers between devices  79.1 us (41%)
  Pallas kernels  42.9 us (22%)
  starting transfers between devices  29.7 us (15%)
  between operations  15 us (8%)
  blocking collectives  13.5 us (7%)
  local copies, waits for them, and re-layouts  7.1 us (4%)
  matrix products  3.07 us (2%)
    ppermute x13, waiting for transfers between devices, permute(): return lax.ppermute(block, tuple(axes) if len(axes) > 1 else axes[0], pairs)  67.4 us
    ppermute x13, starting transfers between devices, permute(): return lax.ppermute(block, tuple(axes) if len(axes) > 1 else axes[0], pairs)  19.6 us
    pallas_call x2, Pallas kernels, unit_terms(): pl.pallas_call(functools.partial(units_kernel, chunks), grid=(4,), out_sh...  17.5 us
    all_to_all x1, blocking collectives, block(): before = lax.all_to_all(ahead, ('xl', 'z'), 0, 0).reshape(STATE_ROWS, SHARE)  13.5 us
    all_to_all x1, starting transfers between devices, block(): slices = lax.all_to_all(packed.reshape(16, -1, SHARE), ('xl', 'z'), 0, 0)  10 us
    all_to_all x1, waiting for transfers between devices, block(): slices = lax.all_to_all(packed.reshape(16, -1, SHARE), ('xl', 'z'), 0, 0)  7.04 us
    pallas_call x1, Pallas kernels, head_terms(): pl.pallas_call(head_kernel, out_shape=[jax.ShapeDtypeStruct((ROWS, SHARE)...  5.88 us
    pallas_call x1, Pallas kernels, inner_part(): pl.pallas_call(inner_kernel, out_shape=jax.ShapeDtypeStruct((HEADS * DH,...  4.89 us
  transfers between devices with their start and end apart: 16, of which 10 were waited for; matrix products, arithmetic and copies ran while one was open for 5% of the time, Pallas kernels for 16%

profile of v1, /device:TPU:1, one launch (start us, length us, event | category | flops | bytes accessed | tf_op | source)
XLA Modules:
  0.0 192.1 jit_solution(1958004367788208332)
XLA Ops:
  7.2 1.0 reshape.80
  9.0 2.7 %shard_map.122 = (f32[5,512]{1,0:T(8,128)}, bf16[640,128]{1,0:T(8,128)(2,1)}) custom-call(bf16[560,512]{1,0:T(8,128)(2,1)} %bitcast.60, bf16[560,512]{1,0:T(8,128)(2,1)} %bitcast.62, f32[5,512]{1,0:T(8,128)} %decay_ref.1), custom_call_target="tpu_custom_call" | custom-call | flops 1000000000 | bytes 3000000 | tf_op jit(solution)/shard_map/pallas_call | solution.py:122
  11.6 10.0 %all-to-all-start = ((bf16[16,40,128]{2,1,0:T(8,128)(2,1)}), bf16[16,40,128]{2,1,0:T(8,128)(2,1)S(1)}, u32[]{:S(2)}, u32[]{:S(2)}) async-start(bf16[16,40,128]{2,1,0:T(8,128)(2,1)} %bitcast.58), calls=%async_computation | async-start | bytes 327680 | tf_op jit(solution)/shard_map/all_to_all | solution.py:389
  22.1 7.0 %all-to-all-done.blocks_ref = bf16[16,40,128]{2,1,0:T(8,128)(2,1)S(1)} async-done(((bf16[16,40,128]{2,1,0:T(8,128)(2,1)}), bf16[16,40,128]{2,1,0:T(8,128)(2,1)S(1)}, u32[]{:S(2)}, u32[]{:S(2)}) %all-to-all-start) | async-done | bytes 163872 | tf_op jit(solution)/shard_map/all_to_all | solution.py:389
  29.9 1.6 shard_map.124
  31.5 13.5 %all_to_all.10 = bf16[16,40,128]{2,1,0:T(8,128)(2,1)S(1)} all-to-all(bf16[16,40,128]{2,1,0:T(8,128)(2,1)} %shard_map.124), channel_id=1, replica_groups=mesh['xh'=2,'c'=2,'xl'=2,'z'=8,'y'=4] {'xl','z'}, dimensions={0} | all-to-all | bytes 327680 | tf_op jit(solution)/shard_map/all_to_all | solution.py:393
  45.9 4.6 %all-gather.4.cloned.1.call-done.own_ref = bf16[8,144,560]{2,1,0:T(8,128)(2,1)} async-done(((bf16[1,144,560]{2,1,0:T(8,128)(2,1)}), bf16[8,144,560]{2,1,0:T(8,128)(2,1)}) %all-gather.4.cloned.1.call-update) | async-done | bytes 1290256 | tf_op jit(solution)/shard_map/all_gather | solution.py:382
  50.6 1.5 fusion.6
  52.0 2.8 %collective-permute-start.1 = (bf16[4,144,560]{2,1,0:T(8,128)(2,1)S(1)}, bf16[4,144,560]{2,1,0:T(8,128)(2,1)S(1)}, u32[]{:S(2)}, u32[]{:S(2)}) collective-permute-start(bf16[4,144,560]{2,1,0:T(8,128)(2,1)S(1)} %get-tuple-element.40), channel_id=1, source_target_pairs={{0,160},{32,0},{128,32},{160,128},{1,161},{33,1},{129,33},{161,129... | collective-permute-start | bytes 1935368 | tf_op jit(solution)/shard_map/ppermute | solution.py:37
  55.5 4.9 %shard_map.123.inner_ref = f32[560,512]{1,0:T(8,128)} custom-call(bf16[560,512]{1,0:T(8,128)(2,1)} %bitcast.52, bf16[560,512]{1,0:T(8,128)(2,1)} %bitcast.61, bf16[560,512]{1,0:T(8,128)(2,1)} %bitcast.63, f32[5,512]{1,0:T(8,128)} %get-tuple-element.21.cumulative_ref, s32[1,512]{1,0:T(1,128)} %bitcast.66), custom_call_target="tpu_custom_call" | custom-call | flops 5000000000 | bytes 4000000 | tf_op jit(solution)/shard_map/pallas_call | solution.py:171
  60.4 2.6 %shard_map.125.mixed_ref = bf16[560,512]{1,0:T(8,128)(2,1)} custom-call(bf16[560,512]{1,0:T(8,128)(2,1)} %bitcast.53, f32[560,512]{1,0:T(8,128)} %shard_map.123.inner_ref, f32[5,512]{1,0:T(8,128)} %get-tuple-element.21.cumulative_ref, bf16[640,128]{1,0:T(8,128)(2,1)S(1)} %bitcast.38), custom_call_target="tpu_custom_call" | custom-call | flops 100000000 | bytes 4000000 | tf_op jit(solution)/shard_map/pallas_call | solution.py:194
  63.0 2.9 %collective-permute-done.1.second_ref = bf16[4,144,560]{2,1,0:T(8,128)(2,1)S(1)} collective-permute-done((bf16[4,144,560]{2,1,0:T(8,128)(2,1)S(1)}, bf16[4,144,560]{2,1,0:T(8,128)(2,1)S(1)}, u32[]{:S(2)}, u32[]{:S(2)}) %collective-permute-start.1) | collective-permute-done | bytes 645152 | tf_op jit(solution)/shard_map/ppermute | solution.py:37
  66.0 3.1 %collective-permute-done.first_ref = bf16[4,144,560]{2,1,0:T(8,128)(2,1)S(1)} collective-permute-done((bf16[4,144,560]{2,1,0:T(8,128)(2,1)S(1)}, bf16[4,144,560]{2,1,0:T(8,128)(2,1)S(1)}, u32[]{:S(2)}, u32[]{:S(2)}) %collective-permute-start) | collective-permute-done | bytes 645152 | tf_op jit(solution)/shard_map/ppermute | solution.py:37
  69.1 5.9 %shard_map.126 = (bf16[2304,128]{1,0:T(8,128)(2,1)}, bf16[2304,128]{1,0:T(8,128)(2,1)}, bf16[2304,128]{1,0:T(8,128)(2,1)}, bf16[2304,128]{1,0:T(8,128)(2,1)}) custom-call(s32[3]{0:T(128)} %pad_add_fusion.place_ref, bf16[560,512]{1,0:T(8,128)(2,1)} %shard_map.125.mixed_ref, bf16[8,144,560]{2,1,0:T(8,128)(2,1)} %all-gather.4.cloned.1.call-done.own_ref, ...), custom_call_target="tpu_custom_call" | custom-call | flops 2000000000 | bytes 5000000 | tf_op jit(solution)/shard_map/pallas_call | solution.py:221
  75.0 3.2 %collective-permute-start.2 = (bf16[2304,128]{1,0:T(8,128)(2,1)}, bf16[2304,128]{1,0:T(8,128)(2,1)S(1)}, u32[]{:S(2)}, u32[]{:S(2)}) collective-permute-start(bf16[2304,128]{1,0:T(8,128)(2,1)} %get-tuple-element.23), channel_id=1, source_target_pairs={{0,2},{1,3},{2,0},{3,1},{4,6},{5,7},{6,4},{7,5},{8,10},{9,11},{10,... | collective-permute-start | bytes 1769480 | tf_op jit(solution)/shard_map/ppermute | solution.py:37
  78.1 2.7 %collective-permute-start.4 = (bf16[2304,128]{1,0:T(8,128)(2,1)}, bf16[2304,128]{1,0:T(8,128)(2,1)S(1)}, u32[]{:S(2)}, u32[]{:S(2)}) collective-permute-start(bf16[2304,128]{1,0:T(8,128)(2,1)} %get-tuple-element.25), channel_id=1, source_target_pairs={{0,3},{1,0},{2,1},{3,2},{4,7},{5,4},{6,5},{7,6},{8,11},{9,8},{10,9... | collective-permute-start | bytes 1769480 | tf_op jit(solution)/shard_map/ppermute | solution.py:37
  81.6 3.1 %convolution_reduce_fusion = f32[8960]{0:T(1024)S(1)} fusion(bf16[256,1]{0,1:T(2,128)(2,1)S(1)} %reshape.105, bf16[256,8960]{1,0:T(8,128)(2,1)} %param.18), kind=kOutput, calls=%fused_computation | convolution fusion | flops 4587520 | bytes 4623872 | tf_op jit(solution)/shard_map/dot_general | solution.py:74
  86.4 1.1 pad.21.vector_ref
  87.5 16.1 %collective-permute-done.3 = bf16[2304,128]{1,0:T(8,128)(2,1)S(1)} collective-permute-done((bf16[2304,128]{1,0:T(8,128)(2,1)}, bf16[2304,128]{1,0:T(8,128)(2,1)S(1)}, u32[]{:S(2)}, u32[]{:S(2)}) %collective-permute-start.3) | collective-permute-done | bytes 589856 | tf_op jit(solution)/shard_map/ppermute | solution.py:37
  103.6 4.0 %shard_map.127 = (f32[32,72,128]{2,1,0:T(8,128)}, bf16[128,2304]{1,0:T(8,128)(2,1)}) custom-call(s32[3]{0:T(128)} %pad_add_fusion.place_ref, bf16[32,72,128]{2,1,0:T(8,128)(2,1)S(1)} %bitcast.39, bf16[32,72,128]{2,1,0:T(8,128)(2,1)S(1)} %bitcast.40, bf16[32,72,128]{2,1,0:T(8,128)(2,1)S(1)} %bitcast.41, bf16[32,72,128]{2,1,0:T(8,128)(2,1)} %bitcast.50, ...), custom_call_target="tpu_custom_call" | custom-call | flops 10000000 | bytes 8000000 | tf_op jit(solution)/shard_map/pallas_call | solution.py:269
  107.6 1.2 collective-permute-start.6
  108.8 1.5 collective-permute-start.5
  110.3 12.0 %collective-permute-done.6.refs_1_ = bf16[128,2304]{1,0:T(8,128)(2,1)S(1)} collective-permute-done((bf16[128,2304]{1,0:T(8,128)(2,1)}, bf16[128,2304]{1,0:T(8,128)(2,1)S(1)}, u32[]{:S(2)}, u32[]{:S(2)}) %collective-permute-start.6) | collective-permute-done | bytes 589856 | tf_op jit(solution)/shard_map/ppermute | solution.py:37
  122.3 2.6 %collective-permute-start.8 = (bf16[8,2,2,72,1120]{4,3,2,1,0:T(8,128)(2,1)}, bf16[8,2,2,72,1120]{4,3,2,1,0:T(8,128)(2,1)}, u32[]{:S(2)}, u32[]{:S(2)}) collective-permute-start(bf16[8,2,2,72,1120]{4,3,2,1,0:T(8,128)(2,1)} %bitcast.45), channel_id=1, source_target_pairs={{0,64},{64,0},{1,65},{65,1},{2,66},{66,2},{3,67},{67,3},{4,68},{68... | collective-permute-start | bytes 15482888 | tf_op jit(solution)/shard_map/ppermute | solution.py:37
  124.9 1.7 collective-permute-start.11
  126.6 7.0 %collective-permute-done.8.refs_3_ = bf16[8,2,2,72,1120]{4,3,2,1,0:T(8,128)(2,1)} collective-permute-done((bf16[8,2,2,72,1120]{4,3,2,1,0:T(8,128)(2,1)}, bf16[8,2,2,72,1120]{4,3,2,1,0:T(8,128)(2,1)}, u32[]{:S(2)}, u32[]{:S(2)}) %collective-permute-start.8) | collective-permute-done | bytes 5160992 | tf_op jit(solution)/shard_map/ppermute | solution.py:37
  133.6 8.8 %shard_map.128 = (bf16[2304,128]{1,0:T(8,128)(2,1)}, bf16[2304,128]{1,0:T(8,128)(2,1)}) custom-call(bf16[128,2304]{1,0:T(8,128)(2,1)} %copy-done.1, bf16[128,2304]{1,0:T(8,128)(2,1)} %copy-done, bf16[8,2,2,72,1120]{4,3,2,1,0:T(8,128)(2,1)} %bitcast.46, bf16[8,2,2,72,1120]{4,3,2,1,0:T(8,128)(2,1)} %collective-permute-done.8.refs_3_), custom_call_target="tpu_custom_call" | custom-call | flops 2642411520 | bytes 10321920 | tf_op jit(solution)/shard_map/pallas_call | solution.py:356
  143.2 8.7 %shard_map.129 = (bf16[2304,128]{1,0:T(8,128)(2,1)}, bf16[2304,128]{1,0:T(8,128)(2,1)}) custom-call(bf16[128,2304]{1,0:T(8,128)(2,1)} %get-tuple-element.34.refs_0_, bf16[128,2304]{1,0:T(8,128)(2,1)} %copy-done.2, bf16[8,2,2,72,1120]{4,3,2,1,0:T(8,128)(2,1)} %bitcast.47, bf16[8,2,2,72,1120]{4,3,2,1,0:T(8,128)(2,1)} %collective-permute-done.8.refs_3_), custom_call_target="tpu_custom_call" | custom-call | flops 2642411520 | bytes 10321920 | tf_op jit(solution)/shard_map/pallas_call | solution.py:356
  152.0 1.7 collective-permute-start.12
  155.2 13.0 %collective-permute-done.12 = bf16[2304,128]{1,0:T(8,128)(2,1)S(1)} collective-permute-done((bf16[2304,128]{1,0:T(8,128)(2,1)}, bf16[2304,128]{1,0:T(8,128)(2,1)S(1)}, u32[]{:S(2)}, u32[]{:S(2)}) %collective-permute-start.12) | collective-permute-done | bytes 589856 | tf_op jit(solution)/shard_map/ppermute | solution.py:37
  168.2 12.8 %collective-permute-done.10 = bf16[2304,128]{1,0:T(8,128)(2,1)S(1)} collective-permute-done((bf16[2304,128]{1,0:T(8,128)(2,1)S(1)}, bf16[2304,128]{1,0:T(8,128)(2,1)S(1)}, u32[]{:S(2)}, u32[]{:S(2)}) %collective-permute-start.10) | collective-permute-done | bytes 589856 | tf_op jit(solution)/shard_map/ppermute | solution.py:37
  181.6 3.7 %shard_map.130 = (bf16[2240,128]{1,0:T(8,128)(2,1)}, bf16[2240,128]{1,0:T(8,128)(2,1)}) custom-call(s32[3]{0:T(128)} %pad_add_fusion.place_ref, f32[1]{0:T(128)S(6)} %sub.13.step_ref, bf16[32,72,128]{2,1,0:T(8,128)(2,1)S(1)} %bitcast.44, bf16[32,72,128]{2,1,0:T(8,128)(2,1)S(1)} %bitcast.43, bf16[32,72,128]{2,1,0:T(8,128)(2,1)S(1)} %bitcast.42, ...), custom_call_target="tpu_custom_call" | custom-call | flops 10000000 | bytes 8000000 | tf_op jit(solution)/shard_map/pallas_call | solution.py:301
  (47 shorter events, 8.1 us)
Async XLA Ops:
  7.2 14.6 %copy-start.4 = (bf16[140,1120]{1,0:T(8,128)(2,1)S(1)}, bf16[140,1120]{1,0:T(8,128)(2,1)}, u32[]{:S(2)}) copy-start(bf16[140,1120]{1,0:T(8,128)(2,1)} %param.20) | copy-start | bytes 940804
  7.2 14.7 %copy-start.5 = (bf16[1120,140]{0,1:T(8,128)(2,1)S(1)}, bf16[1120,140]{0,1:T(8,128)(2,1)}, u32[]{:S(2)}) copy-start(bf16[1120,140]{0,1:T(8,128)(2,1)} %param.21) | copy-start | bytes 940804
  7.2 43.4 %all-gather.4.cloned.1.call-start = ((), (), s32[]{:S(2)}) async-start(), calls=%async_computation.2 | async-start | bytes 1658880 | tf_op jit(solution)/shard_map/all_gather | solution.py:382
  11.6 17.5 %all-to-all-start = ((bf16[16,40,128]{2,1,0:T(8,128)(2,1)}), bf16[16,40,128]{2,1,0:T(8,128)(2,1)S(1)}, u32[]{:S(2)}, u32[]{:S(2)}) async-start(bf16[16,40,128]{2,1,0:T(8,128)(2,1)} %bitcast.58), calls=%async_computation | async-start | bytes 327680 | tf_op jit(solution)/shard_map/all_to_all | solution.py:389
  21.7 100.6 %all-gather.6.cloned.1.call-start = ((), (), s32[]{:S(2)}) async-start(), calls=%async_computation.3 | async-start | bytes 5971968 | tf_op jit(solution)/shard_map/all_gather | solution.py:396
  29.1 15.8 %collective-permute-start.7 = (bf16[2,72,1120]{2,1,0:T(8,128)(2,1)S(1)}, bf16[2,72,1120]{2,1,0:T(8,128)(2,1)S(1)}, u32[]{:S(2)}, u32[]{:S(2)}) collective-permute-start(bf16[2,72,1120]{2,1,0:T(8,128)(2,1)S(1)} %fusion.2), channel_id=1, source_target_pairs={{0,32},{32,128},{128,160},{160,0},{1,33},{33,129},{129,161},{161,1... | collective-permute-start | bytes 967688 | tf_op jit(solution)/shard_map/ppermute | solution.py:37
  52.0 13.9 %collective-permute-start.1 = (bf16[4,144,560]{2,1,0:T(8,128)(2,1)S(1)}, bf16[4,144,560]{2,1,0:T(8,128)(2,1)S(1)}, u32[]{:S(2)}, u32[]{:S(2)}) collective-permute-start(bf16[4,144,560]{2,1,0:T(8,128)(2,1)S(1)} %get-tuple-element.40), channel_id=1, source_target_pairs={{0,160},{32,0},{128,32},{160,128},{1,161},{33,1},{129,33},{161,129... | collective-permute-start | bytes 1935368 | tf_op jit(solution)/shard_map/ppermute | solution.py:37
  54.9 14.2 %collective-permute-start = (bf16[4,144,560]{2,1,0:T(8,128)(2,1)S(1)}, bf16[4,144,560]{2,1,0:T(8,128)(2,1)S(1)}, u32[]{:S(2)}, u32[]{:S(2)}) collective-permute-start(bf16[4,144,560]{2,1,0:T(8,128)(2,1)S(1)} %get-tuple-element.41), channel_id=1, source_target_pairs={{0,32},{32,128},{128,160},{160,0},{1,33},{33,129},{129,161},{161,1... | collective-permute-start | bytes 1935368 | tf_op jit(solution)/shard_map/ppermute | solution.py:37
  75.0 9.9 %copy-start.3 = (bf16[128,2240]{0,1:T(8,128)(2,1)S(1)}, bf16[128,2240]{0,1:T(8,128)(2,1)}, u32[]{:S(2)}) copy-start(bf16[128,2240]{0,1:T(8,128)(2,1)} %param.11) | copy-start | bytes 1720324
  75.0 12.6 %collective-permute-start.2 = (bf16[2304,128]{1,0:T(8,128)(2,1)}, bf16[2304,128]{1,0:T(8,128)(2,1)S(1)}, u32[]{:S(2)}, u32[]{:S(2)}) collective-permute-start(bf16[2304,128]{1,0:T(8,128)(2,1)} %get-tuple-element.23), channel_id=1, source_target_pairs={{0,2},{1,3},{2,0},{3,1},{4,6},{5,7},{6,4},{7,5},{8,10},{9,11},{10,... | collective-permute-start | bytes 1769480 | tf_op jit(solution)/shard_map/ppermute | solution.py:37
  78.1 25.5 %collective-permute-start.3 = (bf16[2304,128]{1,0:T(8,128)(2,1)}, bf16[2304,128]{1,0:T(8,128)(2,1)S(1)}, u32[]{:S(2)}, u32[]{:S(2)}) collective-permute-start(bf16[2304,128]{1,0:T(8,128)(2,1)} %get-tuple-element.24), channel_id=1, source_target_pairs={{0,1},{1,2},{2,3},{3,0},{4,5},{5,6},{6,7},{7,4},{8,9},{9,10},{10,1... | collective-permute-start | bytes 1769480 | tf_op jit(solution)/shard_map/ppermute | solution.py:37
  78.1 25.5 %collective-permute-start.4 = (bf16[2304,128]{1,0:T(8,128)(2,1)}, bf16[2304,128]{1,0:T(8,128)(2,1)S(1)}, u32[]{:S(2)}, u32[]{:S(2)}) collective-permute-start(bf16[2304,128]{1,0:T(8,128)(2,1)} %get-tuple-element.25), channel_id=1, source_target_pairs={{0,3},{1,0},{2,1},{3,2},{4,7},{5,4},{6,5},{7,6},{8,11},{9,8},{10,9... | collective-permute-start | bytes 1769480 | tf_op jit(solution)/shard_map/ppermute | solution.py:37
  107.6 14.6 %collective-permute-start.6 = (bf16[128,2304]{1,0:T(8,128)(2,1)}, bf16[128,2304]{1,0:T(8,128)(2,1)S(1)}, u32[]{:S(2)}, u32[]{:S(2)}) collective-permute-start(bf16[128,2304]{1,0:T(8,128)(2,1)} %get-tuple-element.34.refs_0_), channel_id=1, source_target_pairs={{0,1},{1,2},{2,3},{3,0},{4,5},{5,6},{6,7},{7,4},{8,9},{9,10},{10,1... | collective-permute-start | bytes 1769480 | tf_op jit(solution)/shard_map/ppermute | solution.py:37
  108.8 13.4 %collective-permute-start.5 = (bf16[128,2304]{1,0:T(8,128)(2,1)}, bf16[128,2304]{1,0:T(8,128)(2,1)S(1)}, u32[]{:S(2)}, u32[]{:S(2)}) collective-permute-start(bf16[128,2304]{1,0:T(8,128)(2,1)} %get-tuple-element.34.refs_0_), channel_id=1, source_target_pairs={{0,3},{1,0},{2,1},{3,2},{4,7},{5,4},{6,5},{7,6},{8,11},{9,8},{10,9... | collective-permute-start | bytes 1769480 | tf_op jit(solution)/shard_map/ppermute | solution.py:37
  122.3 11.4 %copy-start = (bf16[128,2304]{1,0:T(8,128)(2,1)}, bf16[128,2304]{1,0:T(8,128)(2,1)S(1)}, u32[]{:S(2)}) copy-start(bf16[128,2304]{1,0:T(8,128)(2,1)S(1)} %collective-permute-done.6.refs_1_) | copy-start | bytes 1769476
  122.3 11.4 %copy-start.1 = (bf16[128,2304]{1,0:T(8,128)(2,1)}, bf16[128,2304]{1,0:T(8,128)(2,1)S(1)}, u32[]{:S(2)}) copy-start(bf16[128,2304]{1,0:T(8,128)(2,1)S(1)} %collective-permute-done.5.refs_0_) | copy-start | bytes 1769476
  122.3 11.3 %collective-permute-start.8 = (bf16[8,2,2,72,1120]{4,3,2,1,0:T(8,128)(2,1)}, bf16[8,2,2,72,1120]{4,3,2,1,0:T(8,128)(2,1)}, u32[]{:S(2)}, u32[]{:S(2)}) collective-permute-start(bf16[8,2,2,72,1120]{4,3,2,1,0:T(8,128)(2,1)} %bitcast.45), channel_id=1, source_target_pairs={{0,64},{64,0},{1,65},{65,1},{2,66},{66,2},{3,67},{67,3},{4,68},{68... | collective-permute-start | bytes 15482888 | tf_op jit(solution)/shard_map/ppermute | solution.py:37
  124.9 17.5 %collective-permute-start.11 = (bf16[128,2304]{1,0:T(8,128)(2,1)}, bf16[128,2304]{1,0:T(8,128)(2,1)S(1)}, u32[]{:S(2)}, u32[]{:S(2)}) collective-permute-start(bf16[128,2304]{1,0:T(8,128)(2,1)} %get-tuple-element.34.refs_0_), channel_id=1, source_target_pairs={{0,2},{1,3},{2,0},{3,1},{4,6},{5,7},{6,4},{7,5},{8,10},{9,11},{10,... | collective-permute-start | bytes 1769480 | tf_op jit(solution)/shard_map/ppermute | solution.py:37
  142.4 11.3 %copy-start.7 = (bf16[2304,128]{1,0:T(8,128)(2,1)S(1)}, bf16[2304,128]{1,0:T(8,128)(2,1)}, u32[]{:S(2)}) copy-start(bf16[2304,128]{1,0:T(8,128)(2,1)} %get-tuple-element.33) | copy-start | bytes 1769476
  142.4 12.2 %copy-start.6 = (bf16[2304,128]{1,0:T(8,128)(2,1)S(1)}, bf16[2304,128]{1,0:T(8,128)(2,1)}, u32[]{:S(2)}) copy-start(bf16[2304,128]{1,0:T(8,128)(2,1)} %get-tuple-element.32) | copy-start | bytes 1769476
  142.4 0.8 copy-start.2
  152.0 16.3 %collective-permute-start.12 = (bf16[2304,128]{1,0:T(8,128)(2,1)}, bf16[2304,128]{1,0:T(8,128)(2,1)S(1)}, u32[]{:S(2)}, u32[]{:S(2)}) collective-permute-start(bf16[2304,128]{1,0:T(8,128)(2,1)} %get-tuple-element.35), channel_id=1, source_target_pairs={{0,2},{1,3},{2,0},{3,1},{4,6},{5,7},{6,4},{7,5},{8,10},{9,11},{10,... | collective-permute-start | bytes 1769480 | tf_op jit(solution)/shard_map/ppermute | solution.py:37
  153.7 27.3 %collective-permute-start.10 = (bf16[2304,128]{1,0:T(8,128)(2,1)S(1)}, bf16[2304,128]{1,0:T(8,128)(2,1)S(1)}, u32[]{:S(2)}, u32[]{:S(2)}) collective-permute-start(bf16[2304,128]{1,0:T(8,128)(2,1)S(1)} %copy-done.7), channel_id=1, source_target_pairs={{0,3},{1,0},{2,1},{3,2},{4,7},{5,4},{6,5},{7,6},{8,11},{9,8},{10,9... | collective-permute-start | bytes 1769480 | tf_op jit(solution)/shard_map/ppermute | solution.py:37
  154.6 27.0 %collective-permute-start.9 = (bf16[2304,128]{1,0:T(8,128)(2,1)S(1)}, bf16[2304,128]{1,0:T(8,128)(2,1)S(1)}, u32[]{:S(2)}, u32[]{:S(2)}) collective-permute-start(bf16[2304,128]{1,0:T(8,128)(2,1)S(1)} %copy-done.6), channel_id=1, source_target_pairs={{0,1},{1,2},{2,3},{3,0},{4,5},{5,6},{6,7},{7,4},{8,9},{9,10},{10,1... | collective-permute-start | bytes 1769480 | tf_op jit(solution)/shard_map/ppermute | solution.py:37
Sparse Core Ops, SparseCore 0:
  10.4 40.1 all-gather.3
  52.4 68.0 all-gather.5

commit v2 on v1

--- a/solution.py
+++ b/solution.py
@@ -311,11 +311,11 @@
 HALF = ROWS // 2
 
 
-def units_kernel(chunks, *refs):
-    token_refs = refs[:chunks]
-    own_ref, other_ref = refs[chunks : chunks + 2]
-    out_refs = refs[chunks + 2 : 2 * chunks + 2]
-    tokens, sums, units = refs[2 * chunks + 2 :]
+def units_kernel(pieces, *refs):
+    token_refs = refs[:pieces]
+    own_ref, other_ref = refs[pieces : pieces + 2]
+    out_refs = refs[pieces + 2 : -3]
+    tokens, sums, units = refs[-3:]
     step = pl.program_id(0)
 
     def up(ref, first):
@@ -327,13 +327,15 @@
         feed = lax.dot_general(
             weight, units[...], (((1,), (1,)), ((), ())), preferred_element_type=F32
         ).astype(BF)
-        for n in range(chunks):
-            out_refs[n][...] = feed[:, SHARE * n : SHARE * (n + 1)]
+        for n, out_ref in enumerate(out_refs):
+            out_ref[...] = feed[:, SHARE * n : SHARE * (n + 1)]
 
     @pl.when(step == 0)
     def _():
-        for n in range(chunks):
-            tokens[SHARE * n : SHARE * (n + 1), :] = token_refs[n][...]
+        row = 0
+        for token_ref in token_refs:
+            tokens[row : row + token_ref.shape[0], :] = token_ref[...]
+            row += token_ref.shape[0]
         sums[...] = up(own_ref, 0)
 
     @pl.when(step == 1)
@@ -350,14 +352,14 @@
 
 
 def unit_terms(tokens, own, other):
-    chunks = len(tokens)
+    chunks = sum(t.shape[0] for t in tokens) // SHARE
     hidden_units = own.shape[4]
     block = (8, 2, 1, PADDED, hidden_units)
     return pl.pallas_call(
-        functools.partial(units_kernel, chunks),
+        functools.partial(units_kernel, len(tokens)),
         grid=(4,),
         out_shape=[jax.ShapeDtypeStruct((ROWS, SHARE), BF)] * chunks,
-        in_specs=[pl.BlockSpec((SHARE, ROWS), lambda i: (0, 0))] * chunks
+        in_specs=[pl.BlockSpec(t.shape, lambda i: (0, 0)) for t in tokens]
         + [
             pl.BlockSpec(block, lambda i: (0, 0, jnp.where(i >= 2, 1, 0), 0, 0)),
             pl.BlockSpec(block, lambda i: (0, 0, jnp.where(i >= 3, 1, 0), 0, 0)),
@@ -378,12 +380,13 @@
     y, c, xl = lax.axis_index("y"), lax.axis_index("c"), lax.axis_index("xl")
     place = jnp.stack([c, xl, y]).astype(jnp.int32)
 
+    def core_half(both):
+        return jnp.where(c == 0, both[..., 0, :, :], both[..., 1, :, :])
+
     out_mine = padded_pieces(w_out.T).reshape(2 * PADDED, -1)
     out_own = lax.all_gather(out_mine, "z", axis=0)
-    out_first, out_second = along_x(out_own[:4], 1), along_x(out_own[4:], -1)
-    both = jnp.stack([padded_pieces(w_up), padded_pieces(w_down.T)])
-    mine = jnp.where(c == 0, both[:, 0], both[:, 1])
-
+    out_weights = [out_own, along_x(out_own[:4], 1), along_x(out_own[4:], -1)]
+    mine = core_half(jnp.stack([padded_pieces(w_up), padded_pieces(w_down.T)]))
     queries, keys, values = queries.T, keys.T, values.T
     cumulative, packed = own_state(keys, values, log_decay)
     slices = lax.all_to_all(packed.reshape(16, -1, SHARE), ("xl", "z"), 0, 0)
@@ -392,12 +395,11 @@
     ahead = scan_blocks(slices)
     before = lax.all_to_all(ahead, ("xl", "z"), 0, 0).reshape(STATE_ROWS, SHARE)
     mine, mine_x, _ = lax.optimization_barrier((mine, mine_x, before))
-    pair = jnp.stack([mine, mine_x])
-    half = lax.all_gather(pair, "z", axis=0)
+    half = lax.all_gather(jnp.stack([mine, mine_x]), "z", axis=0)
     inner = inner_part(queries, keys, values, cumulative, block_ids[None, :])
     mixed = mix(queries, inner, cumulative, before)
 
-    parts = head_terms(place, mixed, [out_own, out_first, out_second])
+    parts = head_terms(place, mixed, out_weights)
     terms = [along_y(parts[i], d) for i, d in enumerate(FARTHEST_FIRST[:3])] + [parts[3]]
 
     shifts, step_size = modulation_of(t_index, w_mod)
@@ -405,16 +407,16 @@
     latent_pieces = padded_pieces(latents.T)
     hidden, normed = norm(place, terms, latent_pieces, vectors)
 
-    theirs = {d: along_y(normed, -d) for d in (1, 3)}
-    theirs[2] = along_y(normed, -2)
-    half, _ = lax.optimization_barrier((half, (theirs[1], theirs[3])))
+    above, below = along_y(normed, -1), along_y(normed, 1)
+    far = [along_y(above[: SHARE // 2], -1), along_y(below[SHARE // 2 :], 1)]
+    half, _ = lax.optimization_barrier((half, normed))
     other = other_core(half)
-    near = unit_terms([theirs[1], theirs[3]], half, other)
+    near = unit_terms([above, below], half, other)
     feeds = []
     for d, part in zip((1, 3), near):
         feeds.append(along_y(part, d))
     normed, _ = lax.optimization_barrier((normed, near[0]))
-    rest = unit_terms([normed, theirs[2]], half, other)
+    rest = unit_terms([normed] + far, half, other)
     feeds += [along_y(rest[1], 2), rest[0]]
     step = step_size[None] if step_size.ndim == 0 else step_size
     velocity, advanced = last(place, step, feeds, hidden, latent_pieces, vectors)

time: 193 us -> 200 us (1.036)
  waiting for transfers between devices: 79.1 us -> 88.1 us
    all_gather x1, waiting for transfers between devices: 0.02 us -> 12.8 us  [block(): half = lax.all_gather(jnp.stack([mine, mine_x]), 'z', axis=0)]
    ppermute x13 -> x14, waiting for transfers between devices: 67.4 us -> 63.5 us  [permute(): return lax.ppermute(block, tuple(axes) if len(axes) > 1 else axes[0], pairs)]
    ppermute x13 -> x14, starting transfers between devices: 19.6 us -> 17.7 us  [permute(): return lax.ppermute(block, tuple(axes) if len(axes) > 1 else axes[0], pairs)]
  transfers between devices with their start and end apart: 16 -> 17, of which waited for: 10 -> 10; matrix products, arithmetic and copies ran while one was open for 5% -> 5% of each run, Pallas kernels for 16% -> 15%
where the time goes in v2:
time: 200 us
  waiting for transfers between devices  88.1 us (44%)
  Pallas kernels  42.9 us (21%)
  starting transfers between devices  27.8 us (14%)
  between operations  15 us (8%)
  blocking collectives  13.5 us (7%)
  local copies, waits for them, and re-layouts  7.75 us (4%)
  matrix products  3.07 us (2%)
    ppermute x14, waiting for transfers between devices, permute(): return lax.ppermute(block, tuple(axes) if len(axes) > 1 else axes[0], pairs)  63.5 us
    ppermute x14, starting transfers between devices, permute(): return lax.ppermute(block, tuple(axes) if len(axes) > 1 else axes[0], pairs)  17.7 us
    pallas_call x2, Pallas kernels, unit_terms(): pl.pallas_call(functools.partial(units_kernel, len(tokens)), grid=(4,), o...  17.5 us
    all_to_all x1, blocking collectives, block(): before = lax.all_to_all(ahead, ('xl', 'z'), 0, 0).reshape(STATE_ROWS, SHARE)  13.5 us
    all_gather x1, waiting for transfers between devices, block(): half = lax.all_gather(jnp.stack([mine, mine_x]), 'z', axis=0)  12.8 us
    all_to_all x1, starting transfers between devices, block(): slices = lax.all_to_all(packed.reshape(16, -1, SHARE), ('xl', 'z'), 0, 0)  10 us
    all_to_all x1, waiting for transfers between devices, block(): slices = lax.all_to_all(packed.reshape(16, -1, SHARE), ('xl', 'z'), 0, 0)  7.04 us
    pallas_call x1, Pallas kernels, head_terms(): pl.pallas_call(head_kernel, out_shape=[jax.ShapeDtypeStruct((ROWS, SHARE)...  5.88 us
  transfers between devices with their start and end apart: 17, of which 10 were waited for; matrix products, arithmetic and copies ran while one was open for 5% of the time, Pallas kernels for 15%

profile of v2, /device:TPU:1, one launch (start us, length us, event | category | flops | bytes accessed | tf_op | source)
XLA Modules:
  0.0 199.8 jit_solution(12400589655982275970)
XLA Ops:
  7.2 1.0 reshape.80
  9.0 2.7 %shard_map.122 = (f32[5,512]{1,0:T(8,128)}, bf16[640,128]{1,0:T(8,128)(2,1)}) custom-call(bf16[560,512]{1,0:T(8,128)(2,1)} %bitcast.60, bf16[560,512]{1,0:T(8,128)(2,1)} %bitcast.62, f32[5,512]{1,0:T(8,128)} %decay_ref.1), custom_call_target="tpu_custom_call" | custom-call | flops 1000000000 | bytes 3000000 | tf_op jit(solution)/shard_map/pallas_call | solution.py:122
  11.6 10.0 %all-to-all-start = ((bf16[16,40,128]{2,1,0:T(8,128)(2,1)}), bf16[16,40,128]{2,1,0:T(8,128)(2,1)S(1)}, u32[]{:S(2)}, u32[]{:S(2)}) async-start(bf16[16,40,128]{2,1,0:T(8,128)(2,1)} %bitcast.58), calls=%async_computation | async-start | bytes 327680 | tf_op jit(solution)/shard_map/all_to_all | solution.py:392
  22.1 7.0 %all-to-all-done.blocks_ref = bf16[16,40,128]{2,1,0:T(8,128)(2,1)S(1)} async-done(((bf16[16,40,128]{2,1,0:T(8,128)(2,1)}), bf16[16,40,128]{2,1,0:T(8,128)(2,1)S(1)}, u32[]{:S(2)}, u32[]{:S(2)}) %all-to-all-start) | async-done | bytes 163872 | tf_op jit(solution)/shard_map/all_to_all | solution.py:392
  29.9 1.6 shard_map.124
  31.5 13.5 %all_to_all.10 = bf16[16,40,128]{2,1,0:T(8,128)(2,1)S(1)} all-to-all(bf16[16,40,128]{2,1,0:T(8,128)(2,1)} %shard_map.124), channel_id=1, replica_groups=mesh['xh'=2,'c'=2,'xl'=2,'z'=8,'y'=4] {'xl','z'}, dimensions={0} | all-to-all | bytes 327680 | tf_op jit(solution)/shard_map/all_to_all | solution.py:396
  45.9 4.6 %all-gather.4.cloned.1.call-done.own_ref = bf16[8,144,560]{2,1,0:T(8,128)(2,1)} async-done(((bf16[1,144,560]{2,1,0:T(8,128)(2,1)}), bf16[8,144,560]{2,1,0:T(8,128)(2,1)}) %all-gather.4.cloned.1.call-update) | async-done | bytes 1290256 | tf_op jit(solution)/shard_map/all_gather | solution.py:387
  50.6 1.5 fusion.6
  52.0 2.8 %collective-permute-start.1 = (bf16[4,144,560]{2,1,0:T(8,128)(2,1)S(1)}, bf16[4,144,560]{2,1,0:T(8,128)(2,1)S(1)}, u32[]{:S(2)}, u32[]{:S(2)}) collective-permute-start(bf16[4,144,560]{2,1,0:T(8,128)(2,1)S(1)} %get-tuple-element.40), channel_id=1, source_target_pairs={{0,160},{32,0},{128,32},{160,128},{1,161},{33,1},{129,33},{161,129... | collective-permute-start | bytes 1935368 | tf_op jit(solution)/shard_map/ppermute | solution.py:37
  55.5 4.9 %shard_map.123.inner_ref = f32[560,512]{1,0:T(8,128)} custom-call(bf16[560,512]{1,0:T(8,128)(2,1)} %bitcast.52, bf16[560,512]{1,0:T(8,128)(2,1)} %bitcast.61, bf16[560,512]{1,0:T(8,128)(2,1)} %bitcast.63, f32[5,512]{1,0:T(8,128)} %get-tuple-element.21.cumulative_ref, s32[1,512]{1,0:T(1,128)} %bitcast.66), custom_call_target="tpu_custom_call" | custom-call | flops 5000000000 | bytes 4000000 | tf_op jit(solution)/shard_map/pallas_call | solution.py:171
  60.4 2.6 %shard_map.125.mixed_ref = bf16[560,512]{1,0:T(8,128)(2,1)} custom-call(bf16[560,512]{1,0:T(8,128)(2,1)} %bitcast.53, f32[560,512]{1,0:T(8,128)} %shard_map.123.inner_ref, f32[5,512]{1,0:T(8,128)} %get-tuple-element.21.cumulative_ref, bf16[640,128]{1,0:T(8,128)(2,1)S(1)} %bitcast.38), custom_call_target="tpu_custom_call" | custom-call | flops 100000000 | bytes 4000000 | tf_op jit(solution)/shard_map/pallas_call | solution.py:194
  63.0 2.9 %collective-permute-done.1.second_ref = bf16[4,144,560]{2,1,0:T(8,128)(2,1)S(1)} collective-permute-done((bf16[4,144,560]{2,1,0:T(8,128)(2,1)S(1)}, bf16[4,144,560]{2,1,0:T(8,128)(2,1)S(1)}, u32[]{:S(2)}, u32[]{:S(2)}) %collective-permute-start.1) | collective-permute-done | bytes 645152 | tf_op jit(solution)/shard_map/ppermute | solution.py:37
  66.0 3.1 %collective-permute-done.first_ref = bf16[4,144,560]{2,1,0:T(8,128)(2,1)S(1)} collective-permute-done((bf16[4,144,560]{2,1,0:T(8,128)(2,1)S(1)}, bf16[4,144,560]{2,1,0:T(8,128)(2,1)S(1)}, u32[]{:S(2)}, u32[]{:S(2)}) %collective-permute-start) | collective-permute-done | bytes 645152 | tf_op jit(solution)/shard_map/ppermute | solution.py:37
  69.1 5.9 %shard_map.126 = (bf16[2304,128]{1,0:T(8,128)(2,1)}, bf16[2304,128]{1,0:T(8,128)(2,1)}, bf16[2304,128]{1,0:T(8,128)(2,1)}, bf16[2304,128]{1,0:T(8,128)(2,1)}) custom-call(s32[3]{0:T(128)} %pad_add_fusion.place_ref, bf16[560,512]{1,0:T(8,128)(2,1)} %shard_map.125.mixed_ref, bf16[8,144,560]{2,1,0:T(8,128)(2,1)} %all-gather.4.cloned.1.call-done.own_ref, ...), custom_call_target="tpu_custom_call" | custom-call | flops 2000000000 | bytes 5000000 | tf_op jit(solution)/shard_map/pallas_call | solution.py:221
  75.0 3.2 %collective-permute-start.2 = (bf16[2304,128]{1,0:T(8,128)(2,1)}, bf16[2304,128]{1,0:T(8,128)(2,1)S(1)}, u32[]{:S(2)}, u32[]{:S(2)}) collective-permute-start(bf16[2304,128]{1,0:T(8,128)(2,1)} %get-tuple-element.23), channel_id=1, source_target_pairs={{0,2},{1,3},{2,0},{3,1},{4,6},{5,7},{6,4},{7,5},{8,10},{9,11},{10,... | collective-permute-start | bytes 1769480 | tf_op jit(solution)/shard_map/ppermute | solution.py:37
  78.1 2.7 %collective-permute-start.4 = (bf16[2304,128]{1,0:T(8,128)(2,1)}, bf16[2304,128]{1,0:T(8,128)(2,1)S(1)}, u32[]{:S(2)}, u32[]{:S(2)}) collective-permute-start(bf16[2304,128]{1,0:T(8,128)(2,1)} %get-tuple-element.25), channel_id=1, source_target_pairs={{0,3},{1,0},{2,1},{3,2},{4,7},{5,4},{6,5},{7,6},{8,11},{9,8},{10,9... | collective-permute-start | bytes 1769480 | tf_op jit(solution)/shard_map/ppermute | solution.py:37
  81.6 3.1 %convolution_reduce_fusion = f32[8960]{0:T(1024)S(1)} fusion(bf16[256,1]{0,1:T(2,128)(2,1)S(1)} %reshape.105, bf16[256,8960]{1,0:T(8,128)(2,1)} %param.18), kind=kOutput, calls=%fused_computation | convolution fusion | flops 4587520 | bytes 4623872 | tf_op jit(solution)/shard_map/dot_general | solution.py:74
  86.4 1.1 pad.21.vector_ref
  87.5 16.1 %collective-permute-done.3 = bf16[2304,128]{1,0:T(8,128)(2,1)S(1)} collective-permute-done((bf16[2304,128]{1,0:T(8,128)(2,1)}, bf16[2304,128]{1,0:T(8,128)(2,1)S(1)}, u32[]{:S(2)}, u32[]{:S(2)}) %collective-permute-start.3) | collective-permute-done | bytes 589856 | tf_op jit(solution)/shard_map/ppermute | solution.py:37
  103.6 4.0 %shard_map.127 = (f32[32,72,128]{2,1,0:T(8,128)}, bf16[128,2304]{1,0:T(8,128)(2,1)}) custom-call(s32[3]{0:T(128)} %pad_add_fusion.place_ref, bf16[32,72,128]{2,1,0:T(8,128)(2,1)S(1)} %bitcast.39, bf16[32,72,128]{2,1,0:T(8,128)(2,1)S(1)} %bitcast.40, bf16[32,72,128]{2,1,0:T(8,128)(2,1)S(1)} %bitcast.41, bf16[32,72,128]{2,1,0:T(8,128)(2,1)} %bitcast.50, ...), custom_call_target="tpu_custom_call" | custom-call | flops 10000000 | bytes 8000000 | tf_op jit(solution)/shard_map/pallas_call | solution.py:269
  107.6 12.8 %all-gather.6.cloned.1.call-done = bf16[16,2,72,1120]{3,2,1,0:T(8,128)(2,1)} async-done(((bf16[2,2,72,1120]{3,2,1,0:T(8,128)(2,1)}), bf16[16,2,72,1120]{3,2,1,0:T(8,128)(2,1)}) %all-gather.6.cloned.1.call-update) | async-done | bytes 5160976 | tf_op jit(solution)/shard_map/all_gather | solution.py:398
  121.3 1.2 collective-permute-start.6
  122.5 1.5 collective-permute-start.5
  124.0 13.6 %collective-permute-done.6.refs_1_ = bf16[128,2304]{1,0:T(8,128)(2,1)S(1)} collective-permute-done((bf16[128,2304]{1,0:T(8,128)(2,1)}, bf16[128,2304]{1,0:T(8,128)(2,1)S(1)}, u32[]{:S(2)}, u32[]{:S(2)}) %collective-permute-start.6) | collective-permute-done | bytes 589856 | tf_op jit(solution)/shard_map/ppermute | solution.py:37
  137.8 2.9 %collective-permute-start.11 = (bf16[64,2304]{1,0:T(8,128)(2,1)S(1)}, bf16[64,2304]{1,0:T(8,128)(2,1)S(1)}, u32[]{:S(2)}, u32[]{:S(2)}) collective-permute-start(bf16[64,2304]{1,0:T(8,128)(2,1)S(1)} %slice.28), channel_id=1, source_target_pairs={{0,3},{1,0},{2,1},{3,2},{4,7},{5,4},{6,5},{7,6},{8,11},{9,8},{10,9... | collective-permute-start | bytes 884744 | tf_op jit(solution)/shard_map/ppermute | solution.py:37
  140.7 8.8 %shard_map.128 = (bf16[2304,128]{1,0:T(8,128)(2,1)}, bf16[2304,128]{1,0:T(8,128)(2,1)}) custom-call(bf16[128,2304]{1,0:T(8,128)(2,1)} %copy-done.1, bf16[128,2304]{1,0:T(8,128)(2,1)} %copy-done, bf16[8,2,2,72,1120]{4,3,2,1,0:T(8,128)(2,1)} %bitcast.46, bf16[8,2,2,72,1120]{4,3,2,1,0:T(8,128)(2,1)} %collective-permute-done.8.refs_3_.refs_4_), custom_call_target="tpu_custom_call" | custom-call | flops 2642411520 | bytes 10321920 | tf_op jit(solution)/shard_map/pallas_call | solution.py:358
  150.9 8.7 %shard_map.129 = (bf16[2304,128]{1,0:T(8,128)(2,1)}, bf16[2304,128]{1,0:T(8,128)(2,1)}) custom-call(bf16[128,2304]{1,0:T(8,128)(2,1)} %get-tuple-element.34.refs_0_, bf16[64,2304]{1,0:T(8,128)(2,1)} %copy-done.6, bf16[64,2304]{1,0:T(8,128)(2,1)} %copy-done.5, bf16[8,2,2,72,1120]{4,3,2,1,0:T(8,128)(2,1)} %bitcast.47, ...), custom_call_target="tpu_custom_call" | custom-call | flops 2642411520 | bytes 10321920 | tf_op jit(solution)/shard_map/pallas_call | solution.py:358
  160.0 1.1 collective-permute-start.10
  161.5 13.4 %collective-permute-done.13 = bf16[2304,128]{1,0:T(8,128)(2,1)S(1)} collective-permute-done((bf16[2304,128]{1,0:T(8,128)(2,1)}, bf16[2304,128]{1,0:T(8,128)(2,1)S(1)}, u32[]{:S(2)}, u32[]{:S(2)}) %collective-permute-start.13) | collective-permute-done | bytes 589856 | tf_op jit(solution)/shard_map/ppermute | solution.py:37
  174.9 11.4 %collective-permute-done.10 = bf16[2304,128]{1,0:T(8,128)(2,1)S(1)} collective-permute-done((bf16[2304,128]{1,0:T(8,128)(2,1)S(1)}, bf16[2304,128]{1,0:T(8,128)(2,1)S(1)}, u32[]{:S(2)}, u32[]{:S(2)}) %collective-permute-start.10) | collective-permute-done | bytes 589856 | tf_op jit(solution)/shard_map/ppermute | solution.py:37
  186.3 3.0 %collective-permute-done.9 = bf16[2304,128]{1,0:T(8,128)(2,1)S(1)} collective-permute-done((bf16[2304,128]{1,0:T(8,128)(2,1)S(1)}, bf16[2304,128]{1,0:T(8,128)(2,1)S(1)}, u32[]{:S(2)}, u32[]{:S(2)}) %collective-permute-start.9) | collective-permute-done | bytes 589856 | tf_op jit(solution)/shard_map/ppermute | solution.py:37
  189.2 3.7 %shard_map.130 = (bf16[2240,128]{1,0:T(8,128)(2,1)}, bf16[2240,128]{1,0:T(8,128)(2,1)}) custom-call(s32[3]{0:T(128)} %pad_add_fusion.place_ref, f32[1]{0:T(128)S(6)} %sub.13.step_ref, bf16[32,72,128]{2,1,0:T(8,128)(2,1)S(1)} %bitcast.44, bf16[32,72,128]{2,1,0:T(8,128)(2,1)S(1)} %bitcast.43, bf16[32,72,128]{2,1,0:T(8,128)(2,1)S(1)} %bitcast.42, ...), custom_call_target="tpu_custom_call" | custom-call | flops 10000000 | bytes 8000000 | tf_op jit(solution)/shard_map/pallas_call | solution.py:301
  (53 shorter events, 8.4 us)
Async XLA Ops:
  7.2 14.6 %copy-start.3 = (bf16[140,1120]{1,0:T(8,128)(2,1)S(1)}, bf16[140,1120]{1,0:T(8,128)(2,1)}, u32[]{:S(2)}) copy-start(bf16[140,1120]{1,0:T(8,128)(2,1)} %param.20) | copy-start | bytes 940804
  7.2 14.7 %copy-start.4 = (bf16[1120,140]{0,1:T(8,128)(2,1)S(1)}, bf16[1120,140]{0,1:T(8,128)(2,1)}, u32[]{:S(2)}) copy-start(bf16[1120,140]{0,1:T(8,128)(2,1)} %param.21) | copy-start | bytes 940804
  7.2 43.4 %all-gather.4.cloned.1.call-start = ((), (), s32[]{:S(2)}) async-start(), calls=%async_computation.2 | async-start | bytes 1658880 | tf_op jit(solution)/shard_map/all_gather | solution.py:387
  11.6 17.5 %all-to-all-start = ((bf16[16,40,128]{2,1,0:T(8,128)(2,1)}), bf16[16,40,128]{2,1,0:T(8,128)(2,1)S(1)}, u32[]{:S(2)}, u32[]{:S(2)}) async-start(bf16[16,40,128]{2,1,0:T(8,128)(2,1)} %bitcast.58), calls=%async_computation | async-start | bytes 327680 | tf_op jit(solution)/shard_map/all_to_all | solution.py:392
  21.7 98.8 %all-gather.6.cloned.1.call-start = ((), (), s32[]{:S(2)}) async-start(), calls=%async_computation.3 | async-start | bytes 5971968 | tf_op jit(solution)/shard_map/all_gather | solution.py:398
  29.1 15.8 %collective-permute-start.7 = (bf16[2,72,1120]{2,1,0:T(8,128)(2,1)S(1)}, bf16[2,72,1120]{2,1,0:T(8,128)(2,1)S(1)}, u32[]{:S(2)}, u32[]{:S(2)}) collective-permute-start(bf16[2,72,1120]{2,1,0:T(8,128)(2,1)S(1)} %fusion.2), channel_id=1, source_target_pairs={{0,32},{32,128},{128,160},{160,0},{1,33},{33,129},{129,161},{161,1... | collective-permute-start | bytes 967688 | tf_op jit(solution)/shard_map/ppermute | solution.py:37
  52.0 13.9 %collective-permute-start.1 = (bf16[4,144,560]{2,1,0:T(8,128)(2,1)S(1)}, bf16[4,144,560]{2,1,0:T(8,128)(2,1)S(1)}, u32[]{:S(2)}, u32[]{:S(2)}) collective-permute-start(bf16[4,144,560]{2,1,0:T(8,128)(2,1)S(1)} %get-tuple-element.40), channel_id=1, source_target_pairs={{0,160},{32,0},{128,32},{160,128},{1,161},{33,1},{129,33},{161,129... | collective-permute-start | bytes 1935368 | tf_op jit(solution)/shard_map/ppermute | solution.py:37
  54.9 14.2 %collective-permute-start = (bf16[4,144,560]{2,1,0:T(8,128)(2,1)S(1)}, bf16[4,144,560]{2,1,0:T(8,128)(2,1)S(1)}, u32[]{:S(2)}, u32[]{:S(2)}) collective-permute-start(bf16[4,144,560]{2,1,0:T(8,128)(2,1)S(1)} %get-tuple-element.41), channel_id=1, source_target_pairs={{0,32},{32,128},{128,160},{160,0},{1,33},{33,129},{129,161},{161,1... | collective-permute-start | bytes 1935368 | tf_op jit(solution)/shard_map/ppermute | solution.py:37
  75.0 9.9 %copy-start.2 = (bf16[128,2240]{0,1:T(8,128)(2,1)S(1)}, bf16[128,2240]{0,1:T(8,128)(2,1)}, u32[]{:S(2)}) copy-start(bf16[128,2240]{0,1:T(8,128)(2,1)} %param.11) | copy-start | bytes 1720324
  75.0 12.6 %collective-permute-start.2 = (bf16[2304,128]{1,0:T(8,128)(2,1)}, bf16[2304,128]{1,0:T(8,128)(2,1)S(1)}, u32[]{:S(2)}, u32[]{:S(2)}) collective-permute-start(bf16[2304,128]{1,0:T(8,128)(2,1)} %get-tuple-element.23), channel_id=1, source_target_pairs={{0,2},{1,3},{2,0},{3,1},{4,6},{5,7},{6,4},{7,5},{8,10},{9,11},{10,... | collective-permute-start | bytes 1769480 | tf_op jit(solution)/shard_map/ppermute | solution.py:37
  78.1 25.5 %collective-permute-start.3 = (bf16[2304,128]{1,0:T(8,128)(2,1)}, bf16[2304,128]{1,0:T(8,128)(2,1)S(1)}, u32[]{:S(2)}, u32[]{:S(2)}) collective-permute-start(bf16[2304,128]{1,0:T(8,128)(2,1)} %get-tuple-element.24), channel_id=1, source_target_pairs={{0,1},{1,2},{2,3},{3,0},{4,5},{5,6},{6,7},{7,4},{8,9},{9,10},{10,1... | collective-permute-start | bytes 1769480 | tf_op jit(solution)/shard_map/ppermute | solution.py:37
  78.1 25.5 %collective-permute-start.4 = (bf16[2304,128]{1,0:T(8,128)(2,1)}, bf16[2304,128]{1,0:T(8,128)(2,1)S(1)}, u32[]{:S(2)}, u32[]{:S(2)}) collective-permute-start(bf16[2304,128]{1,0:T(8,128)(2,1)} %get-tuple-element.25), channel_id=1, source_target_pairs={{0,3},{1,0},{2,1},{3,2},{4,7},{5,4},{6,5},{7,6},{8,11},{9,8},{10,9... | collective-permute-start | bytes 1769480 | tf_op jit(solution)/shard_map/ppermute | solution.py:37
  120.5 20.3 %collective-permute-start.8 = (bf16[8,2,2,72,1120]{4,3,2,1,0:T(8,128)(2,1)}, bf16[8,2,2,72,1120]{4,3,2,1,0:T(8,128)(2,1)}, u32[]{:S(2)}, u32[]{:S(2)}) collective-permute-start(bf16[8,2,2,72,1120]{4,3,2,1,0:T(8,128)(2,1)} %bitcast.45), channel_id=1, source_target_pairs={{0,64},{64,0},{1,65},{65,1},{2,66},{66,2},{3,67},{67,3},{4,68},{68... | collective-permute-start | bytes 15482888 | tf_op jit(solution)/shard_map/ppermute | solution.py:37
  121.3 16.3 %collective-permute-start.6 = (bf16[128,2304]{1,0:T(8,128)(2,1)}, bf16[128,2304]{1,0:T(8,128)(2,1)S(1)}, u32[]{:S(2)}, u32[]{:S(2)}) collective-permute-start(bf16[128,2304]{1,0:T(8,128)(2,1)} %get-tuple-element.34.refs_0_), channel_id=1, source_target_pairs={{0,1},{1,2},{2,3},{3,0},{4,5},{5,6},{6,7},{7,4},{8,9},{9,10},{10,1... | collective-permute-start | bytes 1769480 | tf_op jit(solution)/shard_map/ppermute | solution.py:37
  122.5 15.2 %collective-permute-start.5 = (bf16[128,2304]{1,0:T(8,128)(2,1)}, bf16[128,2304]{1,0:T(8,128)(2,1)S(1)}, u32[]{:S(2)}, u32[]{:S(2)}) collective-permute-start(bf16[128,2304]{1,0:T(8,128)(2,1)} %get-tuple-element.34.refs_0_), channel_id=1, source_target_pairs={{0,3},{1,0},{2,1},{3,2},{4,7},{5,4},{6,5},{7,6},{8,11},{9,8},{10,9... | collective-permute-start | bytes 1769480 | tf_op jit(solution)/shard_map/ppermute | solution.py:37
  137.6 3.1 %copy-start = (bf16[128,2304]{1,0:T(8,128)(2,1)}, bf16[128,2304]{1,0:T(8,128)(2,1)S(1)}, u32[]{:S(2)}) copy-start(bf16[128,2304]{1,0:T(8,128)(2,1)S(1)} %collective-permute-done.6.refs_1_) | copy-start | bytes 1769476
  137.6 11.9 %collective-permute-start.12 = (bf16[64,2304]{1,0:T(8,128)(2,1)S(1)}, bf16[64,2304]{1,0:T(8,128)(2,1)S(1)}, u32[]{:S(2)}, u32[]{:S(2)}) collective-permute-start(bf16[64,2304]{1,0:T(8,128)(2,1)S(1)} %slice.29), channel_id=1, source_target_pairs={{0,1},{1,2},{2,3},{3,0},{4,5},{5,6},{6,7},{7,4},{8,9},{9,10},{10,1... | collective-permute-start | bytes 884744 | tf_op jit(solution)/shard_map/ppermute | solution.py:37
  137.7 3.0 %copy-start.1 = (bf16[128,2304]{1,0:T(8,128)(2,1)}, bf16[128,2304]{1,0:T(8,128)(2,1)S(1)}, u32[]{:S(2)}) copy-start(bf16[128,2304]{1,0:T(8,128)(2,1)S(1)} %collective-permute-done.5.refs_0_) | copy-start | bytes 1769476
  137.8 11.7 %collective-permute-start.11 = (bf16[64,2304]{1,0:T(8,128)(2,1)S(1)}, bf16[64,2304]{1,0:T(8,128)(2,1)S(1)}, u32[]{:S(2)}, u32[]{:S(2)}) collective-permute-start(bf16[64,2304]{1,0:T(8,128)(2,1)S(1)} %slice.28), channel_id=1, source_target_pairs={{0,3},{1,0},{2,1},{3,2},{4,7},{5,4},{6,5},{7,6},{8,11},{9,8},{10,9... | collective-permute-start | bytes 884744 | tf_op jit(solution)/shard_map/ppermute | solution.py:37
  149.5 10.5 %copy-start.8 = (bf16[2304,128]{1,0:T(8,128)(2,1)S(1)}, bf16[2304,128]{1,0:T(8,128)(2,1)}, u32[]{:S(2)}) copy-start(bf16[2304,128]{1,0:T(8,128)(2,1)} %get-tuple-element.33) | copy-start | bytes 1769476
  149.5 11.5 %copy-start.7 = (bf16[2304,128]{1,0:T(8,128)(2,1)S(1)}, bf16[2304,128]{1,0:T(8,128)(2,1)}, u32[]{:S(2)}) copy-start(bf16[2304,128]{1,0:T(8,128)(2,1)} %get-tuple-element.32) | copy-start | bytes 1769476
  149.5 0.7 copy-start.5
  150.2 0.7 copy-start.6
  159.6 15.2 %collective-permute-start.13 = (bf16[2304,128]{1,0:T(8,128)(2,1)}, bf16[2304,128]{1,0:T(8,128)(2,1)S(1)}, u32[]{:S(2)}, u32[]{:S(2)}) collective-permute-start(bf16[2304,128]{1,0:T(8,128)(2,1)} %get-tuple-element.35), channel_id=1, source_target_pairs={{0,2},{1,3},{2,0},{3,1},{4,6},{5,7},{6,4},{7,5},{8,10},{9,11},{10,... | collective-permute-start | bytes 1769480 | tf_op jit(solution)/shard_map/ppermute | solution.py:37
  160.0 26.3 %collective-permute-start.10 = (bf16[2304,128]{1,0:T(8,128)(2,1)S(1)}, bf16[2304,128]{1,0:T(8,128)(2,1)S(1)}, u32[]{:S(2)}, u32[]{:S(2)}) collective-permute-start(bf16[2304,128]{1,0:T(8,128)(2,1)S(1)} %copy-done.8), channel_id=1, source_target_pairs={{0,3},{1,0},{2,1},{3,2},{4,7},{5,4},{6,5},{7,6},{8,11},{9,8},{10,9... | collective-permute-start | bytes 1769480 | tf_op jit(solution)/shard_map/ppermute | solution.py:37
  161.0 28.2 %collective-permute-start.9 = (bf16[2304,128]{1,0:T(8,128)(2,1)S(1)}, bf16[2304,128]{1,0:T(8,128)(2,1)S(1)}, u32[]{:S(2)}, u32[]{:S(2)}) collective-permute-start(bf16[2304,128]{1,0:T(8,128)(2,1)S(1)} %copy-done.7), channel_id=1, source_target_pairs={{0,1},{1,2},{2,3},{3,0},{4,5},{5,6},{6,7},{7,4},{8,9},{9,10},{10,1... | collective-permute-start | bytes 1769480 | tf_op jit(solution)/shard_map/ppermute | solution.py:37
Sparse Core Ops, SparseCore 0:
  10.4 40.1 all-gather.3
  52.4 68.0 all-gather.5

commit v3 on v2

--- a/solution.py
+++ b/solution.py
@@ -314,62 +314,56 @@
 def units_kernel(pieces, *refs):
     token_refs = refs[:pieces]
     own_ref, other_ref = refs[pieces : pieces + 2]
-    out_refs = refs[pieces + 2 : -3]
-    tokens, sums, units = refs[-3:]
-    step = pl.program_id(0)
-
-    def up(ref, first):
-        weight = ref[...].reshape(HALF, -1)
+    out_refs = refs[pieces + 2 : -4]
+    tokens, units, own, arrived_sems = refs[-4:]
+    copies = [
+        pltpu.make_async_copy(own_ref.at[:, :, w], own.at[w], arrived_sems.at[w]) for w in range(2)
+    ]
+    for copy in copies:
+        copy.start()
+    row = 0
+    for token_ref in token_refs:
+        tokens[row : row + token_ref.shape[0], :] = token_ref[...]
+        row += token_ref.shape[0]
+
+    def up(weight, first):
+        weight = weight.reshape(HALF, -1)
         return jnp.dot(tokens[:, first : first + HALF], weight, preferred_element_type=F32)
 
-    def down(ref):
-        weight = ref[...].reshape(HALF, -1)
+    def down(weight, first):
         feed = lax.dot_general(
-            weight, units[...], (((1,), (1,)), ((), ())), preferred_element_type=F32
+            weight.reshape(HALF, -1),
+            units[...],
+            (((1,), (1,)), ((), ())),
+            preferred_element_type=F32,
         ).astype(BF)
         for n, out_ref in enumerate(out_refs):
-            out_ref[...] = feed[:, SHARE * n : SHARE * (n + 1)]
-
-    @pl.when(step == 0)
-    def _():
-        row = 0
-        for token_ref in token_refs:
-            tokens[row : row + token_ref.shape[0], :] = token_ref[...]
-            row += token_ref.shape[0]
-        sums[...] = up(own_ref, 0)
-
-    @pl.when(step == 1)
-    def _():
-        units[...] = jax.nn.gelu(sums[...] + up(other_ref, HALF), approximate=True).astype(BF)
-
-    @pl.when(step == 2)
-    def _():
-        down(own_ref)
-
-    @pl.when(step == 3)
-    def _():
-        down(other_ref)
+            out_ref[first : first + HALF, :] = feed[:, SHARE * n : SHARE * (n + 1)]
+
+    sums = up(other_ref[:, :, 0], HALF)
+    copies[0].wait()
+    sums = sums + up(own[0], 0)
+    units[...] = jax.nn.gelu(sums, approximate=True).astype(BF)
+    down(other_ref[:, :, 1], HALF)
+    copies[1].wait()
+    down(own[1], 0)
 
 
 def unit_terms(tokens, own, other):
     chunks = sum(t.shape[0] for t in tokens) // SHARE
     hidden_units = own.shape[4]
-    block = (8, 2, 1, PADDED, hidden_units)
     return pl.pallas_call(
         functools.partial(units_kernel, len(tokens)),
-        grid=(4,),
         out_shape=[jax.ShapeDtypeStruct((ROWS, SHARE), BF)] * chunks,
-        in_specs=[pl.BlockSpec(t.shape, lambda i: (0, 0)) for t in tokens]
-        + [
-            pl.BlockSpec(block, lambda i: (0, 0, jnp.where(i >= 2, 1, 0), 0, 0)),
-            pl.BlockSpec(block, lambda i: (0, 0, jnp.where(i >= 3, 1, 0), 0, 0)),
-        ],
-        out_specs=[pl.BlockSpec((HALF, SHARE), lambda i: (jnp.where(i >= 3, 1, 0), 0))] * chunks,
+        in_specs=[VMEM] * len(tokens) + [pl.BlockSpec(memory_space=pltpu.HBM), VMEM],
+        out_specs=[VMEM] * chunks,
         scratch_shapes=[
             pltpu.VMEM((SHARE * chunks, ROWS), BF),
-            pltpu.VMEM((SHARE * chunks, hidden_units), F32),
             pltpu.VMEM((SHARE * chunks, hidden_units), BF),
+            pltpu.VMEM((2, 8, 2, PADDED, hidden_units), BF),
+            pltpu.SemaphoreType.DMA((2,)),
         ],
+        compiler_params=pltpu.CompilerParams(vmem_limit_bytes=28 << 20),
         cost_estimate=cost(4 * SHARE * chunks * ROWS * hidden_units, 4 * ROWS * hidden_units),
     )(*tokens, own, other)
 
@@ -410,13 +404,13 @@
     above, below = along_y(normed, -1), along_y(normed, 1)
     far = [along_y(above[: SHARE // 2], -1), along_y(below[SHARE // 2 :], 1)]
     half, _ = lax.optimization_barrier((half, normed))
-    other = other_core(half)
-    near = unit_terms([above, below], half, other)
+    weights = [half, in_vmem(other_core(half))]
+    near = unit_terms([in_vmem(above), in_vmem(below)], *weights)
     feeds = []
     for d, part in zip((1, 3), near):
         feeds.append(along_y(part, d))
     normed, _ = lax.optimization_barrier((normed, near[0]))
-    rest = unit_terms([normed] + far, half, other)
+    rest = unit_terms([normed] + [in_vmem(f) for f in far], *weights)
     feeds += [along_y(rest[1], 2), rest[0]]
     step = step_size[None] if step_size.ndim == 0 else step_size
     velocity, advanced = last(place, step, feeds, hidden, latent_pieces, vectors)

time: 200 us -> 196 us (0.980)
  Pallas kernels: 42.9 us -> 37.2 us
    pallas_call x2, Pallas kernels: 17.5 us -> 11.7 us  [unit_terms(): pl.pallas_call(functools.partial(units_kernel, len(tokens)), out_shape=[j...]
  transfers between devices with their start and end apart: 17 -> 17, of which waited for: 10 -> 10; matrix products, arithmetic and copies ran while one was open for 5% -> 5% of each run, Pallas kernels for 15% -> 14%
where the time goes in v3:
time: 196 us
  waiting for transfers between devices  87.8 us (45%)
  Pallas kernels  37.2 us (19%)
  starting transfers between devices  27.8 us (14%)
  between operations  15 us (8%)
  blocking collectives  13.5 us (7%)
  local copies, waits for them, and re-layouts  9.68 us (5%)
  matrix products  3.07 us (2%)
    ppermute x14, waiting for transfers between devices, permute(): return lax.ppermute(block, tuple(axes) if len(axes) > 1 else axes[0], pairs)  63.3 us
    ppermute x14, starting transfers between devices, permute(): return lax.ppermute(block, tuple(axes) if len(axes) > 1 else axes[0], pairs)  17.7 us
    all_to_all x1, blocking collectives, block(): before = lax.all_to_all(ahead, ('xl', 'z'), 0, 0).reshape(STATE_ROWS, SHARE)  13.5 us
    all_gather x1, waiting for transfers between devices, block(): half = lax.all_gather(jnp.stack([mine, mine_x]), 'z', axis=0)  12.8 us
    pallas_call x2, Pallas kernels, unit_terms(): pl.pallas_call(functools.partial(units_kernel, len(tokens)), out_shape=[j...  11.7 us
    all_to_all x1, starting transfers between devices, block(): slices = lax.all_to_all(packed.reshape(16, -1, SHARE), ('xl', 'z'), 0, 0)  10 us
    all_to_all x1, waiting for transfers between devices, block(): slices = lax.all_to_all(packed.reshape(16, -1, SHARE), ('xl', 'z'), 0, 0)  7.04 us
    pallas_call x1, Pallas kernels, head_terms(): pl.pallas_call(head_kernel, out_shape=[jax.ShapeDtypeStruct((ROWS, SHARE)...  5.93 us
  transfers between devices with their start and end apart: 17, of which 10 were waited for; matrix products, arithmetic and copies ran while one was open for 5% of the time, Pallas kernels for 14%

profile of v3, /device:TPU:1, one launch (start us, length us, event | category | flops | bytes accessed | tf_op | source)
XLA Modules:
  0.0 195.8 jit_solution(13554960968681599794)
XLA Ops:
  7.2 1.0 reshape.80
  9.0 2.7 %shard_map.122 = (f32[5,512]{1,0:T(8,128)}, bf16[640,128]{1,0:T(8,128)(2,1)}) custom-call(bf16[560,512]{1,0:T(8,128)(2,1)} %bitcast.60, bf16[560,512]{1,0:T(8,128)(2,1)} %bitcast.62, f32[5,512]{1,0:T(8,128)} %decay_ref.1), custom_call_target="tpu_custom_call" | custom-call | flops 1000000000 | bytes 3000000 | tf_op jit(solution)/shard_map/pallas_call | solution.py:122
  11.6 10.0 %all-to-all-start = ((bf16[16,40,128]{2,1,0:T(8,128)(2,1)}), bf16[16,40,128]{2,1,0:T(8,128)(2,1)S(1)}, u32[]{:S(2)}, u32[]{:S(2)}) async-start(bf16[16,40,128]{2,1,0:T(8,128)(2,1)} %bitcast.58), calls=%async_computation | async-start | bytes 327680 | tf_op jit(solution)/shard_map/all_to_all | solution.py:386
  22.1 7.0 %all-to-all-done.blocks_ref = bf16[16,40,128]{2,1,0:T(8,128)(2,1)S(1)} async-done(((bf16[16,40,128]{2,1,0:T(8,128)(2,1)}), bf16[16,40,128]{2,1,0:T(8,128)(2,1)S(1)}, u32[]{:S(2)}, u32[]{:S(2)}) %all-to-all-start) | async-done | bytes 163872 | tf_op jit(solution)/shard_map/all_to_all | solution.py:386
  29.9 1.6 shard_map.124
  31.5 13.5 %all_to_all.10 = bf16[16,40,128]{2,1,0:T(8,128)(2,1)S(1)} all-to-all(bf16[16,40,128]{2,1,0:T(8,128)(2,1)} %shard_map.124), channel_id=1, replica_groups=mesh['xh'=2,'c'=2,'xl'=2,'z'=8,'y'=4] {'xl','z'}, dimensions={0} | all-to-all | bytes 327680 | tf_op jit(solution)/shard_map/all_to_all | solution.py:390
  45.9 4.7 %all-gather.4.cloned.1.call-done.own_ref = bf16[8,144,560]{2,1,0:T(8,128)(2,1)} async-done(((bf16[1,144,560]{2,1,0:T(8,128)(2,1)}), bf16[8,144,560]{2,1,0:T(8,128)(2,1)}) %all-gather.4.cloned.1.call-update) | async-done | bytes 1290256 | tf_op jit(solution)/shard_map/all_gather | solution.py:381
  50.6 1.5 fusion.6
  52.0 2.8 %collective-permute-start.1 = (bf16[4,144,560]{2,1,0:T(8,128)(2,1)S(1)}, bf16[4,144,560]{2,1,0:T(8,128)(2,1)S(1)}, u32[]{:S(2)}, u32[]{:S(2)}) collective-permute-start(bf16[4,144,560]{2,1,0:T(8,128)(2,1)S(1)} %get-tuple-element.40), channel_id=1, source_target_pairs={{0,160},{32,0},{128,32},{160,128},{1,161},{33,1},{129,33},{161,129... | collective-permute-start | bytes 1935368 | tf_op jit(solution)/shard_map/ppermute | solution.py:37
  55.5 4.9 %shard_map.123.inner_ref = f32[560,512]{1,0:T(8,128)} custom-call(bf16[560,512]{1,0:T(8,128)(2,1)} %bitcast.52, bf16[560,512]{1,0:T(8,128)(2,1)} %bitcast.61, bf16[560,512]{1,0:T(8,128)(2,1)} %bitcast.63, f32[5,512]{1,0:T(8,128)} %get-tuple-element.21.cumulative_ref, s32[1,512]{1,0:T(1,128)} %bitcast.66), custom_call_target="tpu_custom_call" | custom-call | flops 5000000000 | bytes 4000000 | tf_op jit(solution)/shard_map/pallas_call | solution.py:171
  60.4 2.6 %shard_map.125.mixed_ref = bf16[560,512]{1,0:T(8,128)(2,1)} custom-call(bf16[560,512]{1,0:T(8,128)(2,1)} %bitcast.53, f32[560,512]{1,0:T(8,128)} %shard_map.123.inner_ref, f32[5,512]{1,0:T(8,128)} %get-tuple-element.21.cumulative_ref, bf16[640,128]{1,0:T(8,128)(2,1)S(1)} %bitcast.41), custom_call_target="tpu_custom_call" | custom-call | flops 100000000 | bytes 4000000 | tf_op jit(solution)/shard_map/pallas_call | solution.py:194
  63.1 2.9 %collective-permute-done.1.second_ref = bf16[4,144,560]{2,1,0:T(8,128)(2,1)S(1)} collective-permute-done((bf16[4,144,560]{2,1,0:T(8,128)(2,1)S(1)}, bf16[4,144,560]{2,1,0:T(8,128)(2,1)S(1)}, u32[]{:S(2)}, u32[]{:S(2)}) %collective-permute-start.1) | collective-permute-done | bytes 645152 | tf_op jit(solution)/shard_map/ppermute | solution.py:37
  66.0 3.1 %collective-permute-done.first_ref = bf16[4,144,560]{2,1,0:T(8,128)(2,1)S(1)} collective-permute-done((bf16[4,144,560]{2,1,0:T(8,128)(2,1)S(1)}, bf16[4,144,560]{2,1,0:T(8,128)(2,1)S(1)}, u32[]{:S(2)}, u32[]{:S(2)}) %collective-permute-start) | collective-permute-done | bytes 645152 | tf_op jit(solution)/shard_map/ppermute | solution.py:37
  69.1 5.9 %shard_map.126 = (bf16[2304,128]{1,0:T(8,128)(2,1)}, bf16[2304,128]{1,0:T(8,128)(2,1)}, bf16[2304,128]{1,0:T(8,128)(2,1)}, bf16[2304,128]{1,0:T(8,128)(2,1)}) custom-call(s32[3]{0:T(128)} %pad_add_fusion.place_ref, bf16[560,512]{1,0:T(8,128)(2,1)} %shard_map.125.mixed_ref, bf16[8,144,560]{2,1,0:T(8,128)(2,1)} %all-gather.4.cloned.1.call-done.own_ref, ...), custom_call_target="tpu_custom_call" | custom-call | flops 2000000000 | bytes 5000000 | tf_op jit(solution)/shard_map/pallas_call | solution.py:221
  75.0 3.2 %collective-permute-start.2 = (bf16[2304,128]{1,0:T(8,128)(2,1)}, bf16[2304,128]{1,0:T(8,128)(2,1)S(1)}, u32[]{:S(2)}, u32[]{:S(2)}) collective-permute-start(bf16[2304,128]{1,0:T(8,128)(2,1)} %get-tuple-element.23), channel_id=1, source_target_pairs={{0,2},{1,3},{2,0},{3,1},{4,6},{5,7},{6,4},{7,5},{8,10},{9,11},{10,... | collective-permute-start | bytes 1769480 | tf_op jit(solution)/shard_map/ppermute | solution.py:37
  78.2 2.7 %collective-permute-start.4 = (bf16[2304,128]{1,0:T(8,128)(2,1)}, bf16[2304,128]{1,0:T(8,128)(2,1)S(1)}, u32[]{:S(2)}, u32[]{:S(2)}) collective-permute-start(bf16[2304,128]{1,0:T(8,128)(2,1)} %get-tuple-element.25), channel_id=1, source_target_pairs={{0,3},{1,0},{2,1},{3,2},{4,7},{5,4},{6,5},{7,6},{8,11},{9,8},{10,9... | collective-permute-start | bytes 1769480 | tf_op jit(solution)/shard_map/ppermute | solution.py:37
  81.6 3.1 %convolution_reduce_fusion = f32[8960]{0:T(1024)S(1)} fusion(bf16[256,1]{0,1:T(2,128)(2,1)S(1)} %reshape.105, bf16[256,8960]{1,0:T(8,128)(2,1)} %param.18), kind=kOutput, calls=%fused_computation | convolution fusion | flops 4587520 | bytes 4623872 | tf_op jit(solution)/shard_map/dot_general | solution.py:74
  86.5 1.1 pad.21.vector_ref
  87.6 16.0 %collective-permute-done.3 = bf16[2304,128]{1,0:T(8,128)(2,1)S(1)} collective-permute-done((bf16[2304,128]{1,0:T(8,128)(2,1)}, bf16[2304,128]{1,0:T(8,128)(2,1)S(1)}, u32[]{:S(2)}, u32[]{:S(2)}) %collective-permute-start.3) | collective-permute-done | bytes 589856 | tf_op jit(solution)/shard_map/ppermute | solution.py:37
  103.7 4.0 %shard_map.127 = (f32[32,72,128]{2,1,0:T(8,128)}, bf16[128,2304]{1,0:T(8,128)(2,1)}) custom-call(s32[3]{0:T(128)} %pad_add_fusion.place_ref, bf16[32,72,128]{2,1,0:T(8,128)(2,1)S(1)} %bitcast.42, bf16[32,72,128]{2,1,0:T(8,128)(2,1)S(1)} %bitcast.43, bf16[32,72,128]{2,1,0:T(8,128)(2,1)S(1)} %bitcast.44, bf16[32,72,128]{2,1,0:T(8,128)(2,1)} %bitcast.51, ...), custom_call_target="tpu_custom_call" | custom-call | flops 10000000 | bytes 8000000 | tf_op jit(solution)/shard_map/pallas_call | solution.py:269
  107.7 12.8 %all-gather.6.cloned.1.call-done = bf16[16,2,72,1120]{3,2,1,0:T(8,128)(2,1)} async-done(((bf16[2,2,72,1120]{3,2,1,0:T(8,128)(2,1)}), bf16[16,2,72,1120]{3,2,1,0:T(8,128)(2,1)}) %all-gather.6.cloned.1.call-update) | async-done | bytes 5160976 | tf_op jit(solution)/shard_map/all_gather | solution.py:392
  121.3 1.2 collective-permute-start.6
  122.5 1.5 collective-permute-start.5
  124.0 13.6 %collective-permute-done.6.refs_1_ = bf16[128,2304]{1,0:T(8,128)(2,1)S(1)} collective-permute-done((bf16[128,2304]{1,0:T(8,128)(2,1)}, bf16[128,2304]{1,0:T(8,128)(2,1)S(1)}, u32[]{:S(2)}, u32[]{:S(2)}) %collective-permute-start.6) | collective-permute-done | bytes 589856 | tf_op jit(solution)/shard_map/ppermute | solution.py:37
  137.8 2.9 %collective-permute-start.11 = (bf16[64,2304]{1,0:T(8,128)(2,1)S(1)}, bf16[64,2304]{1,0:T(8,128)(2,1)S(1)}, u32[]{:S(2)}, u32[]{:S(2)}) collective-permute-start(bf16[64,2304]{1,0:T(8,128)(2,1)S(1)} %slice.28), channel_id=1, source_target_pairs={{0,3},{1,0},{2,1},{3,2},{4,7},{5,4},{6,5},{7,6},{8,11},{9,8},{10,9... | collective-permute-start | bytes 884744 | tf_op jit(solution)/shard_map/ppermute | solution.py:37
  140.7 2.5 %copy-done = bf16[16,2,72,1120]{3,2,1,0:T(8,128)(2,1)S(1)} copy-done((bf16[16,2,72,1120]{3,2,1,0:T(8,128)(2,1)S(1)}, bf16[16,2,72,1120]{3,2,1,0:T(8,128)(2,1)}, u32[]{:S(2)}) %copy-start) | copy-done | bytes 5160984
  143.2 5.9 %shard_map.128 = (bf16[2304,128]{1,0:T(8,128)(2,1)S(1)}, bf16[2304,128]{1,0:T(8,128)(2,1)S(1)}) custom-call(bf16[128,2304]{1,0:T(8,128)(2,1)S(1)} %collective-permute-done.5.refs_0_, bf16[128,2304]{1,0:T(8,128)(2,1)S(1)} %collective-permute-done.6.refs_1_, bf16[8,2,2,72,1120]{4,3,2,1,0:T(8,128)(2,1)S(1)} %bitcast.39, ...), custom_call_target="tpu_custom_call" | custom-call | flops 2642411520 | bytes 10321920 | tf_op jit(solution)/shard_map/pallas_call | solution.py:355
  149.1 5.9 %shard_map.129 = (bf16[2304,128]{1,0:T(8,128)(2,1)S(1)}, bf16[2304,128]{1,0:T(8,128)(2,1)S(1)}) custom-call(bf16[128,2304]{1,0:T(8,128)(2,1)S(1)} %copy-done.1, bf16[64,2304]{1,0:T(8,128)(2,1)S(1)} %collective-permute-done.11.refs_1_, bf16[64,2304]{1,0:T(8,128)(2,1)S(1)} %collective-permute-done.12.refs_2_, bf16[8,2,2,72,1120]{4,3,2,1,0:T(8,128)(2,1)S(1)} %bitcast.40, ...), custom_call_target="tpu_custom_call" | custom-call | flops 2642411520 | bytes 10321920 | tf_op jit(solution)/shard_map/pallas_call | solution.py:355
  157.6 13.2 %collective-permute-done.13 = bf16[2304,128]{1,0:T(8,128)(2,1)S(1)} collective-permute-done((bf16[2304,128]{1,0:T(8,128)(2,1)S(1)}, bf16[2304,128]{1,0:T(8,128)(2,1)S(1)}, u32[]{:S(2)}, u32[]{:S(2)}) %collective-permute-start.13) | collective-permute-done | bytes 589856 | tf_op jit(solution)/shard_map/ppermute | solution.py:37
  170.8 11.2 %collective-permute-done.10 = bf16[2304,128]{1,0:T(8,128)(2,1)S(1)} collective-permute-done((bf16[2304,128]{1,0:T(8,128)(2,1)S(1)}, bf16[2304,128]{1,0:T(8,128)(2,1)S(1)}, u32[]{:S(2)}, u32[]{:S(2)}) %collective-permute-start.10) | collective-permute-done | bytes 589856 | tf_op jit(solution)/shard_map/ppermute | solution.py:37
  182.0 3.2 %collective-permute-done.9 = bf16[2304,128]{1,0:T(8,128)(2,1)S(1)} collective-permute-done((bf16[2304,128]{1,0:T(8,128)(2,1)S(1)}, bf16[2304,128]{1,0:T(8,128)(2,1)S(1)}, u32[]{:S(2)}, u32[]{:S(2)}) %collective-permute-start.9) | collective-permute-done | bytes 589856 | tf_op jit(solution)/shard_map/ppermute | solution.py:37
  185.2 3.7 %shard_map.130 = (bf16[2240,128]{1,0:T(8,128)(2,1)}, bf16[2240,128]{1,0:T(8,128)(2,1)}) custom-call(s32[3]{0:T(128)} %pad_add_fusion.place_ref, f32[1]{0:T(128)S(6)} %sub.13.step_ref, bf16[32,72,128]{2,1,0:T(8,128)(2,1)S(1)} %bitcast.48, bf16[32,72,128]{2,1,0:T(8,128)(2,1)S(1)} %bitcast.47, bf16[32,72,128]{2,1,0:T(8,128)(2,1)S(1)} %bitcast.46, ...), custom_call_target="tpu_custom_call" | custom-call | flops 10000000 | bytes 8000000 | tf_op jit(solution)/shard_map/pallas_call | solution.py:301
  (47 shorter events, 8.8 us)
Async XLA Ops:
  7.2 14.6 %copy-start.4 = (bf16[140,1120]{1,0:T(8,128)(2,1)S(1)}, bf16[140,1120]{1,0:T(8,128)(2,1)}, u32[]{:S(2)}) copy-start(bf16[140,1120]{1,0:T(8,128)(2,1)} %param.20) | copy-start | bytes 940804
  7.2 14.7 %copy-start.5 = (bf16[1120,140]{0,1:T(8,128)(2,1)S(1)}, bf16[1120,140]{0,1:T(8,128)(2,1)}, u32[]{:S(2)}) copy-start(bf16[1120,140]{0,1:T(8,128)(2,1)} %param.21) | copy-start | bytes 940804
  7.2 43.4 %all-gather.4.cloned.1.call-start = ((), (), s32[]{:S(2)}) async-start(), calls=%async_computation.2 | async-start | bytes 1658880 | tf_op jit(solution)/shard_map/all_gather | solution.py:381
  11.6 17.5 %all-to-all-start = ((bf16[16,40,128]{2,1,0:T(8,128)(2,1)}), bf16[16,40,128]{2,1,0:T(8,128)(2,1)S(1)}, u32[]{:S(2)}, u32[]{:S(2)}) async-start(bf16[16,40,128]{2,1,0:T(8,128)(2,1)} %bitcast.58), calls=%async_computation | async-start | bytes 327680 | tf_op jit(solution)/shard_map/all_to_all | solution.py:386
  21.7 98.8 %all-gather.6.cloned.1.call-start = ((), (), s32[]{:S(2)}) async-start(), calls=%async_computation.3 | async-start | bytes 5971968 | tf_op jit(solution)/shard_map/all_gather | solution.py:392
  29.1 15.8 %collective-permute-start.7 = (bf16[2,72,1120]{2,1,0:T(8,128)(2,1)S(1)}, bf16[2,72,1120]{2,1,0:T(8,128)(2,1)S(1)}, u32[]{:S(2)}, u32[]{:S(2)}) collective-permute-start(bf16[2,72,1120]{2,1,0:T(8,128)(2,1)S(1)} %fusion.2), channel_id=1, source_target_pairs={{0,32},{32,128},{128,160},{160,0},{1,33},{33,129},{129,161},{161,1... | collective-permute-start | bytes 967688 | tf_op jit(solution)/shard_map/ppermute | solution.py:37
  52.0 13.9 %collective-permute-start.1 = (bf16[4,144,560]{2,1,0:T(8,128)(2,1)S(1)}, bf16[4,144,560]{2,1,0:T(8,128)(2,1)S(1)}, u32[]{:S(2)}, u32[]{:S(2)}) collective-permute-start(bf16[4,144,560]{2,1,0:T(8,128)(2,1)S(1)} %get-tuple-element.40), channel_id=1, source_target_pairs={{0,160},{32,0},{128,32},{160,128},{1,161},{33,1},{129,33},{161,129... | collective-permute-start | bytes 1935368 | tf_op jit(solution)/shard_map/ppermute | solution.py:37
  54.9 14.2 %collective-permute-start = (bf16[4,144,560]{2,1,0:T(8,128)(2,1)S(1)}, bf16[4,144,560]{2,1,0:T(8,128)(2,1)S(1)}, u32[]{:S(2)}, u32[]{:S(2)}) collective-permute-start(bf16[4,144,560]{2,1,0:T(8,128)(2,1)S(1)} %get-tuple-element.41), channel_id=1, source_target_pairs={{0,32},{32,128},{128,160},{160,0},{1,33},{33,129},{129,161},{161,1... | collective-permute-start | bytes 1935368 | tf_op jit(solution)/shard_map/ppermute | solution.py:37
  75.0 9.9 %copy-start.3 = (bf16[128,2240]{0,1:T(8,128)(2,1)S(1)}, bf16[128,2240]{0,1:T(8,128)(2,1)}, u32[]{:S(2)}) copy-start(bf16[128,2240]{0,1:T(8,128)(2,1)} %param.11) | copy-start | bytes 1720324
  75.0 12.6 %collective-permute-start.2 = (bf16[2304,128]{1,0:T(8,128)(2,1)}, bf16[2304,128]{1,0:T(8,128)(2,1)S(1)}, u32[]{:S(2)}, u32[]{:S(2)}) collective-permute-start(bf16[2304,128]{1,0:T(8,128)(2,1)} %get-tuple-element.23), channel_id=1, source_target_pairs={{0,2},{1,3},{2,0},{3,1},{4,6},{5,7},{6,4},{7,5},{8,10},{9,11},{10,... | collective-permute-start | bytes 1769480 | tf_op jit(solution)/shard_map/ppermute | solution.py:37
  78.2 25.5 %collective-permute-start.3 = (bf16[2304,128]{1,0:T(8,128)(2,1)}, bf16[2304,128]{1,0:T(8,128)(2,1)S(1)}, u32[]{:S(2)}, u32[]{:S(2)}) collective-permute-start(bf16[2304,128]{1,0:T(8,128)(2,1)} %get-tuple-element.24), channel_id=1, source_target_pairs={{0,1},{1,2},{2,3},{3,0},{4,5},{5,6},{6,7},{7,4},{8,9},{9,10},{10,1... | collective-permute-start | bytes 1769480 | tf_op jit(solution)/shard_map/ppermute | solution.py:37
  78.2 25.5 %collective-permute-start.4 = (bf16[2304,128]{1,0:T(8,128)(2,1)}, bf16[2304,128]{1,0:T(8,128)(2,1)S(1)}, u32[]{:S(2)}, u32[]{:S(2)}) collective-permute-start(bf16[2304,128]{1,0:T(8,128)(2,1)} %get-tuple-element.25), channel_id=1, source_target_pairs={{0,3},{1,0},{2,1},{3,2},{4,7},{5,4},{6,5},{7,6},{8,11},{9,8},{10,9... | collective-permute-start | bytes 1769480 | tf_op jit(solution)/shard_map/ppermute | solution.py:37
  120.5 20.3 %collective-permute-start.8 = (bf16[8,2,2,72,1120]{4,3,2,1,0:T(8,128)(2,1)}, bf16[8,2,2,72,1120]{4,3,2,1,0:T(8,128)(2,1)S(1)}, u32[]{:S(2)}, u32[]{:S(2)}) collective-permute-start(bf16[8,2,2,72,1120]{4,3,2,1,0:T(8,128)(2,1)} %bitcast.38), channel_id=1, source_target_pairs={{0,64},{64,0},{1,65},{65,1},{2,66},{66,2},{3,67},{67,3},{4,68},{68... | collective-permute-start | bytes 15482888 | tf_op jit(solution)/shard_map/ppermute | solution.py:37
  121.3 16.3 %collective-permute-start.6 = (bf16[128,2304]{1,0:T(8,128)(2,1)}, bf16[128,2304]{1,0:T(8,128)(2,1)S(1)}, u32[]{:S(2)}, u32[]{:S(2)}) collective-permute-start(bf16[128,2304]{1,0:T(8,128)(2,1)} %get-tuple-element.34.refs_0_), channel_id=1, source_target_pairs={{0,1},{1,2},{2,3},{3,0},{4,5},{5,6},{6,7},{7,4},{8,9},{9,10},{10,1... | collective-permute-start | bytes 1769480 | tf_op jit(solution)/shard_map/ppermute | solution.py:37
  122.5 15.2 %collective-permute-start.5 = (bf16[128,2304]{1,0:T(8,128)(2,1)}, bf16[128,2304]{1,0:T(8,128)(2,1)S(1)}, u32[]{:S(2)}, u32[]{:S(2)}) collective-permute-start(bf16[128,2304]{1,0:T(8,128)(2,1)} %get-tuple-element.34.refs_0_), channel_id=1, source_target_pairs={{0,3},{1,0},{2,1},{3,2},{4,7},{5,4},{6,5},{7,6},{8,11},{9,8},{10,9... | collective-permute-start | bytes 1769480 | tf_op jit(solution)/shard_map/ppermute | solution.py:37
  137.6 11.5 %collective-permute-start.12 = (bf16[64,2304]{1,0:T(8,128)(2,1)S(1)}, bf16[64,2304]{1,0:T(8,128)(2,1)S(1)}, u32[]{:S(2)}, u32[]{:S(2)}) collective-permute-start(bf16[64,2304]{1,0:T(8,128)(2,1)S(1)} %slice.29), channel_id=1, source_target_pairs={{0,1},{1,2},{2,3},{3,0},{4,5},{5,6},{6,7},{7,4},{8,9},{9,10},{10,1... | collective-permute-start | bytes 884744 | tf_op jit(solution)/shard_map/ppermute | solution.py:37
  137.7 11.4 %copy-start.1 = (bf16[128,2304]{1,0:T(8,128)(2,1)S(1)}, bf16[128,2304]{1,0:T(8,128)(2,1)}, u32[]{:S(2)}) copy-start(bf16[128,2304]{1,0:T(8,128)(2,1)} %get-tuple-element.34.refs_0_) | copy-start | bytes 1769476
  137.8 11.3 %collective-permute-start.11 = (bf16[64,2304]{1,0:T(8,128)(2,1)S(1)}, bf16[64,2304]{1,0:T(8,128)(2,1)S(1)}, u32[]{:S(2)}, u32[]{:S(2)}) collective-permute-start(bf16[64,2304]{1,0:T(8,128)(2,1)S(1)} %slice.28), channel_id=1, source_target_pairs={{0,3},{1,0},{2,1},{3,2},{4,7},{5,4},{6,5},{7,6},{8,11},{9,8},{10,9... | collective-permute-start | bytes 884744 | tf_op jit(solution)/shard_map/ppermute | solution.py:37
  140.7 2.5 %copy-start = (bf16[16,2,72,1120]{3,2,1,0:T(8,128)(2,1)S(1)}, bf16[16,2,72,1120]{3,2,1,0:T(8,128)(2,1)}, u32[]{:S(2)}) copy-start(bf16[16,2,72,1120]{3,2,1,0:T(8,128)(2,1)} %all-gather.6.cloned.1.call-done) | copy-start | bytes 15482884
  155.0 0.8 copy-start.2
  155.8 15.0 %collective-permute-start.13 = (bf16[2304,128]{1,0:T(8,128)(2,1)S(1)}, bf16[2304,128]{1,0:T(8,128)(2,1)S(1)}, u32[]{:S(2)}, u32[]{:S(2)}) collective-permute-start(bf16[2304,128]{1,0:T(8,128)(2,1)S(1)} %get-tuple-element.35), channel_id=1, source_target_pairs={{0,2},{1,3},{2,0},{3,1},{4,6},{5,7},{6,4},{7,5},{8,10},{9,11},{10,... | collective-permute-start | bytes 1769480 | tf_op jit(solution)/shard_map/ppermute | solution.py:37
  156.1 25.9 %collective-permute-start.10 = (bf16[2304,128]{1,0:T(8,128)(2,1)S(1)}, bf16[2304,128]{1,0:T(8,128)(2,1)S(1)}, u32[]{:S(2)}, u32[]{:S(2)}) collective-permute-start(bf16[2304,128]{1,0:T(8,128)(2,1)S(1)} %get-tuple-element.33), channel_id=1, source_target_pairs={{0,3},{1,0},{2,1},{3,2},{4,7},{5,4},{6,5},{7,6},{8,11},{9,8},{10,9... | collective-permute-start | bytes 1769480 | tf_op jit(solution)/shard_map/ppermute | solution.py:37
  157.0 28.2 %collective-permute-start.9 = (bf16[2304,128]{1,0:T(8,128)(2,1)S(1)}, bf16[2304,128]{1,0:T(8,128)(2,1)S(1)}, u32[]{:S(2)}, u32[]{:S(2)}) collective-permute-start(bf16[2304,128]{1,0:T(8,128)(2,1)S(1)} %get-tuple-element.32), channel_id=1, source_target_pairs={{0,1},{1,2},{2,3},{3,0},{4,5},{5,6},{6,7},{7,4},{8,9},{9,10},{10,1... | collective-permute-start | bytes 1769480 | tf_op jit(solution)/shard_map/ppermute | solution.py:37
Sparse Core Ops, SparseCore 0:
  10.4 40.1 all-gather.3
  52.4 68.0 all-gather.5

commit v4 on v3

--- a/solution.py
+++ b/solution.py
@@ -25,6 +25,7 @@
 ROWS = PIECES * PADDED
 VMEM = pl.BlockSpec(memory_space=pltpu.VMEM)
 SMEM = pl.BlockSpec(memory_space=pltpu.SMEM)
+SMALL = pltpu.CompilerParams(vmem_limit_bytes=56 << 20)
 
 
 def permute(block, axes, route):
@@ -200,11 +201,8 @@
     )(queries, inner, cumulative, in_vmem(before))
 
 
-FARTHEST_FIRST = (2, 1, 3, 0)
-
-
-def head_kernel(place_ref, mixed_ref, own_ref, first_ref, second_ref, *out_refs):
-    for d, out_ref in zip(FARTHEST_FIRST, out_refs):
+def head_kernel(distances, place_ref, mixed_ref, own_ref, first_ref, second_ref, *out_refs):
+    for d, out_ref in zip(distances, out_refs):
         start = pl.multiple_of(((place_ref[2] + d) % 4) * SHARE, SHARE)
         tokens = mixed_ref[:, pl.ds(start, SHARE)]
         row = 0
@@ -217,14 +215,15 @@
             row += rows
 
 
-def head_terms(place, mixed, weights):
-    return pl.pallas_call(
-        head_kernel,
-        out_shape=[jax.ShapeDtypeStruct((ROWS, SHARE), BF)] * 4,
+def head_terms(distances, place, mixed, weights):
+    return pl.pallas_call(
+        functools.partial(head_kernel, distances),
+        out_shape=[jax.ShapeDtypeStruct((ROWS, SHARE), BF)] * len(distances),
         in_specs=[SMEM] + [VMEM] * 4,
-        out_specs=[VMEM] * 4,
-        cost_estimate=cost(2 * 10**9, 5 * 10**6),
-    )(place, mixed, weights[0], *[in_vmem(w) for w in weights[1:]])
+        out_specs=[VMEM] * len(distances),
+        cost_estimate=cost(10**9, 4 * 10**6),
+        compiler_params=SMALL,
+    )(place, mixed, *weights)
 
 
 def piece_table(place_ref):
@@ -276,6 +275,7 @@
         out_specs=(VMEM, VMEM),
         scratch_shapes=[pltpu.VMEM((ROWS, SHARE), F32)],
         cost_estimate=cost(10**7, 8 * 10**6),
+        compiler_params=SMALL,
     )(place, *arrived(terms), latents, vectors)
 
 
@@ -305,6 +305,7 @@
         out_specs=(VMEM, VMEM),
         scratch_shapes=[pltpu.VMEM((WIDTH, SHARE), F32)] * 2,
         cost_estimate=cost(10**7, 8 * 10**6),
+        compiler_params=SMALL,
     )(place, step_size, *arrived(feeds), hidden, latents, vectors)
 
 
@@ -363,7 +364,7 @@
             pltpu.VMEM((2, 8, 2, PADDED, hidden_units), BF),
             pltpu.SemaphoreType.DMA((2,)),
         ],
-        compiler_params=pltpu.CompilerParams(vmem_limit_bytes=28 << 20),
+        compiler_params=pltpu.CompilerParams(vmem_limit_bytes=50 << 20),
         cost_estimate=cost(4 * SHARE * chunks * ROWS * hidden_units, 4 * ROWS * hidden_units),
     )(*tokens, own, other)
 
@@ -379,7 +380,7 @@
 
     out_mine = padded_pieces(w_out.T).reshape(2 * PADDED, -1)
     out_own = lax.all_gather(out_mine, "z", axis=0)
-    out_weights = [out_own, along_x(out_own[:4], 1), along_x(out_own[4:], -1)]
+    out_weights = [out_own, in_vmem(along_x(out_own[:4], 1)), in_vmem(along_x(out_own[4:], -1))]
     mine = core_half(jnp.stack([padded_pieces(w_up), padded_pieces(w_down.T)]))
     queries, keys, values = queries.T, keys.T, values.T
     cumulative, packed = own_state(keys, values, log_decay)
@@ -393,13 +394,18 @@
     inner = inner_part(queries, keys, values, cumulative, block_ids[None, :])
     mixed = mix(queries, inner, cumulative, before)
 
-    parts = head_terms(place, mixed, out_weights)
-    terms = [along_y(parts[i], d) for i, d in enumerate(FARTHEST_FIRST[:3])] + [parts[3]]
+    early = head_terms((2, 1), place, mixed, out_weights)
+    terms = []
+    for d, part in zip((2, 1), early):
+        terms.append(along_y(part, d))
+    mixed, _ = lax.optimization_barrier((mixed, early[0]))
+    later = head_terms((3, 0), place, mixed, out_weights)
+    terms += [along_y(later[0], 3), later[1]]
 
     shifts, step_size = modulation_of(t_index, w_mod)
     vectors = padded_pieces(shifts.reshape(4, WIDTH).T)
     latent_pieces = padded_pieces(latents.T)
-    hidden, normed = norm(place, terms, latent_pieces, vectors)
+    hidden, normed = norm(place, terms, in_vmem(latent_pieces), in_vmem(vectors))
 
     above, below = along_y(normed, -1), along_y(normed, 1)
     far = [along_y(above[: SHARE // 2], -1), along_y(below[SHARE // 2 :], 1)]

time: 196 us -> 199 us (1.015)
  Pallas kernels: 37.2 us -> 44.7 us
  local copies, waits for them, and re-layouts: 9.68 us -> 6.79 us
    pallas_call x2, Pallas kernels: 11.7 us -> 17.1 us  [unit_terms(): pl.pallas_call(functools.partial(units_kernel, len(tokens)), out_shape=[j...]
    unnamed x12 -> x14, local copies, waits for them, and re-layouts: 3.32 us -> 0.03 us
    ppermute x14, waiting for transfers between devices: 63.3 us -> 60.3 us  [permute(): return lax.ppermute(block, tuple(axes) if len(axes) > 1 else axes[0], pairs)]
    pallas_call x1 -> x2, Pallas kernels: 5.93 us -> 8.46 us  [head_terms(): pl.pallas_call(functools.partial(head_kernel, distances), out_shape=[jax....]
  transfers between devices with their start and end apart: 17 -> 17, of which waited for: 10 -> 11; matrix products, arithmetic and copies ran while one was open for 5% -> 5% of each run, Pallas kernels for 14% -> 16%
where the time goes in v4:
time: 199 us; the launch traced here: 198 us
  waiting for transfers between devices  86.5 us (43%)
  Pallas kernels  44.7 us (22%)
  starting transfers between devices  26.7 us (13%)
  between operations  15.1 us (8%)
  blocking collectives  13.5 us (7%)
  local copies, waits for them, and re-layouts  6.79 us (3%)
  matrix products  3.09 us (2%)
    ppermute x14, waiting for transfers between devices, permute(): return lax.ppermute(block, tuple(axes) if len(axes) > 1 else axes[0], pairs)  60.3 us
    pallas_call x2, Pallas kernels, unit_terms(): pl.pallas_call(functools.partial(units_kernel, len(tokens)), out_shape=[j...  17.1 us
    ppermute x14, starting transfers between devices, permute(): return lax.ppermute(block, tuple(axes) if len(axes) > 1 else axes[0], pairs)  16.6 us
    all_gather x1, waiting for transfers between devices, block(): half = lax.all_gather(jnp.stack([mine, mine_x]), 'z', axis=0)  14.6 us
    all_to_all x1, blocking collectives, block(): before = lax.all_to_all(ahead, ('xl', 'z'), 0, 0).reshape(STATE_ROWS, SHARE)  13.5 us
    all_to_all x1, starting transfers between devices, block(): slices = lax.all_to_all(packed.reshape(16, -1, SHARE), ('xl', 'z'), 0, 0)  10 us
    pallas_call x2, Pallas kernels, head_terms(): pl.pallas_call(functools.partial(head_kernel, distances), out_shape=[jax....  8.46 us
    all_to_all x1, waiting for transfers between devices, block(): slices = lax.all_to_all(packed.reshape(16, -1, SHARE), ('xl', 'z'), 0, 0)  7.04 us
  transfers between devices with their start and end apart: 17, of which 11 were waited for; matrix products, arithmetic and copies ran while one was open for 5% of the time, Pallas kernels for 16%

profile of v4, /device:TPU:1, one launch (start us, length us, event | category | flops | bytes accessed | tf_op | source)
XLA Modules:
  0.0 198.1 jit_solution(11125891244279182289)
XLA Ops:
  9.0 2.7 %shard_map.122 = (f32[5,512]{1,0:T(8,128)}, bf16[640,128]{1,0:T(8,128)(2,1)}) custom-call(bf16[560,512]{1,0:T(8,128)(2,1)} %bitcast.59, bf16[560,512]{1,0:T(8,128)(2,1)} %bitcast.61, f32[5,512]{1,0:T(8,128)} %decay_ref.1), custom_call_target="tpu_custom_call" | custom-call | flops 1000000000 | bytes 3000000 | tf_op jit(solution)/shard_map/pallas_call | solution.py:123
  11.6 10.0 %all-to-all-start = ((bf16[16,40,128]{2,1,0:T(8,128)(2,1)}), bf16[16,40,128]{2,1,0:T(8,128)(2,1)S(1)}, u32[]{:S(2)}, u32[]{:S(2)}) async-start(bf16[16,40,128]{2,1,0:T(8,128)(2,1)} %bitcast.57), calls=%async_computation | async-start | bytes 327680 | tf_op jit(solution)/shard_map/all_to_all | solution.py:387
  22.1 7.0 %all-to-all-done.blocks_ref = bf16[16,40,128]{2,1,0:T(8,128)(2,1)S(1)} async-done(((bf16[16,40,128]{2,1,0:T(8,128)(2,1)}), bf16[16,40,128]{2,1,0:T(8,128)(2,1)S(1)}, u32[]{:S(2)}, u32[]{:S(2)}) %all-to-all-start) | async-done | bytes 163872 | tf_op jit(solution)/shard_map/all_to_all | solution.py:387
  29.9 1.6 shard_map.124
  31.5 13.5 %all_to_all.10 = bf16[16,40,128]{2,1,0:T(8,128)(2,1)S(1)} all-to-all(bf16[16,40,128]{2,1,0:T(8,128)(2,1)} %shard_map.124), channel_id=1, replica_groups=mesh['xh'=2,'c'=2,'xl'=2,'z'=8,'y'=4] {'xl','z'}, dimensions={0} | all-to-all | bytes 327680 | tf_op jit(solution)/shard_map/all_to_all | solution.py:391
  45.9 4.7 %all-gather.4.cloned.1.call-done.own_ref = bf16[8,144,560]{2,1,0:T(8,128)(2,1)} async-done(((bf16[1,144,560]{2,1,0:T(8,128)(2,1)}), bf16[8,144,560]{2,1,0:T(8,128)(2,1)}) %all-gather.4.cloned.1.call-update) | async-done | bytes 1290256 | tf_op jit(solution)/shard_map/all_gather | solution.py:382
  50.6 1.5 fusion.6
  52.0 2.8 %collective-permute-start.1 = (bf16[4,144,560]{2,1,0:T(8,128)(2,1)S(1)}, bf16[4,144,560]{2,1,0:T(8,128)(2,1)S(1)}, u32[]{:S(2)}, u32[]{:S(2)}) collective-permute-start(bf16[4,144,560]{2,1,0:T(8,128)(2,1)S(1)} %get-tuple-element.42), channel_id=1, source_target_pairs={{0,160},{32,0},{128,32},{160,128},{1,161},{33,1},{129,33},{161,129... | collective-permute-start | bytes 1935368 | tf_op jit(solution)/shard_map/ppermute | solution.py:38
  55.5 4.9 %shard_map.123.inner_ref = f32[560,512]{1,0:T(8,128)} custom-call(bf16[560,512]{1,0:T(8,128)(2,1)} %bitcast.51, bf16[560,512]{1,0:T(8,128)(2,1)} %bitcast.60, bf16[560,512]{1,0:T(8,128)(2,1)} %bitcast.62, f32[5,512]{1,0:T(8,128)} %get-tuple-element.22.cumulative_ref, s32[1,512]{1,0:T(1,128)} %bitcast.65), custom_call_target="tpu_custom_call" | custom-call | flops 5000000000 | bytes 4000000 | tf_op jit(solution)/shard_map/pallas_call | solution.py:172
  60.4 2.6 %shard_map.125.mixed_ref = bf16[560,512]{1,0:T(8,128)(2,1)} custom-call(bf16[560,512]{1,0:T(8,128)(2,1)} %bitcast.52, f32[560,512]{1,0:T(8,128)} %shard_map.123.inner_ref, f32[5,512]{1,0:T(8,128)} %get-tuple-element.22.cumulative_ref, bf16[640,128]{1,0:T(8,128)(2,1)S(1)} %bitcast.38), custom_call_target="tpu_custom_call" | custom-call | flops 100000000 | bytes 4000000 | tf_op jit(solution)/shard_map/pallas_call | solution.py:195
  63.1 2.9 %collective-permute-done.1.second_ref = bf16[4,144,560]{2,1,0:T(8,128)(2,1)S(1)} collective-permute-done((bf16[4,144,560]{2,1,0:T(8,128)(2,1)S(1)}, bf16[4,144,560]{2,1,0:T(8,128)(2,1)S(1)}, u32[]{:S(2)}, u32[]{:S(2)}) %collective-permute-start.1) | collective-permute-done | bytes 645152 | tf_op jit(solution)/shard_map/ppermute | solution.py:38
  66.0 3.1 %collective-permute-done.first_ref = bf16[4,144,560]{2,1,0:T(8,128)(2,1)S(1)} collective-permute-done((bf16[4,144,560]{2,1,0:T(8,128)(2,1)S(1)}, bf16[4,144,560]{2,1,0:T(8,128)(2,1)S(1)}, u32[]{:S(2)}, u32[]{:S(2)}) %collective-permute-start) | collective-permute-done | bytes 645152 | tf_op jit(solution)/shard_map/ppermute | solution.py:38
  69.1 4.2 %shard_map.126 = (bf16[2304,128]{1,0:T(8,128)(2,1)}, bf16[2304,128]{1,0:T(8,128)(2,1)}) custom-call(s32[3]{0:T(128)} %pad_add_fusion.place_ref, bf16[560,512]{1,0:T(8,128)(2,1)} %shard_map.125.mixed_ref, bf16[8,144,560]{2,1,0:T(8,128)(2,1)} %all-gather.4.cloned.1.call-done.own_ref, bf16[4,144,560]{2,1,0:T(8,128)(2,1)S(1)} %collective-permute-done.first_ref, ...), custom_call_target="tpu_custom_call" | custom-call | flops 1000000000 | bytes 4000000 | tf_op jit(solution)/shard_map/pallas_call | solution.py:219
  73.3 4.2 %shard_map.127 = (bf16[2304,128]{1,0:T(8,128)(2,1)}, bf16[2304,128]{1,0:T(8,128)(2,1)}) custom-call(s32[3]{0:T(128)} %pad_add_fusion.place_ref, bf16[560,512]{1,0:T(8,128)(2,1)} %shard_map.125.mixed_ref, bf16[8,144,560]{2,1,0:T(8,128)(2,1)} %all-gather.4.cloned.1.call-done.own_ref, bf16[4,144,560]{2,1,0:T(8,128)(2,1)S(1)} %collective-permute-done.first_ref, ...), custom_call_target="tpu_custom_call" | custom-call | flops 1000000000 | bytes 4000000 | tf_op jit(solution)/shard_map/pallas_call | solution.py:219
  77.6 2.5 %collective-permute-start.4 = (bf16[2304,128]{1,0:T(8,128)(2,1)}, bf16[2304,128]{1,0:T(8,128)(2,1)S(1)}, u32[]{:S(2)}, u32[]{:S(2)}) collective-permute-start(bf16[2304,128]{1,0:T(8,128)(2,1)} %get-tuple-element.27), channel_id=1, source_target_pairs={{0,3},{1,0},{2,1},{3,2},{4,7},{5,4},{6,5},{7,6},{8,11},{9,8},{10,9... | collective-permute-start | bytes 1769480 | tf_op jit(solution)/shard_map/ppermute | solution.py:38
  80.1 2.1 %collective-permute-start.2 = (bf16[2304,128]{1,0:T(8,128)(2,1)}, bf16[2304,128]{1,0:T(8,128)(2,1)}, u32[]{:S(2)}, u32[]{:S(2)}) collective-permute-start(bf16[2304,128]{1,0:T(8,128)(2,1)} %get-tuple-element.24), channel_id=1, source_target_pairs={{0,2},{1,3},{2,0},{3,1},{4,6},{5,7},{6,4},{7,5},{8,10},{9,11},{10,... | collective-permute-start | bytes 1769480 | tf_op jit(solution)/shard_map/ppermute | solution.py:38
  83.0 3.1 %convolution_reduce_fusion = f32[8960]{0:T(1024)S(1)} fusion(bf16[256,1]{0,1:T(2,128)(2,1)S(1)} %reshape.105, bf16[256,8960]{1,0:T(8,128)(2,1)} %param.18), kind=kOutput, calls=%fused_computation | convolution fusion | flops 4587520 | bytes 4623872 | tf_op jit(solution)/shard_map/dot_general | solution.py:75
  86.6 1.5 copy.14
  88.1 1.4 pad.21.vector_ref
  89.4 2.2 %collective-permute-done.3 = bf16[2304,128]{1,0:T(8,128)(2,1)S(1)} collective-permute-done((bf16[2304,128]{1,0:T(8,128)(2,1)}, bf16[2304,128]{1,0:T(8,128)(2,1)S(1)}, u32[]{:S(2)}, u32[]{:S(2)}) %collective-permute-start.3) | collective-permute-done | bytes 589856 | tf_op jit(solution)/shard_map/ppermute | solution.py:38
  91.6 10.7 %collective-permute-done.2 = bf16[2304,128]{1,0:T(8,128)(2,1)} collective-permute-done((bf16[2304,128]{1,0:T(8,128)(2,1)}, bf16[2304,128]{1,0:T(8,128)(2,1)}, u32[]{:S(2)}, u32[]{:S(2)}) %collective-permute-start.2) | collective-permute-done | bytes 589856 | tf_op jit(solution)/shard_map/ppermute | solution.py:38
  102.3 3.6 %shard_map.128 = (f32[32,72,128]{2,1,0:T(8,128)}, bf16[128,2304]{1,0:T(8,128)(2,1)}) custom-call(s32[3]{0:T(128)} %pad_add_fusion.place_ref, bf16[32,72,128]{2,1,0:T(8,128)(2,1)} %bitcast.11.t0, bf16[32,72,128]{2,1,0:T(8,128)(2,1)S(1)} %bitcast.40, bf16[32,72,128]{2,1,0:T(8,128)(2,1)S(1)} %bitcast.39, bf16[32,72,128]{2,1,0:T(8,128)(2,1)} %bitcast.49, ...), custom_call_target="tpu_custom_call" | custom-call | flops 10000000 | bytes 8000000 | tf_op jit(solution)/shard_map/pallas_call | solution.py:268
  105.9 14.6 %all-gather.6.cloned.1.call-done = bf16[16,2,72,1120]{3,2,1,0:T(8,128)(2,1)} async-done(((bf16[2,2,72,1120]{3,2,1,0:T(8,128)(2,1)}), bf16[16,2,72,1120]{3,2,1,0:T(8,128)(2,1)}) %all-gather.6.cloned.1.call-update) | async-done | bytes 5160976 | tf_op jit(solution)/shard_map/all_gather | solution.py:393
  122.5 1.5 collective-permute-start.5
  124.0 13.6 %collective-permute-done.6.refs_1_ = bf16[128,2304]{1,0:T(8,128)(2,1)S(1)} collective-permute-done((bf16[128,2304]{1,0:T(8,128)(2,1)}, bf16[128,2304]{1,0:T(8,128)(2,1)S(1)}, u32[]{:S(2)}, u32[]{:S(2)}) %collective-permute-start.6) | collective-permute-done | bytes 589856 | tf_op jit(solution)/shard_map/ppermute | solution.py:38
  137.8 2.9 %collective-permute-start.11 = (bf16[64,2304]{1,0:T(8,128)(2,1)S(1)}, bf16[64,2304]{1,0:T(8,128)(2,1)S(1)}, u32[]{:S(2)}, u32[]{:S(2)}) collective-permute-start(bf16[64,2304]{1,0:T(8,128)(2,1)S(1)} %slice.28), channel_id=1, source_target_pairs={{0,3},{1,0},{2,1},{3,2},{4,7},{5,4},{6,5},{7,6},{8,11},{9,8},{10,9... | collective-permute-start | bytes 884744 | tf_op jit(solution)/shard_map/ppermute | solution.py:38
  140.7 8.0 %shard_map.129 = (bf16[2304,128]{1,0:T(8,128)(2,1)}, bf16[2304,128]{1,0:T(8,128)(2,1)}) custom-call(bf16[128,2304]{1,0:T(8,128)(2,1)S(1)} %collective-permute-done.5.refs_0_, bf16[128,2304]{1,0:T(8,128)(2,1)S(1)} %collective-permute-done.6.refs_1_, bf16[8,2,2,72,1120]{4,3,2,1,0:T(8,128)(2,1)} %bitcast.45, ...), custom_call_target="tpu_custom_call" | custom-call | flops 2642411520 | bytes 10321920 | tf_op jit(solution)/shard_map/pallas_call | solution.py:356
  148.7 9.1 %shard_map.130 = (bf16[2304,128]{1,0:T(8,128)(2,1)}, bf16[2304,128]{1,0:T(8,128)(2,1)}) custom-call(bf16[128,2304]{1,0:T(8,128)(2,1)} %get-tuple-element.36.refs_0_, bf16[64,2304]{1,0:T(8,128)(2,1)S(1)} %collective-permute-done.11.refs_1_, bf16[64,2304]{1,0:T(8,128)(2,1)S(1)} %collective-permute-done.12.refs_2_, bf16[8,2,2,72,1120]{4,3,2,1,0:T(8,128)(2,1)} %bitcast.46, ...), custom_call_target="tpu_custom_call" | custom-call | flops 2642411520 | bytes 10321920 | tf_op jit(solution)/shard_map/pallas_call | solution.py:356
  159.8 13.4 %collective-permute-done.13 = bf16[2304,128]{1,0:T(8,128)(2,1)S(1)} collective-permute-done((bf16[2304,128]{1,0:T(8,128)(2,1)}, bf16[2304,128]{1,0:T(8,128)(2,1)S(1)}, u32[]{:S(2)}, u32[]{:S(2)}) %collective-permute-start.13) | collective-permute-done | bytes 589856 | tf_op jit(solution)/shard_map/ppermute | solution.py:38
  173.2 11.5 %collective-permute-done.10 = bf16[2304,128]{1,0:T(8,128)(2,1)S(1)} collective-permute-done((bf16[2304,128]{1,0:T(8,128)(2,1)S(1)}, bf16[2304,128]{1,0:T(8,128)(2,1)S(1)}, u32[]{:S(2)}, u32[]{:S(2)}) %collective-permute-start.10) | collective-permute-done | bytes 589856 | tf_op jit(solution)/shard_map/ppermute | solution.py:38
  184.7 2.9 %collective-permute-done.9 = bf16[2304,128]{1,0:T(8,128)(2,1)S(1)} collective-permute-done((bf16[2304,128]{1,0:T(8,128)(2,1)S(1)}, bf16[2304,128]{1,0:T(8,128)(2,1)S(1)}, u32[]{:S(2)}, u32[]{:S(2)}) %collective-permute-start.9) | collective-permute-done | bytes 589856 | tf_op jit(solution)/shard_map/ppermute | solution.py:38
  187.6 3.7 %shard_map.131 = (bf16[2240,128]{1,0:T(8,128)(2,1)}, bf16[2240,128]{1,0:T(8,128)(2,1)}) custom-call(s32[3]{0:T(128)} %pad_add_fusion.place_ref, f32[1]{0:T(128)S(6)} %sub.13.step_ref, bf16[32,72,128]{2,1,0:T(8,128)(2,1)S(1)} %bitcast.43, bf16[32,72,128]{2,1,0:T(8,128)(2,1)S(1)} %bitcast.42, bf16[32,72,128]{2,1,0:T(8,128)(2,1)S(1)} %bitcast.41, ...), custom_call_target="tpu_custom_call" | custom-call | flops 10000000 | bytes 8000000 | tf_op jit(solution)/shard_map/pallas_call | solution.py:301
  (50 shorter events, 9.0 us)
Async XLA Ops:
  7.2 14.6 %copy-start.3 = (bf16[140,1120]{1,0:T(8,128)(2,1)S(1)}, bf16[140,1120]{1,0:T(8,128)(2,1)}, u32[]{:S(2)}) copy-start(bf16[140,1120]{1,0:T(8,128)(2,1)} %param.20) | copy-start | bytes 940804
  7.2 14.7 %copy-start.4 = (bf16[1120,140]{0,1:T(8,128)(2,1)S(1)}, bf16[1120,140]{0,1:T(8,128)(2,1)}, u32[]{:S(2)}) copy-start(bf16[1120,140]{0,1:T(8,128)(2,1)} %param.21) | copy-start | bytes 940804
  7.2 43.4 %all-gather.4.cloned.1.call-start = ((), (), s32[]{:S(2)}) async-start(), calls=%async_computation.2 | async-start | bytes 1658880 | tf_op jit(solution)/shard_map/all_gather | solution.py:382
  11.6 17.5 %all-to-all-start = ((bf16[16,40,128]{2,1,0:T(8,128)(2,1)}), bf16[16,40,128]{2,1,0:T(8,128)(2,1)S(1)}, u32[]{:S(2)}, u32[]{:S(2)}) async-start(bf16[16,40,128]{2,1,0:T(8,128)(2,1)} %bitcast.57), calls=%async_computation | async-start | bytes 327680 | tf_op jit(solution)/shard_map/all_to_all | solution.py:387
  21.7 98.8 %all-gather.6.cloned.1.call-start = ((), (), s32[]{:S(2)}) async-start(), calls=%async_computation.3 | async-start | bytes 5971968 | tf_op jit(solution)/shard_map/all_gather | solution.py:393
  29.1 15.8 %collective-permute-start.7 = (bf16[2,72,1120]{2,1,0:T(8,128)(2,1)S(1)}, bf16[2,72,1120]{2,1,0:T(8,128)(2,1)S(1)}, u32[]{:S(2)}, u32[]{:S(2)}) collective-permute-start(bf16[2,72,1120]{2,1,0:T(8,128)(2,1)S(1)} %fusion.2), channel_id=1, source_target_pairs={{0,32},{32,128},{128,160},{160,0},{1,33},{33,129},{129,161},{161,1... | collective-permute-start | bytes 967688 | tf_op jit(solution)/shard_map/ppermute | solution.py:38
  52.0 13.9 %collective-permute-start.1 = (bf16[4,144,560]{2,1,0:T(8,128)(2,1)S(1)}, bf16[4,144,560]{2,1,0:T(8,128)(2,1)S(1)}, u32[]{:S(2)}, u32[]{:S(2)}) collective-permute-start(bf16[4,144,560]{2,1,0:T(8,128)(2,1)S(1)} %get-tuple-element.42), channel_id=1, source_target_pairs={{0,160},{32,0},{128,32},{160,128},{1,161},{33,1},{129,33},{161,129... | collective-permute-start | bytes 1935368 | tf_op jit(solution)/shard_map/ppermute | solution.py:38
  54.9 14.2 %collective-permute-start = (bf16[4,144,560]{2,1,0:T(8,128)(2,1)S(1)}, bf16[4,144,560]{2,1,0:T(8,128)(2,1)S(1)}, u32[]{:S(2)}, u32[]{:S(2)}) collective-permute-start(bf16[4,144,560]{2,1,0:T(8,128)(2,1)S(1)} %get-tuple-element.43), channel_id=1, source_target_pairs={{0,32},{32,128},{128,160},{160,0},{1,33},{33,129},{129,161},{161,1... | collective-permute-start | bytes 1935368 | tf_op jit(solution)/shard_map/ppermute | solution.py:38
  73.3 13.0 %copy-start.2 = (bf16[128,2240]{0,1:T(8,128)(2,1)S(1)}, bf16[128,2240]{0,1:T(8,128)(2,1)}, u32[]{:S(2)}) copy-start(bf16[128,2240]{0,1:T(8,128)(2,1)} %param.11) | copy-start | bytes 1720324
  77.6 11.9 %collective-permute-start.4 = (bf16[2304,128]{1,0:T(8,128)(2,1)}, bf16[2304,128]{1,0:T(8,128)(2,1)S(1)}, u32[]{:S(2)}, u32[]{:S(2)}) collective-permute-start(bf16[2304,128]{1,0:T(8,128)(2,1)} %get-tuple-element.27), channel_id=1, source_target_pairs={{0,3},{1,0},{2,1},{3,2},{4,7},{5,4},{6,5},{7,6},{8,11},{9,8},{10,9... | collective-permute-start | bytes 1769480 | tf_op jit(solution)/shard_map/ppermute | solution.py:38
  80.1 11.5 %collective-permute-start.3 = (bf16[2304,128]{1,0:T(8,128)(2,1)}, bf16[2304,128]{1,0:T(8,128)(2,1)S(1)}, u32[]{:S(2)}, u32[]{:S(2)}) collective-permute-start(bf16[2304,128]{1,0:T(8,128)(2,1)} %get-tuple-element.25), channel_id=1, source_target_pairs={{0,1},{1,2},{2,3},{3,0},{4,5},{5,6},{6,7},{7,4},{8,9},{9,10},{10,1... | collective-permute-start | bytes 1769480 | tf_op jit(solution)/shard_map/ppermute | solution.py:38
  80.1 22.2 %collective-permute-start.2 = (bf16[2304,128]{1,0:T(8,128)(2,1)}, bf16[2304,128]{1,0:T(8,128)(2,1)}, u32[]{:S(2)}, u32[]{:S(2)}) collective-permute-start(bf16[2304,128]{1,0:T(8,128)(2,1)} %get-tuple-element.24), channel_id=1, source_target_pairs={{0,2},{1,3},{2,0},{3,1},{4,6},{5,7},{6,4},{7,5},{8,10},{9,11},{10,... | collective-permute-start | bytes 1769480 | tf_op jit(solution)/shard_map/ppermute | solution.py:38
  86.5 62.1 %copy-start.1 = (bf16[32,72,128]{2,1,0:T(8,128)(2,1)}, bf16[32,72,128]{2,1,0:T(8,128)(2,1)S(1)}, u32[]{:S(2)}) copy-start(bf16[32,72,128]{2,1,0:T(8,128)(2,1)S(1)} %pad.20.latent_ref) | copy-start | bytes 1769476
  89.4 59.3 %copy-start = (f32[32,72,4]{2,1,0:T(8,128)}, f32[32,72,4]{2,1,0:T(8,128)S(1)}, u32[]{:S(2)}) copy-start(f32[32,72,4]{2,1,0:T(8,128)S(1)} %pad.21.vector_ref) | copy-start | bytes 110596
  120.5 20.3 %collective-permute-start.8 = (bf16[8,2,2,72,1120]{4,3,2,1,0:T(8,128)(2,1)}, bf16[8,2,2,72,1120]{4,3,2,1,0:T(8,128)(2,1)S(1)}, u32[]{:S(2)}, u32[]{:S(2)}) collective-permute-start(bf16[8,2,2,72,1120]{4,3,2,1,0:T(8,128)(2,1)} %bitcast.44), channel_id=1, source_target_pairs={{0,64},{64,0},{1,65},{65,1},{2,66},{66,2},{3,67},{67,3},{4,68},{68... | collective-permute-start | bytes 15482888 | tf_op jit(solution)/shard_map/ppermute | solution.py:38
  121.3 16.3 %collective-permute-start.6 = (bf16[128,2304]{1,0:T(8,128)(2,1)}, bf16[128,2304]{1,0:T(8,128)(2,1)S(1)}, u32[]{:S(2)}, u32[]{:S(2)}) collective-permute-start(bf16[128,2304]{1,0:T(8,128)(2,1)} %get-tuple-element.36.refs_0_), channel_id=1, source_target_pairs={{0,1},{1,2},{2,3},{3,0},{4,5},{5,6},{6,7},{7,4},{8,9},{9,10},{10,1... | collective-permute-start | bytes 1769480 | tf_op jit(solution)/shard_map/ppermute | solution.py:38
  122.5 15.2 %collective-permute-start.5 = (bf16[128,2304]{1,0:T(8,128)(2,1)}, bf16[128,2304]{1,0:T(8,128)(2,1)S(1)}, u32[]{:S(2)}, u32[]{:S(2)}) collective-permute-start(bf16[128,2304]{1,0:T(8,128)(2,1)} %get-tuple-element.36.refs_0_), channel_id=1, source_target_pairs={{0,3},{1,0},{2,1},{3,2},{4,7},{5,4},{6,5},{7,6},{8,11},{9,8},{10,9... | collective-permute-start | bytes 1769480 | tf_op jit(solution)/shard_map/ppermute | solution.py:38
  137.6 11.1 %collective-permute-start.12 = (bf16[64,2304]{1,0:T(8,128)(2,1)S(1)}, bf16[64,2304]{1,0:T(8,128)(2,1)S(1)}, u32[]{:S(2)}, u32[]{:S(2)}) collective-permute-start(bf16[64,2304]{1,0:T(8,128)(2,1)S(1)} %slice.29), channel_id=1, source_target_pairs={{0,1},{1,2},{2,3},{3,0},{4,5},{5,6},{6,7},{7,4},{8,9},{9,10},{10,1... | collective-permute-start | bytes 884744 | tf_op jit(solution)/shard_map/ppermute | solution.py:38
  137.8 11.0 %collective-permute-start.11 = (bf16[64,2304]{1,0:T(8,128)(2,1)S(1)}, bf16[64,2304]{1,0:T(8,128)(2,1)S(1)}, u32[]{:S(2)}, u32[]{:S(2)}) collective-permute-start(bf16[64,2304]{1,0:T(8,128)(2,1)S(1)} %slice.28), channel_id=1, source_target_pairs={{0,3},{1,0},{2,1},{3,2},{4,7},{5,4},{6,5},{7,6},{8,11},{9,8},{10,9... | collective-permute-start | bytes 884744 | tf_op jit(solution)/shard_map/ppermute | solution.py:38
  148.7 9.6 %copy-start.6 = (bf16[2304,128]{1,0:T(8,128)(2,1)S(1)}, bf16[2304,128]{1,0:T(8,128)(2,1)}, u32[]{:S(2)}) copy-start(bf16[2304,128]{1,0:T(8,128)(2,1)} %get-tuple-element.35) | copy-start | bytes 1769476
  148.7 10.4 %copy-start.5 = (bf16[2304,128]{1,0:T(8,128)(2,1)S(1)}, bf16[2304,128]{1,0:T(8,128)(2,1)}, u32[]{:S(2)}) copy-start(bf16[2304,128]{1,0:T(8,128)(2,1)} %get-tuple-element.34) | copy-start | bytes 1769476
  157.9 15.3 %collective-permute-start.13 = (bf16[2304,128]{1,0:T(8,128)(2,1)}, bf16[2304,128]{1,0:T(8,128)(2,1)S(1)}, u32[]{:S(2)}, u32[]{:S(2)}) collective-permute-start(bf16[2304,128]{1,0:T(8,128)(2,1)} %get-tuple-element.37), channel_id=1, source_target_pairs={{0,2},{1,3},{2,0},{3,1},{4,6},{5,7},{6,4},{7,5},{8,10},{9,11},{10,... | collective-permute-start | bytes 1769480 | tf_op jit(solution)/shard_map/ppermute | solution.py:38
  158.3 26.4 %collective-permute-start.10 = (bf16[2304,128]{1,0:T(8,128)(2,1)S(1)}, bf16[2304,128]{1,0:T(8,128)(2,1)S(1)}, u32[]{:S(2)}, u32[]{:S(2)}) collective-permute-start(bf16[2304,128]{1,0:T(8,128)(2,1)S(1)} %copy-done.6), channel_id=1, source_target_pairs={{0,3},{1,0},{2,1},{3,2},{4,7},{5,4},{6,5},{7,6},{8,11},{9,8},{10,9... | collective-permute-start | bytes 1769480 | tf_op jit(solution)/shard_map/ppermute | solution.py:38
  159.2 28.4 %collective-permute-start.9 = (bf16[2304,128]{1,0:T(8,128)(2,1)S(1)}, bf16[2304,128]{1,0:T(8,128)(2,1)S(1)}, u32[]{:S(2)}, u32[]{:S(2)}) collective-permute-start(bf16[2304,128]{1,0:T(8,128)(2,1)S(1)} %copy-done.5), channel_id=1, source_target_pairs={{0,1},{1,2},{2,3},{3,0},{4,5},{5,6},{6,7},{7,4},{8,9},{9,10},{10,1... | collective-permute-start | bytes 1769480 | tf_op jit(solution)/shard_map/ppermute | solution.py:38
Sparse Core Ops, SparseCore 0:
  10.4 40.1 all-gather.3
  52.4 68.0 all-gather.5

commit v5 on v4

--- a/solution.py
+++ b/solution.py
@@ -312,20 +312,47 @@
 HALF = ROWS // 2
 
 
-def units_kernel(pieces, *refs):
-    token_refs = refs[:pieces]
+def stacked(token_refs, tokens):
+    row = 0
+    for token_ref in token_refs:
+        tokens[row : row + token_ref.shape[0], :] = token_ref[...]
+        row += token_ref.shape[0]
+
+
+def up_kernel(pieces, *refs):
+    own_ref, out_ref, tokens = refs[pieces:]
+    stacked(refs[:pieces], tokens)
+    weight = own_ref[...].reshape(HALF, -1)
+    out_ref[...] = jnp.dot(tokens[:, 0:HALF], weight, preferred_element_type=F32)
+
+
+def own_sums(tokens, own):
+    rows = sum(t.shape[0] for t in tokens)
+    hidden_units = own.shape[4]
+    block = (8, 2, 1, PADDED, hidden_units)
+    return pl.pallas_call(
+        functools.partial(up_kernel, len(tokens)),
+        grid=(1,),
+        out_shape=jax.ShapeDtypeStruct((rows, hidden_units), F32),
+        in_specs=[pl.BlockSpec(t.shape, lambda i: (0, 0)) for t in tokens]
+        + [pl.BlockSpec(block, lambda i: (0, 0, 0, 0, 0))],
+        out_specs=pl.BlockSpec((rows, hidden_units), lambda i: (0, 0)),
+        scratch_shapes=[pltpu.VMEM((rows, ROWS), BF)],
+        cost_estimate=cost(rows * ROWS * hidden_units, ROWS * hidden_units),
+        compiler_params=SMALL,
+    )(*tokens, own)
+
+
+def units_kernel(pieces, with_sums, *refs):
     own_ref, other_ref = refs[pieces : pieces + 2]
-    out_refs = refs[pieces + 2 : -4]
+    out_refs = refs[pieces + 2 + with_sums : -4]
     tokens, units, own, arrived_sems = refs[-4:]
     copies = [
         pltpu.make_async_copy(own_ref.at[:, :, w], own.at[w], arrived_sems.at[w]) for w in range(2)
     ]
-    for copy in copies:
+    for copy in copies[with_sums:]:
         copy.start()
-    row = 0
-    for token_ref in token_refs:
-        tokens[row : row + token_ref.shape[0], :] = token_ref[...]
-        row += token_ref.shape[0]
+    stacked(refs[:pieces], tokens)
 
     def up(weight, first):
         weight = weight.reshape(HALF, -1)
@@ -342,21 +369,26 @@
             out_ref[first : first + HALF, :] = feed[:, SHARE * n : SHARE * (n + 1)]
 
     sums = up(other_ref[:, :, 0], HALF)
-    copies[0].wait()
-    sums = sums + up(own[0], 0)
+    if with_sums:
+        sums = sums + refs[pieces + 2][...]
+    else:
+        copies[0].wait()
+        sums = sums + up(own[0], 0)
     units[...] = jax.nn.gelu(sums, approximate=True).astype(BF)
     down(other_ref[:, :, 1], HALF)
     copies[1].wait()
     down(own[1], 0)
 
 
-def unit_terms(tokens, own, other):
+def unit_terms(tokens, own, other, sums=()):
     chunks = sum(t.shape[0] for t in tokens) // SHARE
     hidden_units = own.shape[4]
     return pl.pallas_call(
-        functools.partial(units_kernel, len(tokens)),
+        functools.partial(units_kernel, len(tokens), len(sums)),
         out_shape=[jax.ShapeDtypeStruct((ROWS, SHARE), BF)] * chunks,
-        in_specs=[VMEM] * len(tokens) + [pl.BlockSpec(memory_space=pltpu.HBM), VMEM],
+        in_specs=[VMEM] * len(tokens)
+        + [pl.BlockSpec(memory_space=pltpu.HBM), VMEM]
+        + [VMEM] * len(sums),
         out_specs=[VMEM] * chunks,
         scratch_shapes=[
             pltpu.VMEM((SHARE * chunks, ROWS), BF),
@@ -364,9 +396,9 @@
             pltpu.VMEM((2, 8, 2, PADDED, hidden_units), BF),
             pltpu.SemaphoreType.DMA((2,)),
         ],
-        compiler_params=pltpu.CompilerParams(vmem_limit_bytes=50 << 20),
+        compiler_params=pltpu.CompilerParams(vmem_limit_bytes=48 << 20),
         cost_estimate=cost(4 * SHARE * chunks * ROWS * hidden_units, 4 * ROWS * hidden_units),
-    )(*tokens, own, other)
+    )(*tokens, own, other, *sums)
 
 
 def block(
@@ -411,7 +443,8 @@
     far = [along_y(above[: SHARE // 2], -1), along_y(below[SHARE // 2 :], 1)]
     half, _ = lax.optimization_barrier((half, normed))
     weights = [half, in_vmem(other_core(half))]
-    near = unit_terms([in_vmem(above), in_vmem(below)], *weights)
+    sums = own_sums([above, below], half)
+    near = unit_terms([above, below], *weights, [sums])
     feeds = []
     for d, part in zip((1, 3), near):
         feeds.append(along_y(part, d))

time: 199 us -> 203 us (1.020)
  Pallas kernels: 44.7 us -> 49.3 us
  waiting for transfers between devices: 86.5 us -> 84.2 us
    ppermute x14, waiting for transfers between devices: 60.3 us -> 53.2 us  [permute(): return lax.ppermute(block, tuple(axes) if len(axes) > 1 else axes[0], pairs)]
    pallas_call x2 -> x3, Pallas kernels: 17.1 us -> 21.7 us  [the longest x2 17.5 us: unit_terms(): pl.pallas_call(functools.partial(units_kernel, len(tokens), len(sums)), o...]
    all_gather x1, waiting for transfers between devices: 14.6 us -> 18.5 us  [block(): half = lax.all_gather(jnp.stack([mine, mine_x]), 'z', axis=0)]
  transfers between devices with their start and end apart: 17 -> 17, of which waited for: 11 -> 9; matrix products, arithmetic and copies ran while one was open for 5% -> 4% of each run, Pallas kernels for 16% -> 22%
where the time goes in v5:
time: 203 us; the launch traced here: 202 us
  waiting for transfers between devices  84.2 us (41%)
  Pallas kernels  49.3 us (24%)
  starting transfers between devices  28.6 us (14%)
  between operations  15 us (7%)
  blocking collectives  13.2 us (7%)
  local copies, waits for them, and re-layouts  7.36 us (4%)
  matrix products  3.09 us (2%)
    ppermute x14, waiting for transfers between devices, permute(): return lax.ppermute(block, tuple(axes) if len(axes) > 1 else axes[0], pairs)  53.2 us
    all_gather x1, waiting for transfers between devices, block(): half = lax.all_gather(jnp.stack([mine, mine_x]), 'z', axis=0)  18.5 us
    ppermute x14, starting transfers between devices, permute(): return lax.ppermute(block, tuple(axes) if len(axes) > 1 else axes[0], pairs)  18.5 us
    pallas_call x2, Pallas kernels, unit_terms(): pl.pallas_call(functools.partial(units_kernel, len(tokens), len(sums)), o...  17.5 us
    all_to_all x1, blocking collectives, block(): before = lax.all_to_all(ahead, ('xl', 'z'), 0, 0).reshape(STATE_ROWS, SHARE)  13.2 us
    all_to_all x1, starting transfers between devices, block(): slices = lax.all_to_all(packed.reshape(16, -1, SHARE), ('xl', 'z'), 0, 0)  10 us
    pallas_call x2, Pallas kernels, head_terms(): pl.pallas_call(functools.partial(head_kernel, distances), out_shape=[jax....  8.38 us
    all_to_all x1, waiting for transfers between devices, block(): slices = lax.all_to_all(packed.reshape(16, -1, SHARE), ('xl', 'z'), 0, 0)  7.04 us
  transfers between devices with their start and end apart: 17, of which 9 were waited for; matrix products, arithmetic and copies ran while one was open for 4% of the time, Pallas kernels for 22%

profile of v5, /device:TPU:1, one launch (start us, length us, event | category | flops | bytes accessed | tf_op | source)
XLA Modules:
  0.0 202.5 jit_solution(14363022609794873517)
XLA Ops:
  7.2 1.0 reshape.80
  8.9 2.7 %shard_map.122 = (f32[5,512]{1,0:T(8,128)}, bf16[640,128]{1,0:T(8,128)(2,1)}) custom-call(bf16[560,512]{1,0:T(8,128)(2,1)} %bitcast.60, bf16[560,512]{1,0:T(8,128)(2,1)} %bitcast.62, f32[5,512]{1,0:T(8,128)} %decay_ref.1), custom_call_target="tpu_custom_call" | custom-call | flops 1000000000 | bytes 3000000 | tf_op jit(solution)/shard_map/pallas_call | solution.py:123
  11.7 10.0 %all-to-all-start = ((bf16[16,40,128]{2,1,0:T(8,128)(2,1)}), bf16[16,40,128]{2,1,0:T(8,128)(2,1)S(1)}, u32[]{:S(2)}, u32[]{:S(2)}) async-start(bf16[16,40,128]{2,1,0:T(8,128)(2,1)} %bitcast.58), calls=%async_computation | async-start | bytes 327680 | tf_op jit(solution)/shard_map/all_to_all | solution.py:419
  22.1 7.0 %all-to-all-done.blocks_ref = bf16[16,40,128]{2,1,0:T(8,128)(2,1)S(1)} async-done(((bf16[16,40,128]{2,1,0:T(8,128)(2,1)}), bf16[16,40,128]{2,1,0:T(8,128)(2,1)S(1)}, u32[]{:S(2)}, u32[]{:S(2)}) %all-to-all-start) | async-done | bytes 163872 | tf_op jit(solution)/shard_map/all_to_all | solution.py:419
  29.9 1.6 shard_map.124
  31.5 13.2 %all_to_all.10 = bf16[16,40,128]{2,1,0:T(8,128)(2,1)S(1)} all-to-all(bf16[16,40,128]{2,1,0:T(8,128)(2,1)} %shard_map.124), channel_id=1, replica_groups=mesh['xh'=2,'c'=2,'xl'=2,'z'=8,'y'=4] {'xl','z'}, dimensions={0} | all-to-all | bytes 327680 | tf_op jit(solution)/shard_map/all_to_all | solution.py:423
  45.7 5.4 %all-gather.4.cloned.1.call-done.own_ref = bf16[8,144,560]{2,1,0:T(8,128)(2,1)} async-done(((bf16[1,144,560]{2,1,0:T(8,128)(2,1)}), bf16[8,144,560]{2,1,0:T(8,128)(2,1)}) %all-gather.4.cloned.1.call-update) | async-done | bytes 1290256 | tf_op jit(solution)/shard_map/all_gather | solution.py:414
  51.1 1.5 fusion.6
  52.5 1.2 collective-permute-start
  53.7 1.6 collective-permute-start.1
  55.9 4.9 %shard_map.123.inner_ref = f32[560,512]{1,0:T(8,128)} custom-call(bf16[560,512]{1,0:T(8,128)(2,1)} %bitcast.52, bf16[560,512]{1,0:T(8,128)(2,1)} %bitcast.61, bf16[560,512]{1,0:T(8,128)(2,1)} %bitcast.63, f32[5,512]{1,0:T(8,128)} %get-tuple-element.22.cumulative_ref, s32[1,512]{1,0:T(1,128)} %bitcast.66), custom_call_target="tpu_custom_call" | custom-call | flops 5000000000 | bytes 4000000 | tf_op jit(solution)/shard_map/pallas_call | solution.py:172
  60.8 2.6 %shard_map.125.mixed_ref = bf16[560,512]{1,0:T(8,128)(2,1)} custom-call(bf16[560,512]{1,0:T(8,128)(2,1)} %bitcast.53, f32[560,512]{1,0:T(8,128)} %shard_map.123.inner_ref, f32[5,512]{1,0:T(8,128)} %get-tuple-element.22.cumulative_ref, bf16[640,128]{1,0:T(8,128)(2,1)S(1)} %bitcast.38), custom_call_target="tpu_custom_call" | custom-call | flops 100000000 | bytes 4000000 | tf_op jit(solution)/shard_map/pallas_call | solution.py:195
  63.4 3.4 %collective-permute-done.first_ref = bf16[4,144,560]{2,1,0:T(8,128)(2,1)S(1)} collective-permute-done((bf16[4,144,560]{2,1,0:T(8,128)(2,1)S(1)}, bf16[4,144,560]{2,1,0:T(8,128)(2,1)S(1)}, u32[]{:S(2)}, u32[]{:S(2)}) %collective-permute-start) | collective-permute-done | bytes 645152 | tf_op jit(solution)/shard_map/ppermute | solution.py:38
  66.8 4.2 %shard_map.126 = (bf16[2304,128]{1,0:T(8,128)(2,1)}, bf16[2304,128]{1,0:T(8,128)(2,1)}) custom-call(s32[3]{0:T(128)} %pad_add_fusion.place_ref, bf16[560,512]{1,0:T(8,128)(2,1)} %shard_map.125.mixed_ref, bf16[8,144,560]{2,1,0:T(8,128)(2,1)} %all-gather.4.cloned.1.call-done.own_ref, bf16[4,144,560]{2,1,0:T(8,128)(2,1)S(1)} %collective-permute-done.first_ref, ...), custom_call_target="tpu_custom_call" | custom-call | flops 1000000000 | bytes 4000000 | tf_op jit(solution)/shard_map/pallas_call | solution.py:219
  71.0 3.3 %collective-permute-start.2 = (bf16[2304,128]{1,0:T(8,128)(2,1)}, bf16[2304,128]{1,0:T(8,128)(2,1)S(1)}, u32[]{:S(2)}, u32[]{:S(2)}) collective-permute-start(bf16[2304,128]{1,0:T(8,128)(2,1)} %get-tuple-element.24), channel_id=1, source_target_pairs={{0,2},{1,3},{2,0},{3,1},{4,6},{5,7},{6,4},{7,5},{8,10},{9,11},{10,... | collective-permute-start | bytes 1769480 | tf_op jit(solution)/shard_map/ppermute | solution.py:38
  74.3 4.2 %shard_map.127 = (bf16[2304,128]{1,0:T(8,128)(2,1)}, bf16[2304,128]{1,0:T(8,128)(2,1)}) custom-call(s32[3]{0:T(128)} %pad_add_fusion.place_ref, bf16[560,512]{1,0:T(8,128)(2,1)} %shard_map.125.mixed_ref, bf16[8,144,560]{2,1,0:T(8,128)(2,1)} %all-gather.4.cloned.1.call-done.own_ref, bf16[4,144,560]{2,1,0:T(8,128)(2,1)S(1)} %collective-permute-done.first_ref, ...), custom_call_target="tpu_custom_call" | custom-call | flops 1000000000 | bytes 4000000 | tf_op jit(solution)/shard_map/pallas_call | solution.py:219
  80.7 3.1 %convolution_reduce_fusion = f32[8960]{0:T(1024)S(1)} fusion(bf16[256,1]{0,1:T(2,128)(2,1)S(1)} %reshape.105, bf16[256,8960]{1,0:T(8,128)(2,1)} %param.18), kind=kOutput, calls=%fused_computation | convolution fusion | flops 4587520 | bytes 4623872 | tf_op jit(solution)/shard_map/dot_general | solution.py:75
  84.1 1.5 copy.14
  85.8 1.2 copy-done.2
  87.1 10.8 %collective-permute-done.4 = bf16[2304,128]{1,0:T(8,128)(2,1)S(1)} collective-permute-done((bf16[2304,128]{1,0:T(8,128)(2,1)}, bf16[2304,128]{1,0:T(8,128)(2,1)S(1)}, u32[]{:S(2)}, u32[]{:S(2)}) %collective-permute-start.4) | collective-permute-done | bytes 589856 | tf_op jit(solution)/shard_map/ppermute | solution.py:38
  98.2 3.6 %shard_map.128 = (f32[32,72,128]{2,1,0:T(8,128)}, bf16[128,2304]{1,0:T(8,128)(2,1)}) custom-call(s32[3]{0:T(128)} %pad_add_fusion.place_ref, bf16[32,72,128]{2,1,0:T(8,128)(2,1)S(1)} %bitcast.39, bf16[32,72,128]{2,1,0:T(8,128)(2,1)} %bitcast.12.t1, bf16[32,72,128]{2,1,0:T(8,128)(2,1)S(1)} %bitcast.40, bf16[32,72,128]{2,1,0:T(8,128)(2,1)} %bitcast.50, ...), custom_call_target="tpu_custom_call" | custom-call | flops 10000000 | bytes 8000000 | tf_op jit(solution)/shard_map/pallas_call | solution.py:268
  101.9 18.5 %all-gather.6.cloned.1.call-done = bf16[16,2,72,1120]{3,2,1,0:T(8,128)(2,1)} async-done(((bf16[2,2,72,1120]{3,2,1,0:T(8,128)(2,1)}), bf16[16,2,72,1120]{3,2,1,0:T(8,128)(2,1)}) %all-gather.6.cloned.1.call-update) | async-done | bytes 5160976 | tf_op jit(solution)/shard_map/all_gather | solution.py:425
  121.2 2.5 %collective-permute-start.5 = (bf16[128,2304]{1,0:T(8,128)(2,1)}, bf16[128,2304]{1,0:T(8,128)(2,1)S(1)}, u32[]{:S(2)}, u32[]{:S(2)}) collective-permute-start(bf16[128,2304]{1,0:T(8,128)(2,1)} %get-tuple-element.36.refs_0_), channel_id=1, source_target_pairs={{0,3},{1,0},{2,1},{3,2},{4,7},{5,4},{6,5},{7,6},{8,11},{9,8},{10,9... | collective-permute-start | bytes 1769480 | tf_op jit(solution)/shard_map/ppermute | solution.py:38
  123.7 13.0 %collective-permute-done.5.refs_0_ = bf16[128,2304]{1,0:T(8,128)(2,1)S(1)} collective-permute-done((bf16[128,2304]{1,0:T(8,128)(2,1)}, bf16[128,2304]{1,0:T(8,128)(2,1)S(1)}, u32[]{:S(2)}, u32[]{:S(2)}) %collective-permute-start.5) | collective-permute-done | bytes 589856 | tf_op jit(solution)/shard_map/ppermute | solution.py:38
  136.7 3.4 %collective-permute-start.11 = (bf16[64,2304]{1,0:T(8,128)(2,1)S(1)}, bf16[64,2304]{1,0:T(8,128)(2,1)S(1)}, u32[]{:S(2)}, u32[]{:S(2)}) collective-permute-start(bf16[64,2304]{1,0:T(8,128)(2,1)S(1)} %slice.28), channel_id=1, source_target_pairs={{0,3},{1,0},{2,1},{3,2},{4,7},{5,4},{6,5},{7,6},{8,11},{9,8},{10,9... | collective-permute-start | bytes 884744 | tf_op jit(solution)/shard_map/ppermute | solution.py:38
  140.9 4.2 %shard_map.129.refs_4_ = f32[256,1120]{1,0:T(8,128)} custom-call(bf16[128,2304]{1,0:T(8,128)(2,1)} %copy-done.3, bf16[128,2304]{1,0:T(8,128)(2,1)} %copy-done.4, bf16[8,2,2,72,1120]{4,3,2,1,0:T(8,128)(2,1)} %bitcast.45), custom_call_target="tpu_custom_call" | custom-call | flops 660602880 | bytes 2580480 | tf_op jit(solution)/shard_map/pallas_call | solution.py:333
  145.2 8.4 %shard_map.130 = (bf16[2304,128]{1,0:T(8,128)(2,1)S(1)}, bf16[2304,128]{1,0:T(8,128)(2,1)}) custom-call(bf16[128,2304]{1,0:T(8,128)(2,1)} %copy-done.3, bf16[128,2304]{1,0:T(8,128)(2,1)} %copy-done.4, bf16[8,2,2,72,1120]{4,3,2,1,0:T(8,128)(2,1)} %bitcast.46, bf16[8,2,2,72,1120]{4,3,2,1,0:T(8,128)(2,1)S(1)} %collective-permute-done.8.refs_3_.refs_4_, ...), custom_call_target="tpu_custom_call" | custom-call | flops 2642411520 | bytes 10321920 | tf_op jit(solution)/shard_map/pallas_call | solution.py:386
  153.9 9.1 %shard_map.131 = (bf16[2304,128]{1,0:T(8,128)(2,1)}, bf16[2304,128]{1,0:T(8,128)(2,1)}) custom-call(bf16[128,2304]{1,0:T(8,128)(2,1)} %get-tuple-element.36.refs_0_, bf16[64,2304]{1,0:T(8,128)(2,1)S(1)} %collective-permute-done.11.refs_1_, bf16[64,2304]{1,0:T(8,128)(2,1)S(1)} %collective-permute-done.12.refs_2_, bf16[8,2,2,72,1120]{4,3,2,1,0:T(8,128)(2,1)} %bitcast.47, ...), custom_call_target="tpu_custom_call" | custom-call | flops 2642411520 | bytes 10321920 | tf_op jit(solution)/shard_map/pallas_call | solution.py:386
  163.0 3.2 %collective-permute-start.13 = (bf16[2304,128]{1,0:T(8,128)(2,1)}, bf16[2304,128]{1,0:T(8,128)(2,1)S(1)}, u32[]{:S(2)}, u32[]{:S(2)}) collective-permute-start(bf16[2304,128]{1,0:T(8,128)(2,1)} %get-tuple-element.37), channel_id=1, source_target_pairs={{0,2},{1,3},{2,0},{3,1},{4,6},{5,7},{6,4},{7,5},{8,10},{9,11},{10,... | collective-permute-start | bytes 1769480 | tf_op jit(solution)/shard_map/ppermute | solution.py:38
  166.3 15.4 %collective-permute-done.13 = bf16[2304,128]{1,0:T(8,128)(2,1)S(1)} collective-permute-done((bf16[2304,128]{1,0:T(8,128)(2,1)}, bf16[2304,128]{1,0:T(8,128)(2,1)S(1)}, u32[]{:S(2)}, u32[]{:S(2)}) %collective-permute-start.13) | collective-permute-done | bytes 589856 | tf_op jit(solution)/shard_map/ppermute | solution.py:38
  181.6 10.2 %collective-permute-done.10 = bf16[2304,128]{1,0:T(8,128)(2,1)S(1)} collective-permute-done((bf16[2304,128]{1,0:T(8,128)(2,1)S(1)}, bf16[2304,128]{1,0:T(8,128)(2,1)S(1)}, u32[]{:S(2)}, u32[]{:S(2)}) %collective-permute-start.10) | collective-permute-done | bytes 589856 | tf_op jit(solution)/shard_map/ppermute | solution.py:38
  191.9 3.7 %shard_map.132 = (bf16[2240,128]{1,0:T(8,128)(2,1)}, bf16[2240,128]{1,0:T(8,128)(2,1)}) custom-call(s32[3]{0:T(128)} %pad_add_fusion.place_ref, f32[1]{0:T(128)S(6)} %sub.13.step_ref, bf16[32,72,128]{2,1,0:T(8,128)(2,1)S(1)} %bitcast.41, bf16[32,72,128]{2,1,0:T(8,128)(2,1)S(1)} %bitcast.43, bf16[32,72,128]{2,1,0:T(8,128)(2,1)S(1)} %bitcast.42, ...), custom_call_target="tpu_custom_call" | custom-call | flops 10000000 | bytes 8000000 | tf_op jit(solution)/shard_map/pallas_call | solution.py:301
  (57 shorter events, 7.7 us)
Async XLA Ops:
  7.2 43.9 %all-gather.4.cloned.1.call-start = ((), (), s32[]{:S(2)}) async-start(), calls=%async_computation.2 | async-start | bytes 1658880 | tf_op jit(solution)/shard_map/all_gather | solution.py:414
  8.9 12.8 %copy-start.6 = (bf16[140,1120]{1,0:T(8,128)(2,1)S(1)}, bf16[140,1120]{1,0:T(8,128)(2,1)}, u32[]{:S(2)}) copy-start(bf16[140,1120]{1,0:T(8,128)(2,1)} %param.20) | copy-start | bytes 940804
  8.9 12.9 %copy-start.7 = (bf16[1120,140]{0,1:T(8,128)(2,1)S(1)}, bf16[1120,140]{0,1:T(8,128)(2,1)}, u32[]{:S(2)}) copy-start(bf16[1120,140]{0,1:T(8,128)(2,1)} %param.21) | copy-start | bytes 940804
  11.7 17.5 %all-to-all-start = ((bf16[16,40,128]{2,1,0:T(8,128)(2,1)}), bf16[16,40,128]{2,1,0:T(8,128)(2,1)S(1)}, u32[]{:S(2)}, u32[]{:S(2)}) async-start(bf16[16,40,128]{2,1,0:T(8,128)(2,1)} %bitcast.58), calls=%async_computation | async-start | bytes 327680 | tf_op jit(solution)/shard_map/all_to_all | solution.py:419
  21.7 98.7 %all-gather.6.cloned.1.call-start = ((), (), s32[]{:S(2)}) async-start(), calls=%async_computation.3 | async-start | bytes 5971968 | tf_op jit(solution)/shard_map/all_gather | solution.py:425
  29.2 15.5 %collective-permute-start.7 = (bf16[2,72,1120]{2,1,0:T(8,128)(2,1)S(1)}, bf16[2,72,1120]{2,1,0:T(8,128)(2,1)S(1)}, u32[]{:S(2)}, u32[]{:S(2)}) collective-permute-start(bf16[2,72,1120]{2,1,0:T(8,128)(2,1)S(1)} %fusion.2), channel_id=1, source_target_pairs={{0,32},{32,128},{128,160},{160,0},{1,33},{33,129},{129,161},{161,1... | collective-permute-start | bytes 967688 | tf_op jit(solution)/shard_map/ppermute | solution.py:38
  52.5 14.3 %collective-permute-start = (bf16[4,144,560]{2,1,0:T(8,128)(2,1)S(1)}, bf16[4,144,560]{2,1,0:T(8,128)(2,1)S(1)}, u32[]{:S(2)}, u32[]{:S(2)}) collective-permute-start(bf16[4,144,560]{2,1,0:T(8,128)(2,1)S(1)} %get-tuple-element.43), channel_id=1, source_target_pairs={{0,32},{32,128},{128,160},{160,0},{1,33},{33,129},{129,161},{161,1... | collective-permute-start | bytes 1935368 | tf_op jit(solution)/shard_map/ppermute | solution.py:38
  53.7 13.1 %collective-permute-start.1 = (bf16[4,144,560]{2,1,0:T(8,128)(2,1)S(1)}, bf16[4,144,560]{2,1,0:T(8,128)(2,1)S(1)}, u32[]{:S(2)}, u32[]{:S(2)}) collective-permute-start(bf16[4,144,560]{2,1,0:T(8,128)(2,1)S(1)} %get-tuple-element.42), channel_id=1, source_target_pairs={{0,160},{32,0},{128,32},{160,128},{1,161},{33,1},{129,33},{161,129... | collective-permute-start | bytes 1935368 | tf_op jit(solution)/shard_map/ppermute | solution.py:38
  71.0 8.2 %copy-start.8 = (bf16[2304,128]{1,0:T(8,128)(2,1)S(1)}, bf16[2304,128]{1,0:T(8,128)(2,1)}, u32[]{:S(2)}) copy-start(bf16[2304,128]{1,0:T(8,128)(2,1)} %get-tuple-element.25) | copy-start | bytes 1769476
  71.0 26.9 %collective-permute-start.2 = (bf16[2304,128]{1,0:T(8,128)(2,1)}, bf16[2304,128]{1,0:T(8,128)(2,1)S(1)}, u32[]{:S(2)}, u32[]{:S(2)}) collective-permute-start(bf16[2304,128]{1,0:T(8,128)(2,1)} %get-tuple-element.24), channel_id=1, source_target_pairs={{0,2},{1,3},{2,0},{3,1},{4,6},{5,7},{6,4},{7,5},{8,10},{9,11},{10,... | collective-permute-start | bytes 1769480 | tf_op jit(solution)/shard_map/ppermute | solution.py:38
  78.5 19.5 %collective-permute-start.4 = (bf16[2304,128]{1,0:T(8,128)(2,1)}, bf16[2304,128]{1,0:T(8,128)(2,1)S(1)}, u32[]{:S(2)}, u32[]{:S(2)}) collective-permute-start(bf16[2304,128]{1,0:T(8,128)(2,1)} %get-tuple-element.27), channel_id=1, source_target_pairs={{0,3},{1,0},{2,1},{3,2},{4,7},{5,4},{6,5},{7,6},{8,11},{9,8},{10,9... | collective-permute-start | bytes 1769480 | tf_op jit(solution)/shard_map/ppermute | solution.py:38
  79.2 19.0 %collective-permute-start.3 = (bf16[2304,128]{1,0:T(8,128)(2,1)S(1)}, bf16[2304,128]{1,0:T(8,128)(2,1)}, u32[]{:S(2)}, u32[]{:S(2)}) collective-permute-start(bf16[2304,128]{1,0:T(8,128)(2,1)S(1)} %copy-done.8), channel_id=1, source_target_pairs={{0,1},{1,2},{2,3},{3,0},{4,5},{5,6},{6,7},{7,4},{8,9},{9,10},{10,1... | collective-permute-start | bytes 1769480 | tf_op jit(solution)/shard_map/ppermute | solution.py:38
  83.8 1.8 copy-start.5
  85.7 1.3 copy-start.2
  87.0 14.8 %copy-start.1 = (bf16[32,72,128]{2,1,0:T(8,128)(2,1)}, bf16[32,72,128]{2,1,0:T(8,128)(2,1)S(1)}, u32[]{:S(2)}) copy-start(bf16[32,72,128]{2,1,0:T(8,128)(2,1)S(1)} %pad.20.latent_ref) | copy-start | bytes 1769476
  87.1 14.8 %copy-start = (f32[32,72,4]{2,1,0:T(8,128)}, f32[32,72,4]{2,1,0:T(8,128)S(1)}, u32[]{:S(2)}) copy-start(f32[32,72,4]{2,1,0:T(8,128)S(1)} %pad.21.vector_ref) | copy-start | bytes 110596
  120.4 24.8 %collective-permute-start.8 = (bf16[8,2,2,72,1120]{4,3,2,1,0:T(8,128)(2,1)}, bf16[8,2,2,72,1120]{4,3,2,1,0:T(8,128)(2,1)S(1)}, u32[]{:S(2)}, u32[]{:S(2)}) collective-permute-start(bf16[8,2,2,72,1120]{4,3,2,1,0:T(8,128)(2,1)} %bitcast.44), channel_id=1, source_target_pairs={{0,64},{64,0},{1,65},{65,1},{2,66},{66,2},{3,67},{67,3},{4,68},{68... | collective-permute-start | bytes 15482888 | tf_op jit(solution)/shard_map/ppermute | solution.py:38
  121.2 15.5 %collective-permute-start.5 = (bf16[128,2304]{1,0:T(8,128)(2,1)}, bf16[128,2304]{1,0:T(8,128)(2,1)S(1)}, u32[]{:S(2)}, u32[]{:S(2)}) collective-permute-start(bf16[128,2304]{1,0:T(8,128)(2,1)} %get-tuple-element.36.refs_0_), channel_id=1, source_target_pairs={{0,3},{1,0},{2,1},{3,2},{4,7},{5,4},{6,5},{7,6},{8,11},{9,8},{10,9... | collective-permute-start | bytes 1769480 | tf_op jit(solution)/shard_map/ppermute | solution.py:38
  123.7 16.4 %collective-permute-start.6 = (bf16[128,2304]{1,0:T(8,128)(2,1)}, bf16[128,2304]{1,0:T(8,128)(2,1)S(1)}, u32[]{:S(2)}, u32[]{:S(2)}) collective-permute-start(bf16[128,2304]{1,0:T(8,128)(2,1)} %get-tuple-element.36.refs_0_), channel_id=1, source_target_pairs={{0,1},{1,2},{2,3},{3,0},{4,5},{5,6},{6,7},{7,4},{8,9},{9,10},{10,1... | collective-permute-start | bytes 1769480 | tf_op jit(solution)/shard_map/ppermute | solution.py:38
  136.7 3.5 %copy-start.3 = (bf16[128,2304]{1,0:T(8,128)(2,1)}, bf16[128,2304]{1,0:T(8,128)(2,1)S(1)}, u32[]{:S(2)}) copy-start(bf16[128,2304]{1,0:T(8,128)(2,1)S(1)} %collective-permute-done.5.refs_0_) | copy-start | bytes 1769476
  136.7 17.1 %collective-permute-start.11 = (bf16[64,2304]{1,0:T(8,128)(2,1)S(1)}, bf16[64,2304]{1,0:T(8,128)(2,1)S(1)}, u32[]{:S(2)}, u32[]{:S(2)}) collective-permute-start(bf16[64,2304]{1,0:T(8,128)(2,1)S(1)} %slice.28), channel_id=1, source_target_pairs={{0,3},{1,0},{2,1},{3,2},{4,7},{5,4},{6,5},{7,6},{8,11},{9,8},{10,9... | collective-permute-start | bytes 884744 | tf_op jit(solution)/shard_map/ppermute | solution.py:38
  140.1 0.8 copy-start.4
  140.1 13.7 %collective-permute-start.12 = (bf16[64,2304]{1,0:T(8,128)(2,1)S(1)}, bf16[64,2304]{1,0:T(8,128)(2,1)S(1)}, u32[]{:S(2)}, u32[]{:S(2)}) collective-permute-start(bf16[64,2304]{1,0:T(8,128)(2,1)S(1)} %slice.29), channel_id=1, source_target_pairs={{0,1},{1,2},{2,3},{3,0},{4,5},{5,6},{6,7},{7,4},{8,9},{9,10},{10,1... | collective-permute-start | bytes 884744 | tf_op jit(solution)/shard_map/ppermute | solution.py:38
  153.5 12.7 %copy-start.9 = (bf16[2304,128]{1,0:T(8,128)(2,1)S(1)}, bf16[2304,128]{1,0:T(8,128)(2,1)}, u32[]{:S(2)}) copy-start(bf16[2304,128]{1,0:T(8,128)(2,1)} %get-tuple-element.35) | copy-start | bytes 1769476
  153.5 28.1 %collective-permute-start.9 = (bf16[2304,128]{1,0:T(8,128)(2,1)S(1)}, bf16[2304,128]{1,0:T(8,128)(2,1)S(1)}, u32[]{:S(2)}, u32[]{:S(2)}) collective-permute-start(bf16[2304,128]{1,0:T(8,128)(2,1)S(1)} %get-tuple-element.34), channel_id=1, source_target_pairs={{0,1},{1,2},{2,3},{3,0},{4,5},{5,6},{6,7},{7,4},{8,9},{9,10},{10,1... | collective-permute-start | bytes 1769480 | tf_op jit(solution)/shard_map/ppermute | solution.py:38
  163.0 18.7 %collective-permute-start.13 = (bf16[2304,128]{1,0:T(8,128)(2,1)}, bf16[2304,128]{1,0:T(8,128)(2,1)S(1)}, u32[]{:S(2)}, u32[]{:S(2)}) collective-permute-start(bf16[2304,128]{1,0:T(8,128)(2,1)} %get-tuple-element.37), channel_id=1, source_target_pairs={{0,2},{1,3},{2,0},{3,1},{4,6},{5,7},{6,4},{7,5},{8,10},{9,11},{10,... | collective-permute-start | bytes 1769480 | tf_op jit(solution)/shard_map/ppermute | solution.py:38
  166.2 25.7 %collective-permute-start.10 = (bf16[2304,128]{1,0:T(8,128)(2,1)S(1)}, bf16[2304,128]{1,0:T(8,128)(2,1)S(1)}, u32[]{:S(2)}, u32[]{:S(2)}) collective-permute-start(bf16[2304,128]{1,0:T(8,128)(2,1)S(1)} %copy-done.9), channel_id=1, source_target_pairs={{0,3},{1,0},{2,1},{3,2},{4,7},{5,4},{6,5},{7,6},{8,11},{9,8},{10,9... | collective-permute-start | bytes 1769480 | tf_op jit(solution)/shard_map/ppermute | solution.py:38
Sparse Core Ops, SparseCore 0:
  10.3 40.6 all-gather.3
  52.9 67.5 all-gather.5
